TPU v7x, 256 devices: a whole 4x4x8 slice. The times are simulated.
256 devices in a mesh: seq: 32 (over z, y_hi, core), vocab: 8 (over x, y_lo).
Axes of the slice: x: 4, y: 4 (y_hi: 2, y_lo: 2; y = y_hi * 2 + y_lo), z: 8, core: 2. Of those that a mesh axis runs over, the one named last changes fastest.
Arguments:
- tokens: bfloat16 [16384, 2048], P('seq'), may hold values from -6 to 6
- attention_gain: bfloat16 [2048], replicated, may hold values from 0.099609375 to 1.8984375
- query_weight: bfloat16 [2048, 2048], P(None, 'vocab')
- key_weight: bfloat16 [2048, 1024], P(None, 'vocab')
- value_weight: bfloat16 [2048, 1024], P(None, 'vocab'), may hold values from -0.125 to 0.125
- out_weight: bfloat16 [2048, 2048], P('vocab'), may hold values from -0.125 to 0.125
- forward_gain: bfloat16 [2048], replicated, may hold values from 0.099609375 to 1.8984375
- gate_weight: bfloat16 [2048, 4096], P(None, 'vocab'), may hold values from -0.125 to 0.125
- up_weight: bfloat16 [2048, 4096], P(None, 'vocab'), may hold values from -0.125 to 0.125
- down_weight: bfloat16 [4096, 2048], P('vocab'), may hold values from -0.09375 to 0.09375
- final_gain: bfloat16 [2048], replicated, may hold values from 0.099609375 to 1.8984375
- head_weight: bfloat16 [92160, 2048], P(('seq', 'vocab')), may hold values from -0.375 to 0.375
- segment_ids: int32 [16384], replicated, may hold values from 0 to 3, as said below
- token_order: int32 [16384], P('seq'), may hold values from 0 to 16383, as said below
- live_blocks: int32 [32, 32], P('seq'), may hold values from 0 to 1, as said below
- cache_slots: int32 [16384], P('seq'), may hold values from 0 to 511, as said below
Outputs:
- hidden_out: bfloat16 [16384, 2048], P('seq', 'vocab')
- kv_cache: bfloat16 [16384, 2, 1024], P('seq', None, 'vocab')
- final_rms: float32 [4], replicated
- top_logit: float32 [4], replicated
Inputs may be any that keep to these rules, and one draw needn't show every extreme that they name: `segment_ids`: Non-decreasing; each request covers 1 to 8192 consecutive positions, one request exactly 8192. `token_order`: each initial position appears in exactly one slot. The 512 slots of each slot block hold two runs of 256 consecutive initial positions, each run starting at a multiple of 256 and increasing along the slots. live_blocks[b, s] is 1 exactly when some slot of block b and some slot of block (b - s) mod 32 share a request with the key's position not after the query's. `cache_slots`: within each slot block of 512 slots the values are a permutation.
All inputs are finite; a program needn't handle non-finite values.
Results may differ from a plain program's by a relative error of at most 0.02.
Values may be sent and summed in bfloat16 or wider, within the bound.
A program may use at most 128 MiB of HBM per device.

v0:
```python
import jax
import jax.numpy as jnp
from jax import lax
from jax.sharding import PartitionSpec as P

HD = 128
REQS = 4


epsilon = 1e-06
rope_base = 1000000.0
neg_fill = -1e30


def rms_scale(values, gain):
    mean_square = jnp.mean(values * values, axis=-1, keepdims=True)
    return values * lax.rsqrt(mean_square + epsilon) * gain.astype(jnp.float32)


def rotate(values, position):
    half = values.shape[-1] // 2
    inverse = rope_base ** (-jnp.arange(half, dtype=jnp.float32) * 2.0 / values.shape[-1])
    angle = position.astype(jnp.float32)[:, None] * inverse[None, :]
    angle = jnp.concatenate([angle, angle], axis=-1)[:, None, :]
    first = values[..., :half]
    second = values[..., half:]
    turned = jnp.concatenate([-second, first], axis=-1)
    return values * jnp.cos(angle) + turned * jnp.sin(angle)


def lookup_small(index, table):
    entries = jnp.arange(table.shape[0], dtype=jnp.int32)
    return jnp.sum(jnp.where(index[:, None] == entries[None, :], table[None, :], 0), axis=1)


def block_update(
    carry, query, order_query, segment_query, key_rows, value_rows, order_key, segment_key, live_key
):
    allowed = (
        (segment_query[:, None] == segment_key[None, :])
        & (order_key[None, :] <= order_query[:, None])
        & (live_key[None, :] > 0)
    )
    group_count = query.shape[1]
    head_size = query.shape[3]

    def compute(state):
        top, weight_sum, weighted = state
        key_heads = key_rows.reshape(key_rows.shape[0], group_count, head_size)
        value_heads = value_rows.reshape(value_rows.shape[0], group_count, head_size)
        scores = jnp.einsum(
            "qcgd,kcd->cgqk", query, key_heads, preferred_element_type=jnp.float32
        ) * head_size ** (-0.5)
        scores = jnp.where(allowed[None, None], scores, neg_fill)
        new_top = jnp.maximum(top, jnp.max(scores, axis=-1))
        probs = jnp.where(allowed[None, None], jnp.exp(scores - new_top[..., None]), 0.0)
        keep = jnp.exp(top - new_top)
        weight_sum = weight_sum * keep + jnp.sum(probs, axis=-1)
        added = jnp.einsum(
            "cgqk,kcd->cgqd",
            probs.astype(jnp.bfloat16),
            value_heads,
            preferred_element_type=jnp.float32,
        )
        weighted = weighted * keep[..., None] + added
        return (new_top, weight_sum, weighted)

    def unchanged(state):
        return state

    return lax.cond(jnp.any(allowed), compute, unchanged, carry)


def per_device(
    tokens,
    attention_gain,
    query_weight,
    key_weight,
    value_weight,
    out_weight,
    forward_gain,
    gate_weight,
    up_weight,
    down_weight,
    final_gain,
    head_weight,
    segment_ids,
    token_order,
    live_blocks,
    cache_slots,
):
    local_rows = tokens.shape[0]
    block_count = lax.axis_size("seq")
    my_block = lax.axis_index("seq")
    column_block = lax.axis_index("vocab")
    column_width = tokens.shape[1] // lax.axis_size("vocab")
    request = jnp.arange(REQS, dtype=jnp.int32)
    counts = jnp.sum((segment_ids[None, :] == request[:, None]).astype(jnp.int32), axis=1)
    starts = jnp.sum((segment_ids[None, :] < request[:, None]).astype(jnp.int32), axis=1)
    segment = segment_ids[token_order]
    position = token_order - lookup_small(segment, starts)
    live_row = live_blocks[0]
    normed = rms_scale(tokens.astype(jnp.float32), attention_gain).astype(jnp.bfloat16)
    query_heads = rotate(
        jnp.dot(normed, query_weight, preferred_element_type=jnp.float32).reshape(
            local_rows, -1, HD
        ),
        position,
    ).astype(jnp.bfloat16)
    key_heads = rotate(
        jnp.dot(normed, key_weight, preferred_element_type=jnp.float32).reshape(local_rows, -1, HD),
        position,
    ).astype(jnp.bfloat16)
    key_flat = key_heads.reshape(local_rows, -1)
    value_flat = jnp.dot(normed, value_weight, preferred_element_type=jnp.float32).astype(
        jnp.bfloat16
    )
    group_count = key_heads.shape[1]
    group = query_heads.shape[1] // group_count
    kv_cache = (
        jnp.zeros((local_rows, 2, key_flat.shape[1]), jnp.bfloat16)
        .at[cache_slots]
        .set(jnp.stack([key_flat, value_flat], axis=1))
    )
    query = query_heads.reshape(local_rows, group_count, group, HD)
    carry = (
        jnp.full((group_count, group, local_rows), neg_fill, jnp.float32),
        jnp.zeros((group_count, group, local_rows), jnp.float32),
        jnp.zeros((group_count, group, local_rows, HD), jnp.float32),
    )
    key_piece = lax.all_gather(key_flat, "seq", axis=0, tiled=True)
    value_piece = lax.all_gather(value_flat, "seq", axis=0, tiled=True)
    order_piece = lax.all_gather(token_order, "seq", axis=0, tiled=True)
    piece_rows = key_piece.shape[0]
    key_block = jnp.arange(piece_rows, dtype=jnp.int32) // local_rows
    live_key = lookup_small((my_block - key_block) % block_count, live_row)
    segment_key = segment_ids[order_piece]
    span_rows = 2048

    def one_span(index, inner):
        low_row = index * span_rows

        def take(values):
            return lax.dynamic_slice_in_dim(values, low_row, span_rows, 0)

        return block_update(
            inner,
            query,
            token_order,
            segment,
            take(key_piece),
            take(value_piece),
            take(order_piece),
            take(segment_key),
            take(live_key),
        )

    carry = lax.fori_loop(0, piece_rows // span_rows, one_span, carry)
    top, weight_sum, weighted = carry
    heads_out = (weighted / weight_sum[..., None]).astype(jnp.bfloat16)
    heads_out = jnp.transpose(heads_out, (2, 0, 1, 3)).reshape(local_rows, -1)
    partial_sum = jnp.dot(heads_out, out_weight, preferred_element_type=jnp.float32)
    token_values = tokens.astype(jnp.float32)
    attention_sum = lax.psum(partial_sum.astype(jnp.bfloat16), "vocab").astype(jnp.float32)
    residual = token_values + attention_sum
    mid_normed = rms_scale(residual, forward_gain).astype(jnp.bfloat16)
    residual_cols = lax.dynamic_slice_in_dim(residual, column_block * column_width, column_width, 1)
    gate = jnp.dot(mid_normed, gate_weight, preferred_element_type=jnp.float32)
    upward = jnp.dot(mid_normed, up_weight, preferred_element_type=jnp.float32)
    activated = (jax.nn.silu(gate) * upward).astype(jnp.bfloat16)
    forward_cols = lax.psum_scatter(
        jnp.dot(activated, down_weight, preferred_element_type=jnp.float32).astype(jnp.bfloat16),
        "vocab",
        scatter_dimension=1,
        tiled=True,
    ).astype(jnp.float32)
    hidden_out = (residual_cols + forward_cols).astype(jnp.bfloat16)
    last_index = starts + counts - 1
    matches = (token_order[None, :] == last_index[:, None]).astype(jnp.bfloat16)
    picked = jnp.dot(matches, hidden_out, preferred_element_type=jnp.float32)
    placed = lax.dynamic_update_slice(
        jnp.zeros((REQS, tokens.shape[1]), jnp.float32), picked, (0, column_block * column_width)
    )
    last_rows = lax.psum(placed, ("seq", "vocab"))
    mean_square = jnp.mean(last_rows * last_rows, axis=-1, keepdims=True)
    final_rms = jnp.sqrt(mean_square[:, 0] + epsilon)
    last_normed = (
        last_rows * lax.rsqrt(mean_square + epsilon) * final_gain.astype(jnp.float32)
    ).astype(jnp.bfloat16)
    logits = lax.dot_general(
        last_normed, head_weight, (((1,), (1,)), ((), ())), preferred_element_type=jnp.float32
    )
    top_logit = lax.pmax(jnp.max(logits, axis=1), ("seq", "vocab"))
    return (hidden_out, kv_cache, final_rms, top_logit)


def solution(mesh):
    return jax.shard_map(
        per_device,
        mesh=mesh,
        in_specs=(
            P("seq", None),
            P(),
            P(None, "vocab"),
            P(None, "vocab"),
            P(None, "vocab"),
            P("vocab", None),
            P(),
            P(None, "vocab"),
            P(None, "vocab"),
            P("vocab", None),
            P(),
            P(("seq", "vocab"), None),
            P(),
            P("seq"),
            P("seq", None),
            P("seq"),
        ),
        out_specs=(P("seq", "vocab"), P("seq", None, "vocab"), P(), P()),
        check_vma=False,
    )
```

profile of v0, /device:TPU:1, one launch (start us, length us, event | category | flops | bytes accessed | tf_op | source)
XLA Modules:
  0.0 718.6 jit_solution(11018523615109273286)
XLA Ops:
  10.2 2.6 fusion.55
  13.6 3.1 gather_fusion
  18.6 3.2 convolution_convert_fusion.2
  22.9 2.8 fusion.53
  30.6 46.6 %all-gather = s32[32,1,512]{2,1,0:T(1,128)S(1)} all-gather(s32[1,1,512]{2,1,0:T(1,128)S(1)} %bitcast.92), channel_id=1, replica_groups=mesh['seq'=32,'vocab'=8] {'seq'}, dimensions={0}, use_global_device_ids=true | all-gather | bytes 67584 | tf_op jit(solution)/shard_map/all_gather | solution.py:133
  77.9 160.9 %gather_fusion.1 = s32[16384]{0:T(1024)} fusion(s32[16384]{0:T(1024)S(1)} %copy-done.1, s32[16384]{0:T(1024)} %fusion.41), kind=kCustom, calls=%fused_computation.1 | custom fusion | bytes 196608 | tf_op jit(solution)/shard_map/gather | solution.py:137
  241.9 6.4 copy.58
  248.3 6.4 copy.59
  255.6 110.5 %while.17 = (s32[]{:T(128)}, f32[1,2,512]{2,1,0:T(2,128)S(1)}, f32[1,2,512]{2,1,0:T(2,128)S(1)}, f32[1,2,512,128]{3,2,1,0:T(8,128)}, s32[512]{0:T(512)S(1)}, /*i...) while((s32[]{:T(128)}, f32[1,2,512]{2,1,0:T(2,128)S(1)}, ...), condition=%wide.region_10.11_spmd, body=%wide.region_4.10_spmd.sunk | while | flops 1106514944 | bytes 36046212 | solution.py:158
  257.1 2.4 fusion.70
  260.1 9.4 %conditional.2 = ((f32[1,2,512]{2,1,0:T(2,128)S(1)}, f32[1,2,512]{2,1,0:T(2,128)S(1)}, f32[1,2,512,128]{3,2,1,0:T(8,128)})) conditional(s32[]{:T(128)} %convert_element_type.170, (f32[1,2,512]{2,1,0:T(2,128)S(1)}, f32[1,2,512]{2,1,0:T(2,128)S(1)}, f32[1,2,512,128]{3,2,1,0:T(8,128)}) %tuple.61, (pred[512,2048]{0,1:T(8,128)(4,1)S(1)}, ...), branch_computations={%region_6.6_spmd, %region_7.9_spmd} | conditional | flops 1101270016 | bytes 34931800 | solution.py:71
  260.1 2.9 fusion
  263.0 4.1 fusion.10
  270.9 2.4 fusion.70
  273.9 9.4 %conditional.2 = ((f32[1,2,512]{2,1,0:T(2,128)S(1)}, f32[1,2,512]{2,1,0:T(2,128)S(1)}, f32[1,2,512,128]{3,2,1,0:T(8,128)})) conditional(s32[]{:T(128)} %convert_element_type.170, (f32[1,2,512]{2,1,0:T(2,128)S(1)}, f32[1,2,512]{2,1,0:T(2,128)S(1)}, f32[1,2,512,128]{3,2,1,0:T(8,128)}) %tuple.61, (pred[512,2048]{0,1:T(8,128)(4,1)S(1)}, ...), branch_computations={%region_6.6_spmd, %region_7.9_spmd} | conditional | flops 1101270016 | bytes 34931800 | solution.py:71
  273.9 2.9 fusion
  276.8 4.1 fusion.10
  284.7 2.4 fusion.70
  287.7 9.4 %conditional.2 = ((f32[1,2,512]{2,1,0:T(2,128)S(1)}, f32[1,2,512]{2,1,0:T(2,128)S(1)}, f32[1,2,512,128]{3,2,1,0:T(8,128)})) conditional(s32[]{:T(128)} %convert_element_type.170, (f32[1,2,512]{2,1,0:T(2,128)S(1)}, f32[1,2,512]{2,1,0:T(2,128)S(1)}, f32[1,2,512,128]{3,2,1,0:T(8,128)}) %tuple.61, (pred[512,2048]{0,1:T(8,128)(4,1)S(1)}, ...), branch_computations={%region_6.6_spmd, %region_7.9_spmd} | conditional | flops 1101270016 | bytes 34931800 | solution.py:71
  287.7 2.9 fusion
  290.7 4.1 fusion.10
  298.5 2.4 fusion.70
  301.5 9.4 %conditional.2 = ((f32[1,2,512]{2,1,0:T(2,128)S(1)}, f32[1,2,512]{2,1,0:T(2,128)S(1)}, f32[1,2,512,128]{3,2,1,0:T(8,128)})) conditional(s32[]{:T(128)} %convert_element_type.170, (f32[1,2,512]{2,1,0:T(2,128)S(1)}, f32[1,2,512]{2,1,0:T(2,128)S(1)}, f32[1,2,512,128]{3,2,1,0:T(8,128)}) %tuple.61, (pred[512,2048]{0,1:T(8,128)(4,1)S(1)}, ...), branch_computations={%region_6.6_spmd, %region_7.9_spmd} | conditional | flops 1101270016 | bytes 34931800 | solution.py:71
  301.6 2.9 fusion
  304.5 4.1 fusion.10
  312.3 2.4 fusion.70
  315.3 9.4 %conditional.2 = ((f32[1,2,512]{2,1,0:T(2,128)S(1)}, f32[1,2,512]{2,1,0:T(2,128)S(1)}, f32[1,2,512,128]{3,2,1,0:T(8,128)})) conditional(s32[]{:T(128)} %convert_element_type.170, (f32[1,2,512]{2,1,0:T(2,128)S(1)}, f32[1,2,512]{2,1,0:T(2,128)S(1)}, f32[1,2,512,128]{3,2,1,0:T(8,128)}) %tuple.61, (pred[512,2048]{0,1:T(8,128)(4,1)S(1)}, ...), branch_computations={%region_6.6_spmd, %region_7.9_spmd} | conditional | flops 1101270016 | bytes 34931800 | solution.py:71
  315.4 2.9 fusion
  318.3 4.1 fusion.10
  326.2 2.4 fusion.70
  329.2 9.4 %conditional.2 = ((f32[1,2,512]{2,1,0:T(2,128)S(1)}, f32[1,2,512]{2,1,0:T(2,128)S(1)}, f32[1,2,512,128]{3,2,1,0:T(8,128)})) conditional(s32[]{:T(128)} %convert_element_type.170, (f32[1,2,512]{2,1,0:T(2,128)S(1)}, f32[1,2,512]{2,1,0:T(2,128)S(1)}, f32[1,2,512,128]{3,2,1,0:T(8,128)}) %tuple.61, (pred[512,2048]{0,1:T(8,128)(4,1)S(1)}, ...), branch_computations={%region_6.6_spmd, %region_7.9_spmd} | conditional | flops 1101270016 | bytes 34931800 | solution.py:71
  329.2 2.9 fusion
  332.1 4.1 fusion.10
  343.0 9.4 %conditional.2 = ((f32[1,2,512]{2,1,0:T(2,128)S(1)}, f32[1,2,512]{2,1,0:T(2,128)S(1)}, f32[1,2,512,128]{3,2,1,0:T(8,128)})) conditional(s32[]{:T(128)} %convert_element_type.170, (f32[1,2,512]{2,1,0:T(2,128)S(1)}, f32[1,2,512]{2,1,0:T(2,128)S(1)}, f32[1,2,512,128]{3,2,1,0:T(8,128)}) %tuple.61, (pred[512,2048]{0,1:T(8,128)(4,1)S(1)}, ...), branch_computations={%region_6.6_spmd, %region_7.9_spmd} | conditional | flops 1101270016 | bytes 34931800 | solution.py:71
  343.0 2.9 fusion
  345.9 4.1 fusion.10
  356.8 9.4 %conditional.2 = ((f32[1,2,512]{2,1,0:T(2,128)S(1)}, f32[1,2,512]{2,1,0:T(2,128)S(1)}, f32[1,2,512,128]{3,2,1,0:T(8,128)})) conditional(s32[]{:T(128)} %convert_element_type.170, (f32[1,2,512]{2,1,0:T(2,128)S(1)}, f32[1,2,512]{2,1,0:T(2,128)S(1)}, f32[1,2,512,128]{3,2,1,0:T(8,128)}) %tuple.61, (pred[512,2048]{0,1:T(8,128)(4,1)S(1)}, ...), branch_computations={%region_6.6_spmd, %region_7.9_spmd} | conditional | flops 1101270016 | bytes 34931800 | solution.py:71
  356.8 2.9 fusion
  359.8 4.1 fusion.10
  367.5 3.3 convolution_convert_fusion
  371.2 103.4 %all-reduce.2.cloned.1.call-done = bf16[512,2048]{1,0:T(8,128)(2,1)} async-done(((bf16[512,2048]{1,0:T(8,128)(2,1)}), bf16[512,2048]{1,0:T(8,128)(2,1)}) %all-reduce.2.cloned.1.call-update) | async-done | bytes 2097168 | tf_op jit(solution)/shard_map/psum | solution.py:164
  474.6 5.0 convert_add_fusion
  479.6 2.4 fusion.51
  482.0 7.0 convolution_convert_fusion.1
  489.3 53.4 %reduce-scatter.2.cloned.1.call-done = bf16[512,256]{1,0:T(8,128)(2,1)} async-done(((bf16[512,2048]{1,0:T(8,128)(2,1)}), bf16[512,256]{1,0:T(8,128)(2,1)}) %reduce-scatter.2.cloned.1.call-update) | async-done | bytes 262160 | tf_op jit(solution)/shard_map/reduce_scatter | solution.py:171
  544.2 77.9 %psum.15 = f32[4,2048]{1,0:T(4,128)S(1)} all-reduce(f32[4,2048]{1,0:T(4,128)S(1)} %convolution_dynamic-update-slice_fusion), channel_id=1, replica_groups=mesh['seq'=32,'vocab'=8] {'seq','vocab'}, use_global_device_ids=true, to_apply=%region_16.17 | all-reduce | flops 8192 | bytes 65536 | tf_op jit(solution)/shard_map/psum | solution.py:184
  624.8 14.0 %scatter_fusion = bf16[512,2,128]{2,1,0:T(2,128)(2,1)S(1)} fusion(bf16[512,2,128]{2,1,0:T(2,128)(2,1)S(1)} %broadcast_in_dim.127, s32[512]{0:T(512)S(1)} %compare_select_fusion.1, bf16[512,2,128]{2,1,0:T(2,128)(2,1)S(1)} %copy.61), kind=kCustom, calls=%fused_computation.2 | custom fusion | bytes 788480 | tf_op jit(solution)/shard_map/scatter | solution.py:123
  638.8 73.3 %pmax.7 = f32[4]{0:T(128)} all-reduce(f32[4]{0:T(128)S(1)} %convolution_reduce_fusion), channel_id=1, replica_groups=mesh['seq'=32,'vocab'=8] {'seq','vocab'}, use_global_device_ids=true, to_apply=%region_19.20 | all-reduce | flops 4 | bytes 32 | tf_op jit(solution)/shard_map/pmax | solution.py:193
  (176 shorter events, 56.7 us)
Async XLA Ops:
  7.2 474.8 %copy-start = (bf16[512,2048]{1,0:T(8,128)(2,1)S(1)}, bf16[512,2048]{1,0:T(8,128)(2,1)}, u32[]{:S(2)}) copy-start(bf16[512,2048]{1,0:T(8,128)(2,1)} %param.29) | copy-start | bytes 6291460
  7.2 5.6 copy-start.1
  7.2 6.4 copy-start.12
  7.2 234.7 %all-gather.4.cloned.1.call-start = ((), (), s32[]{:S(2)}) async-start(), calls=%async_computation.1 | async-start | bytes 4325376 | tf_op jit(solution)/shard_map/all_gather | solution.py:131
  18.6 229.8 %all-gather.6.cloned.1.call-start = ((), (), s32[]{:S(2)}) async-start(), calls=%async_computation.2 | async-start | bytes 4325376 | tf_op jit(solution)/shard_map/all_gather | solution.py:132
  21.9 452.7 %all-reduce.2.cloned.1.call-start = ((), (), s32[]{:S(2)}) async-start(), calls=%async_computation.3 | async-start | bytes 4194304 | tf_op jit(solution)/shard_map/psum | solution.py:164
  77.9 160.9 %copy-start.16 = (s32[1,32]{1,0:T(1,128)S(1)}, s32[1,32]{1,0:T(1,128)}, u32[]{:S(2)}) copy-start(s32[1,32]{1,0:T(1,128)} %param.34) | copy-start | bytes 388
  77.9 162.0 %copy-start.6 = (f32[512,2,64]{2,0,1:T(8,128)S(1)}, f32[512,2,64]{2,0,1:T(8,128)}, u32[]{:S(2)}) copy-start(f32[512,2,64]{2,0,1:T(8,128)} %copy.65) | copy-start | bytes 786436
  248.3 7.3 %copy-start.10 = (bf16[512,1,2,128]{3,0,2,1:T(8,128)(2,1)S(1)}, bf16[512,1,2,128]{3,0,2,1:T(8,128)(2,1)}, u32[]{:S(2)}) copy-start(bf16[512,1,2,128]{3,0,2,1:T(8,128)(2,1)} %fusion.30) | copy-start | bytes 786436
  260.1 2.9 copy-start.4
  267.1 2.3 copy-start.5
  273.9 2.9 copy-start.4
  281.0 2.3 copy-start.5
  287.7 2.9 copy-start.4
  294.8 2.3 copy-start.5
  301.5 2.9 copy-start.4
  308.6 2.3 copy-start.5
  315.4 2.9 copy-start.4
  322.4 2.3 copy-start.5
  329.2 2.9 copy-start.4
  336.2 2.3 copy-start.5
  343.0 2.9 copy-start.4
  350.0 2.3 copy-start.5
  356.8 2.9 copy-start.4
  363.9 2.3 copy-start.5
  366.2 4.9 copy-start.13
  370.9 171.9 %reduce-scatter.2.cloned.1.call-start = ((), (), s32[]{:S(2)}) async-start(), calls=%async_computation.4 | async-start | bytes 2359296 | tf_op jit(solution)/shard_map/reduce_scatter | solution.py:171
  474.6 5.0 copy-start.2
  474.6 5.0 copy-start.3
  474.6 5.0 copy-start.18
  482.0 7.0 copy-start.14
  482.0 7.1 copy-start.7
  482.0 7.1 copy-start.9
  482.0 7.3 %copy-start.17 = (s32[4]{0:T(128)S(1)}, s32[4]{0:T(128)}, u32[]{:S(2)}) copy-start(s32[4]{0:T(128)} %get-tuple-element.334) | copy-start | bytes 52
  482.0 7.3 %copy-start.15 = (s32[512]{0:T(512)S(1)}, s32[512]{0:T(512)}, u32[]{:S(2)}) copy-start(s32[512]{0:T(512)} %param.35) | copy-start | bytes 6148
  544.0 168.1 %copy-start.11 = (bf16[512,256]{1,0:T(8,128)(2,1)}, bf16[512,256]{1,0:T(8,128)(2,1)S(1)}, u32[]{:S(2)}) copy-start(bf16[512,256]{1,0:T(8,128)(2,1)S(1)} %add_convert_fusion) | copy-start | bytes 786436
  638.8 73.3 %copy-start.8 = (bf16[512,2,128]{2,1,0:T(2,128)(2,1)}, bf16[512,2,128]{2,1,0:T(2,128)(2,1)S(1)}, u32[]{:S(2)}) copy-start(bf16[512,2,128]{2,1,0:T(2,128)(2,1)S(1)} %scatter_fusion) | copy-start | bytes 786436
Sparse Core Ops, SparseCore 0:
  18.7 91.2 all-gather.3
  112.6 83.7 all-gather.5
  371.0 103.5 all-reduce.1
  489.2 53.5 reduce-scatter.1
where the time goes:
time: 721 us; the launch traced here: 719 us
  local copies, waits for them, and re-layouts  205 us (28%)
  blocking collectives  198 us (27%)
  waiting for transfers between devices  157 us (22%)
  matrix products  79.5 us (11%)
  other arithmetic  59 us (8%)
  between operations  14.1 us (2%)
    gather x1, local copies, waits for them, and re-layouts, per_device(): segment_key = segment_ids[order_piece]  161 us
    psum x1, waiting for transfers between devices, per_device(): lax.psum(partial_sum.astype(jnp.bfloat16), 'vocab').astype(jnp.float32)  103 us
    psum x1, blocking collectives, per_device(): last_rows = lax.psum(placed, ('seq', 'vocab'))  77.9 us
    pmax x1, blocking collectives, per_device(): top_logit = lax.pmax(jnp.max(logits, axis=1), ('seq', 'vocab'))  73.3 us
    reduce_scatter x1, waiting for transfers between devices, per_device(): lax.psum_scatter(jnp.dot(activated, down_weight, preferred_element_type=j...  53.4 us
    all_gather x1, blocking collectives, per_device(): order_piece = lax.all_gather(token_order, 'seq', axis=0, tiled=True)  46.6 us
    dot_general x8, matrix products, compute(): jnp.einsum('cgqk,kcd->cgqd', probs.astype(jnp.bfloat16), value_heads, pre...  32.8 us
    dot_general x8, matrix products, compute(): jnp.einsum('qcgd,kcd->cgqk', query, key_heads, preferred_element_type=jnp...  23.2 us
  transfers between devices with their start and end apart: 4, of which 2 were waited for; matrix products, arithmetic and copies ran while one was open for 25% of the time, Pallas kernels for 0%

commit v1 on v0

v1 whole, which is shorter than its diff:
```python
import functools

import jax
import jax.numpy as jnp
from jax import lax
from jax.experimental import pallas as pl
from jax.experimental.pallas import tpu as pltpu
from jax.sharding import PartitionSpec as P

MESH = pl.DeviceIdType.MESH
HD = 128
REQS = 4
epsilon = 1e-06
rope_base = 1000000.0
neg_fill = -1e30
VM = pl.BlockSpec(memory_space=pltpu.VMEM)
SM = pl.BlockSpec(memory_space=pltpu.SMEM)
HB = pl.BlockSpec(memory_space=pl.ANY)
F32 = jnp.float32
BF16 = jnp.bfloat16
LIMIT = 62 * 1024 * 1024


def params(cid=None):
    if cid is None:
        return pltpu.CompilerParams(vmem_limit_bytes=LIMIT)
    return pltpu.CompilerParams(
        collective_id=cid, has_side_effects=True, vmem_limit_bytes=LIMIT
    )


def seq_at(s, dz, dy, dc):
    z, y, c = s // 4, (s // 2) % 2, s % 2
    return ((z + dz + 8) % 8) * 4 + ((y + dy) % 2) * 2 + (c + dc) % 2


def vocab_at(v, dx, dy):
    x, y = v // 2, v % 2
    return ((x + dx + 4) % 4) * 2 + (y + dy) % 2


def greet(peers):
    barrier = pltpu.get_barrier_semaphore()
    for peer in peers:
        pl.semaphore_signal(barrier, inc=1, device_id=peer, device_id_type=MESH)
    pl.semaphore_wait(barrier, len(peers))


def project_kernel(
    base_ref, tok_ref, gain_ref, wq_ref, wk_ref, wv_ref, cos_ref, sin_ref, slot_ref,
    q_ref, kv_ref, cache_ref,
):
    gain = gain_ref[...].astype(F32)

    def rows_step(i, carry):
        rows = pl.ds(pl.multiple_of(i * 128, 128), 128)
        x = tok_ref[rows, :].astype(F32)
        scale = lax.rsqrt(jnp.mean(x * x, axis=-1, keepdims=True) + epsilon)
        normed = (x * scale * gain).astype(BF16)
        cos = cos_ref[rows, :]
        sin = sin_ref[rows, :]

        def turn(u):
            return u * cos + pltpu.roll(u, 64, axis=1) * sin

        q = jnp.dot(normed, wq_ref[...], preferred_element_type=F32)
        q_ref[rows, 0:128] = turn(q[:, 0:128]).astype(BF16)
        q_ref[rows, 128:256] = turn(q[:, 128:256]).astype(BF16)
        k = jnp.dot(normed, wk_ref[...], preferred_element_type=F32)
        kv_ref[rows, 0:128] = turn(k).astype(BF16)
        v = jnp.dot(normed, wv_ref[...], preferred_element_type=F32)
        kv_ref[rows, 128:256] = v.astype(BF16)
        return carry

    lax.fori_loop(0, 4, rows_step, 0)
    lane = lax.broadcasted_iota(jnp.int32, (16, 256), 1)
    run = jnp.where(lane < 128, base_ref[0] // 256, base_ref[1] // 256)
    kv_ref[512:528, :] = run.astype(F32).astype(BF16)
    slots = slot_ref[...]

    def cache_step(i, carry):
        row = i * 128 + lax.broadcasted_iota(jnp.int32, (128, 512), 0)
        pick = jnp.where(row == slots, 1.0, 0.0).astype(BF16)
        moved = jnp.dot(pick, kv_ref[0:512, :], preferred_element_type=F32)
        cache_ref[pl.ds(pl.multiple_of(i * 128, 128), 128), :] = moved.astype(BF16)
        return carry

    lax.fori_loop(0, 4, cache_step, 0)


PIECE_ROWS = ((0, 256), (256, 272))


def gather_kernel(kv_ref, w_ref, kv_all, w_all, own_sem, send_sem, kv_sem, w_sem):
    s = lax.axis_index("seq")
    v = lax.axis_index("vocab")
    c = s % 2
    up = (seq_at(s, 1, 0, 0), v)
    down = (seq_at(s, -1, 0, 0), v)
    side = (seq_at(s, 0, 1, 0), v)
    core = (seq_at(s, 0, 0, 1), v)
    right = (s, vocab_at(v, 1, 0))
    left = (s, vocab_at(v, -1, 0))
    near = (s, vocab_at(v, 0, 1))
    greet([up, down, side, core, right, left, near])

    started = []

    def kv_view(block, p):
        low, count = PIECE_ROWS[p]
        return kv_all.at[block, pl.ds(low, count), :]

    def kv_copy(src, block, p, peer):
        return pltpu.make_async_remote_copy(
            src_ref=src, dst_ref=kv_view(block, p), send_sem=send_sem.at[len(started)],
            recv_sem=kv_sem.at[block, p], device_id=peer, device_id_type=MESH,
        )

    def w_copy(src, shard, p, peer):
        return pltpu.make_async_remote_copy(
            src_ref=src, dst_ref=w_all.at[shard, p], send_sem=send_sem.at[len(started)],
            recv_sem=w_sem.at[shard, p], device_id=peer, device_id_type=MESH,
        )

    def go(copy):
        copy.start()
        started.append(copy)

    def kv_take(dz, dy, p, peers):
        block = seq_at(s, dz, dy, 0)
        kv_copy(kv_view(block, p), block, p, core).wait_recv()
        for peer in peers:
            go(kv_copy(kv_view(block, p), block, p, peer))

    def w_take(dx, dy, p, peers):
        shard = vocab_at(v, dx, dy)
        part = 2 * c + p
        w_copy(w_all.at[shard, part], shard, part, core).wait_recv()
        for peer in peers:
            go(w_copy(w_all.at[shard, part], shard, part, peer))

    own = []
    for p in range(2):
        low, count = PIECE_ROWS[p]
        src = kv_ref.at[pl.ds(low, count), :]
        for peer in (up, down, side, core):
            go(kv_copy(src, s, p, peer))
        part = 2 * c + p
        for peer in (right, left, near):
            go(w_copy(w_ref.at[part], v, part, peer))
    own.append(pltpu.make_async_copy(kv_ref, kv_all.at[s], own_sem.at[0]))
    own.append(pltpu.make_async_copy(w_ref, w_all.at[v], own_sem.at[1]))
    for copy in own:
        copy.start()

    for d in (1, 2):
        for p in range(2):
            kv_take(-d, 0, p, (up, core))
            kv_take(d, 0, p, (down, core))
    for p in range(2):
        w_take(-1, 0, p, (right, core) if p == 0 else (core,))
        w_take(1, 0, p, (left, core) if p == 1 else (core,))
    for p in range(2):
        kv_take(0, 1, p, (up, down, core))
    for p in range(2):
        w_take(0, 1, p, (right, left, core))
    for p in range(2):
        kv_take(-3, 0, p, (up, side, core) if p == 0 else (side, core))
        kv_take(3, 0, p, (down, side, core) if p == 1 else (side, core))
    for p in range(2):
        kv_take(-1, 1, p, (up, core))
        kv_take(1, 1, p, (down, core))
    for p in range(2):
        w_take(2, 0, p, (core,))
    for p in range(2):
        kv_take(4, 0, p, (side, core))
    for p in range(2):
        w_take(-1, 1, p, (right, core) if p == 0 else (core,))
        w_take(1, 1, p, (left, core) if p == 1 else (core,))
    for p in range(2):
        kv_take(-2, 1, p, (core,))
        kv_take(2, 1, p, (core,))
    for p in range(2):
        kv_take(-3, 1, p, (core,))
        kv_take(3, 1, p, (core,))
    for p in range(2):
        w_take(2, 1, p, (core,))
    for p in range(2):
        kv_take(4, 1, p, (core,))

    for dz in range(8):
        for dy in range(2):
            for p in range(2):
                block = seq_at(s, dz, dy, 1)
                kv_copy(kv_view(block, p), block, p, core).wait_recv()
    for dx in range(4):
        for dy in range(2):
            if (dx, dy) != (0, 0):
                for p in range(2):
                    shard = vocab_at(v, dx, dy)
                    part = 2 * (1 - c) + p
                    w_copy(w_all.at[shard, part], shard, part, core).wait_recv()
    for copy in own:
        copy.wait()
    for copy in started:
        copy.wait_send()


SLOTS = 8


def attend_kernel(
    where_ref, base_ref, starts_ref, live_ref, me_ref, q_ref, kv_ref, o_ref,
    buf, sem, q_rows, top, total, acc,
):
    me = me_ref[0]
    scale = HD ** (-0.5) * 1.4426950408889634
    for r in range(2):
        for h in range(2):
            q_rows[r, pl.ds(h * 256, 256), :] = q_ref[
                pl.ds(r * 256, 256), pl.ds(h * 128, 128)
            ]
    top[...] = jnp.full_like(top, neg_fill)
    total[...] = jnp.zeros_like(total)
    acc[...] = jnp.zeros_like(acc)

    def low_of(position):
        low = starts_ref[0]
        for r in range(1, REQS):
            low = jnp.where(starts_ref[r] <= position, starts_ref[r], low)
        return low

    base0, base1 = base_ref[0], base_ref[1]
    first0, first1 = low_of(base0) // 256, low_of(base1) // 256
    last0, last1 = low_of(base0 + 255), low_of(base1 + 255)
    count0 = base0 // 256 - first0 + 1
    count1 = base1 // 256 - first1 + 1
    n = count0 + count1

    def key_run(i):
        return jnp.where(i < count0, first0 + i, first1 + i - count0)

    def fetch(i):
        entry = where_ref[key_run(i)]
        slot = i % SLOTS
        return pltpu.make_async_copy(
            kv_ref.at[entry // 2, pl.ds((entry % 2) * 256, 256), :], buf.at[slot], sem.at[slot]
        )

    for i in range(SLOTS - 1):

        @pl.when(i < n)
        def _():
            fetch(i).start()

    def update(i, r, masked, run, base):
        slot = i % SLOTS
        keys = buf[slot, :, 0:128]
        values = buf[slot, :, 128:256]
        scores = lax.dot_general(
            keys, q_rows[r], (((1,), (1,)), ((), ())), preferred_element_type=F32
        )
        if masked:
            lane = lax.broadcasted_iota(jnp.int32, (1, 512), 1)
            q_pos = base + (lane % 256)
            low = jnp.full((1, 512), starts_ref[0], jnp.int32)
            for req in range(1, REQS):
                low = jnp.where(starts_ref[req] <= q_pos, starts_ref[req], low)
            k_pos = run * 256 + lax.broadcasted_iota(jnp.int32, (256, 512), 0)
            allowed = (k_pos <= q_pos) & (k_pos >= low)
            scores = jnp.where(allowed, scores, neg_fill)
        old = top[r]
        new = jnp.maximum(old, jnp.max(scores, axis=0, keepdims=True))
        probs = jnp.exp2((scores - new) * scale)
        if masked:
            probs = jnp.where(allowed, probs, 0.0)
        keep = jnp.exp2((old - new) * scale)
        top[r] = new
        total[r] = total[r] * keep + jnp.sum(probs, axis=0, keepdims=True)
        added = lax.dot_general(
            values, probs.astype(BF16), (((0,), (0,)), ((), ())), preferred_element_type=F32
        )
        acc[r] = acc[r] * keep + added

    def step(i, carry):
        @pl.when(i + SLOTS - 1 < n)
        def _():
            fetch(i + SLOTS - 1).start()

        fetch(i).wait()
        r = jnp.where(i < count0, 0, 1)
        run = key_run(i)
        base = jnp.where(r == 0, base0, base1)
        last_low = jnp.where(r == 0, last0, last1)
        entry = where_ref[run]
        live = live_ref[(me - entry // 2 + 32) % 32] > 0
        whole = (run * 256 < base) & (run * 256 >= last_low)

        @pl.when(live & whole)
        def _():
            update(i, r, False, run, base)

        @pl.when(live & jnp.logical_not(whole))
        def _():
            update(i, r, True, run, base)

        return carry

    lax.fori_loop(0, n, step, 0)
    for r in range(2):
        done = acc[r] / total[r]
        for h in range(2):
            o_ref[pl.ds(r * 256, 256), pl.ds(h * 128, 128)] = jnp.transpose(
                done[:, h * 256 : (h + 1) * 256]
            ).astype(BF16)


def middle_kernel(
    heads_ref, w_ref, tok_ref, gain_ref, wg_ref, wu_ref, wd_ref, out_ref,
    heads, w, tok_rows, tok_cols, wg, wu, wd, att, att_send, att_cols, normed, act, part, got,
    load_sem, head_send, head_recv, norm_send, norm_recv, att_sent, att_recv, part_send, part_recv,
):
    s = lax.axis_index("seq")
    v = lax.axis_index("vocab")
    others = [(v + r) % 8 for r in range(1, 8)]
    cols = pl.ds(pl.multiple_of(v * 256, 256), 256)
    rows = pl.ds(pl.multiple_of(v * 64, 64), 64)
    loads = [
        pltpu.make_async_copy(w_ref, w, load_sem.at[0]),
        pltpu.make_async_copy(tok_ref.at[rows, :], tok_rows, load_sem.at[1]),
        pltpu.make_async_copy(tok_ref.at[:, cols], tok_cols, load_sem.at[2]),
        pltpu.make_async_copy(wg_ref, wg, load_sem.at[3]),
        pltpu.make_async_copy(wu_ref, wu, load_sem.at[4]),
        pltpu.make_async_copy(wd_ref, wd, load_sem.at[5]),
        pltpu.make_async_copy(heads_ref.at[rows, :], heads.at[v], load_sem.at[6]),
    ]
    for copy in loads:
        copy.start()
    greet([(s, other) for other in others])

    def to(src, dst, sends, recvs, i, slot, other):
        return pltpu.make_async_remote_copy(
            src_ref=src, dst_ref=dst, send_sem=sends.at[i], recv_sem=recvs.at[slot],
            device_id=(s, other), device_id_type=MESH,
        )

    sent = []

    def go(copy):
        copy.start()
        sent.append(copy)

    for i, other in enumerate(others):
        src = heads_ref.at[pl.ds(pl.multiple_of(other * 64, 64), 64), :]
        go(to(src, heads.at[v], head_send, head_recv, i, v, other))
    for i, other in enumerate(others):
        to(heads.at[other], heads.at[other], head_send, head_recv, i, other, other).wait_recv()
    for i in (0, 1, 6):
        loads[i].wait()

    def project(j, square):
        wide = pl.ds(pl.multiple_of(j * 512, 512), 512)
        total = jnp.dot(heads[0], w[0:256, wide], preferred_element_type=F32)
        for k in range(1, 8):
            total += jnp.dot(
                heads[k], w[k * 256 : (k + 1) * 256, wide], preferred_element_type=F32
            )
        att_send[2 * j] = total[:, 0:256].astype(BF16)
        att_send[2 * j + 1] = total[:, 256:512].astype(BF16)
        residual = tok_rows[:, wide].astype(F32) + total
        att[:, wide] = residual
        return square + jnp.sum(residual * residual, axis=-1, keepdims=True)

    square = lax.fori_loop(0, 4, project, jnp.zeros((64, 1), F32))
    inverse = lax.rsqrt(square / 2048 + epsilon)
    mine = (att[...] * inverse * gain_ref[...].astype(F32)).astype(BF16)
    normed[v, 0] = mine[0:32]
    normed[v, 1] = mine[32:64]

    right, left, near = vocab_at(v, 1, 0), vocab_at(v, -1, 0), vocab_at(v, 0, 1)
    count = [0]

    def pass_on(owner, p, other):
        view = normed.at[owner, p]
        copy = pltpu.make_async_remote_copy(
            src_ref=view, dst_ref=view, send_sem=norm_send.at[count[0]],
            recv_sem=norm_recv.at[owner, p], device_id=(s, other), device_id_type=MESH,
        )
        count[0] += 1
        go(copy)

    def arrive(dx, dy, p, peers):
        owner = vocab_at(v, dx, dy)
        view = normed.at[owner, p]
        pltpu.make_async_remote_copy(
            src_ref=view, dst_ref=view, send_sem=norm_send.at[0],
            recv_sem=norm_recv.at[owner, p], device_id=(s, near), device_id_type=MESH,
        ).wait_recv()
        for peer in peers:
            pass_on(owner, p, peer)

    for p in range(2):
        for peer in (right, left, near):
            pass_on(v, p, peer)
    for i, other in enumerate(others):
        go(to(att_send.at[other], att_cols.at[v], att_sent, att_recv, i, v, other))
    own_cols = pltpu.make_async_copy(att_send.at[v], att_cols.at[v], load_sem.at[7])
    own_cols.start()
    for p in range(2):
        arrive(-1, 0, p, (right,) if p == 0 else ())
        arrive(1, 0, p, (left,) if p == 1 else ())
        arrive(0, 1, p, (right, left))
    for p in range(2):
        arrive(-1, 1, p, (right,) if p == 0 else ())
        arrive(1, 1, p, (left,) if p == 1 else ())
    for p in range(2):
        arrive(2, 0, p, ())
        arrive(2, 1, p, ())
    for i in (2, 3, 4, 5):
        loads[i].wait()

    def feed(i, carry):
        x = normed[pl.ds(2 * i, 2)].reshape(128, 2048)
        gate = jnp.dot(x, wg[...], preferred_element_type=F32)
        upward = jnp.dot(x, wu[...], preferred_element_type=F32)
        value = gate / (1.0 + jnp.exp(-gate)) * upward
        act[pl.ds(pl.multiple_of(i * 128, 128), 128), :] = value.astype(BF16)
        return carry

    lax.fori_loop(0, 4, feed, 0)

    def lower(other):
        wide = pl.ds(pl.multiple_of(other * 256, 256), 256)
        return jnp.dot(act[...], wd[:, wide], preferred_element_type=F32).astype(BF16)

    for i, other in enumerate(others):
        part[i] = lower(other)
        go(to(part.at[i], got.at[v], part_send, part_recv, i, v, other))
    got[v] = lower(v)
    own_cols.wait()
    for i, other in enumerate(others):
        to(att_cols.at[other], att_cols.at[other], att_sent, att_recv, i, other, other).wait_recv()
    for i, other in enumerate(others):
        to(got.at[other], got.at[other], part_send, part_recv, i, other, other).wait_recv()

    def finish(i, carry):
        chunk = pl.ds(pl.multiple_of(i * 64, 64), 64)
        residual = tok_cols[chunk, :].astype(F32) + att_cols[i].astype(F32)
        total = got[0, chunk, :].astype(F32)
        for k in range(1, 8):
            total += got[k, chunk, :].astype(F32)
        out_ref[chunk, :] = (residual + total).astype(BF16)
        return carry

    lax.fori_loop(0, 8, finish, 0)
    for copy in sent:
        copy.wait_send()


def last_kernel(
    match_ref, hidden_ref, gain_ref, head_ref, rms_ref, top_ref,
    head, row_send, seq_got, wide_got, max_send, seq_max, wide_send, vocab_max,
    load_sem, send_sem, seq_sem, wide_sem, max_sem, last_sem,
):
    s = lax.axis_index("seq")
    v = lax.axis_index("vocab")
    load = pltpu.make_async_copy(head_ref, head, load_sem.at[0])
    load.start()
    seqs = [(s + r) % 32 for r in range(1, 32)]
    vocabs = [(v + r) % 8 for r in range(1, 8)]
    greet([(other, v) for other in seqs] + [(s, other) for other in vocabs])
    sent = []

    def exchange(src, dst, sems, index, peers, slots):
        for peer in peers:
            copy = pltpu.make_async_remote_copy(
                src_ref=src, dst_ref=dst.at[index], send_sem=send_sem.at[len(sent)],
                recv_sem=sems.at[index], device_id=peer, device_id_type=MESH,
            )
            copy.start()
            sent.append(copy)
        for peer, slot in zip(peers, slots):
            pltpu.make_async_remote_copy(
                src_ref=src, dst_ref=dst.at[slot], send_sem=send_sem.at[0],
                recv_sem=sems.at[slot], device_id=peer, device_id_type=MESH,
            ).wait_recv()

    seq_peers = [(other, v) for other in seqs]
    vocab_peers = [(s, other) for other in vocabs]
    picked = jnp.dot(match_ref[...], hidden_ref[...], preferred_element_type=F32)
    row_send[...] = picked
    seq_got[s] = picked
    exchange(row_send, seq_got, seq_sem, s, seq_peers, seqs)
    mine = jnp.sum(seq_got[...], axis=0)
    wide_send[...] = mine
    wide_got[v] = mine
    exchange(wide_send, wide_got, wide_sem, v, vocab_peers, vocabs)
    square = jnp.zeros((8, 1), F32)
    for k in range(8):
        square += jnp.sum(wide_got[k] * wide_got[k], axis=-1, keepdims=True)
    mean_square = square / 2048 + epsilon
    rms_ref[...] = jnp.broadcast_to(jnp.sqrt(mean_square), (8, 128))
    inverse = lax.rsqrt(mean_square)
    load.wait()
    logits = jnp.zeros((8, 360), F32)
    for k in range(8):
        gain = gain_ref[:, k * 256 : (k + 1) * 256].astype(F32)
        normed = (wide_got[k] * inverse * gain).astype(BF16)
        logits += lax.dot_general(
            normed, head[:, k * 256 : (k + 1) * 256], (((1,), (1,)), ((), ())),
            preferred_element_type=F32,
        )
    best = jnp.broadcast_to(jnp.max(logits, axis=-1, keepdims=True), (8, 128))
    max_send[0] = best
    seq_max[s] = best
    exchange(max_send.at[0], seq_max, max_sem, s, seq_peers, seqs)
    best = jnp.max(seq_max[...], axis=0)
    max_send[1] = best
    vocab_max[v] = best
    exchange(max_send.at[1], vocab_max, last_sem, v, vocab_peers, vocabs)
    top_ref[...] = jnp.max(vocab_max[...], axis=0)
    for copy in sent:
        copy.wait_send()


def per_device(
    tokens,
    attention_gain,
    query_weight,
    key_weight,
    value_weight,
    out_weight,
    forward_gain,
    gate_weight,
    up_weight,
    down_weight,
    final_gain,
    head_weight,
    segment_ids,
    token_order,
    live_blocks,
    cache_slots,
):
    shape = jax.ShapeDtypeStruct
    me = lax.axis_index("seq").astype(jnp.int32)
    request = jnp.arange(8, dtype=jnp.int32)
    starts = jnp.sum((segment_ids[None, :] < request[:, None]).astype(jnp.int32), axis=1)
    begins = jnp.where(starts[None, :REQS] <= token_order[:, None], starts[None, :REQS], 0)
    position = token_order - jnp.max(begins, axis=1)
    inverse = rope_base ** (-jnp.arange(64, dtype=F32) * 2.0 / 128)
    angle = position.astype(F32)[:, None] * inverse[None, :]
    cos, sin = jnp.cos(angle), jnp.sin(angle)
    cos = jnp.concatenate([cos, cos], axis=1)
    sin = jnp.concatenate([-sin, sin], axis=1)
    base = jnp.stack([token_order[0], token_order[256]])

    query, kv, cache = pl.pallas_call(
        project_kernel,
        out_shape=(shape((512, 256), BF16), shape((528, 256), BF16), shape((512, 256), BF16)),
        in_specs=[SM] + [VM] * 8,
        out_specs=(VM, VM, VM),
        compiler_params=params(),
        name="project",
    )(
        base, tokens, attention_gain[None], query_weight, key_weight, value_weight, cos, sin,
        cache_slots[None],
    )

    kv_all, w_all = pl.pallas_call(
        gather_kernel,
        out_shape=(shape((32, 528, 256), BF16), shape((8, 4, 64, 2048), BF16)),
        in_specs=[VM, HB],
        out_specs=(HB, HB),
        scratch_shapes=[
            pltpu.SemaphoreType.DMA((2,)),
            pltpu.SemaphoreType.DMA((128,)),
            pltpu.SemaphoreType.DMA((32, 2)),
            pltpu.SemaphoreType.DMA((8, 4)),
        ],
        compiler_params=params(0),
        name="gather",
    )(kv, out_weight.reshape(4, 64, 2048))

    runs = jnp.stack([kv_all[:, 512, 0], kv_all[:, 512, 128]], axis=1).astype(jnp.int32).reshape(64)
    entry = jnp.arange(64, dtype=jnp.int32)
    where = jnp.sum(jnp.where(runs[None, :] == entry[:, None], entry[None, :], 0), axis=1)
    heads = pl.pallas_call(
        attend_kernel,
        out_shape=shape((512, 256), BF16),
        in_specs=[SM, SM, SM, SM, SM, VM, HB],
        out_specs=VM,
        scratch_shapes=[
            pltpu.VMEM((SLOTS, 256, 256), BF16),
            pltpu.SemaphoreType.DMA((SLOTS,)),
            pltpu.VMEM((2, 512, 128), BF16),
            pltpu.VMEM((2, 1, 512), F32),
            pltpu.VMEM((2, 1, 512), F32),
            pltpu.VMEM((2, 128, 512), F32),
        ],
        compiler_params=params(),
        name="attend",
    )(where, base, starts, live_blocks[0], me[None], query, kv_all)

    dma = pltpu.SemaphoreType.DMA
    hidden = pl.pallas_call(
        middle_kernel,
        out_shape=shape((512, 256), BF16),
        in_specs=[VM, HB, HB, VM, HB, HB, HB],
        out_specs=VM,
        scratch_shapes=[
            pltpu.VMEM((8, 64, 256), BF16),
            pltpu.VMEM((2048, 2048), BF16),
            pltpu.VMEM((64, 2048), BF16),
            pltpu.VMEM((512, 256), BF16),
            pltpu.VMEM((2048, 512), BF16),
            pltpu.VMEM((2048, 512), BF16),
            pltpu.VMEM((512, 2048), BF16),
            pltpu.VMEM((64, 2048), F32),
            pltpu.VMEM((8, 64, 256), BF16),
            pltpu.VMEM((8, 64, 256), BF16),
            pltpu.VMEM((8, 2, 32, 2048), BF16),
            pltpu.VMEM((512, 512), BF16),
            pltpu.VMEM((7, 512, 256), BF16),
            pltpu.VMEM((8, 512, 256), BF16),
            dma((8,)), dma((7,)), dma((8,)), dma((16,)), dma((8, 2)), dma((7,)), dma((8,)),
            dma((7,)), dma((8,)),
        ],
        compiler_params=params(1),
        name="middle",
    )(
        heads, w_all.reshape(2048, 2048), tokens, forward_gain[None], gate_weight, up_weight,
        down_weight,
    )

    ends = jnp.concatenate([starts[1:REQS], jnp.full((1,), segment_ids.shape[0], jnp.int32)])
    last_index = jnp.concatenate([ends - 1, jnp.full((8 - REQS,), -1, jnp.int32)])
    match = (token_order[None, :] == last_index[:, None]).astype(BF16)
    rms, top = pl.pallas_call(
        last_kernel,
        out_shape=(shape((8, 128), F32), shape((8, 128), F32)),
        in_specs=[VM, VM, VM, HB],
        out_specs=(VM, VM),
        scratch_shapes=[
            pltpu.VMEM((360, 2048), BF16),
            pltpu.VMEM((8, 256), F32),
            pltpu.VMEM((32, 8, 256), F32),
            pltpu.VMEM((8, 8, 256), F32),
            pltpu.VMEM((2, 8, 128), F32),
            pltpu.VMEM((32, 8, 128), F32),
            pltpu.VMEM((8, 256), F32),
            pltpu.VMEM((8, 8, 128), F32),
            dma((1,)), dma((80,)), dma((32,)), dma((8,)), dma((32,)), dma((8,)),
        ],
        compiler_params=params(2),
        name="last",
    )(match, hidden, final_gain[None], head_weight)
    return (hidden, cache.reshape(512, 2, 128), rms[:REQS, 0], top[:REQS, 0])


def solution(mesh):
    return jax.shard_map(
        per_device,
        mesh=mesh,
        in_specs=(
            P("seq", None),
            P(),
            P(None, "vocab"),
            P(None, "vocab"),
            P(None, "vocab"),
            P("vocab", None),
            P(),
            P(None, "vocab"),
            P(None, "vocab"),
            P("vocab", None),
            P(),
            P(("seq", "vocab"), None),
            P(),
            P("seq"),
            P("seq", None),
            P("seq"),
        ),
        out_specs=(P("seq", "vocab"), P("seq", None, "vocab"), P(), P()),
        check_vma=False,
    )
```

time: 721 us -> 208 us (0.29)
  blocking collectives: 198 us -> 0 us
  local copies, waits for them, and re-layouts: 205 us -> 7.91 us
  Pallas kernels: 0 us -> 191 us
  waiting for transfers between devices: 157 us -> 0 us
  matrix products: 79.5 us -> 0 us
  other arithmetic: 59 us -> 7.89 us
  between operations: 14.1 us -> 0.73 us
    pallas_call x0 -> x5, Pallas kernels: none -> 191 us  [the longest x1 65.7 us: per_device(): pl.pallas_call(middle_kernel, out_shape=shape((512, 256), BF16), in_specs...]
    gather x2 -> x0, local copies, waits for them, and re-layouts: 164 us -> none  [the longest x1 161 us: per_device(): segment_key = segment_ids[order_piece]]
    psum x1 -> x0, waiting for transfers between devices: 103 us -> none  [per_device(): lax.psum(partial_sum.astype(jnp.bfloat16), 'vocab').astype(jnp.float32)]
    dot_general x24 -> x0, matrix products: 79.5 us -> none  [the longest x8 32.8 us: compute(): jnp.einsum('cgqk,kcd->cgqd', probs.astype(jnp.bfloat16), value_heads, pre...]
    psum x1 -> x0, blocking collectives: 77.9 us -> none  [per_device(): last_rows = lax.psum(placed, ('seq', 'vocab'))]
    pmax x1 -> x0, blocking collectives: 73.3 us -> none  [per_device(): top_logit = lax.pmax(jnp.max(logits, axis=1), ('seq', 'vocab'))]
    reduce_scatter x1 -> x0, waiting for transfers between devices: 53.4 us -> none  [per_device(): lax.psum_scatter(jnp.dot(activated, down_weight, preferred_element_type=j...]
    all_gather x1 -> x0, blocking collectives: 46.6 us -> none  [per_device(): order_piece = lax.all_gather(token_order, 'seq', axis=0, tiled=True)]
  transfers between devices with their start and end apart: 4 -> 0, of which waited for: 2 -> 0; matrix products, arithmetic and copies ran while one was open for 25% -> 0% of each run, Pallas kernels for 0% -> 0%
where the time goes in v1:
time: 208 us; the launch traced here: 207 us
  Pallas kernels  191 us (92%)
  local copies, waits for them, and re-layouts  7.91 us (4%)
  other arithmetic  7.89 us (4%)
    pallas_call x1, Pallas kernels, per_device(): pl.pallas_call(middle_kernel, out_shape=shape((512, 256), BF16), in_specs...  65.7 us
    pallas_call x1, Pallas kernels, per_device(): pl.pallas_call(gather_kernel, out_shape=(shape((32, 528, 256), BF16), sha...  53.6 us
    pallas_call x1, Pallas kernels, per_device(): pl.pallas_call(last_kernel, out_shape=(shape((8, 128), F32), shape((8, 12...  49.8 us
    pallas_call x1, Pallas kernels, per_device(): pl.pallas_call(attend_kernel, out_shape=shape((512, 256), BF16), in_specs...  15 us
    pallas_call x1, Pallas kernels, per_device(): pl.pallas_call(project_kernel, out_shape=(shape((512, 256), BF16), shape(...  6.75 us

profile of v1, /device:TPU:1, one launch (start us, length us, event | category | flops | bytes accessed | tf_op | source)
XLA Modules:
  0.0 207.5 jit_solution(8597994747415290844)
XLA Ops:
  0.6 0.0 copy-start.2
  0.6 0.0 copy-start.5
  0.7 1.1 convert_reduce_fusion.starts_ref
  1.8 0.0 copy-start.3
  1.8 0.8 select_reduce_fusion.1
  2.5 0.7 subtract_convert_fusion
  3.2 1.0 fusion
  4.2 1.0 pad_maximum_fusion
  5.2 0.0 copy-done.2
  5.2 0.5 fusion.1
  5.7 1.9 pad_add_fusion.base_ref
  7.7 0.0 copy-done.5
  7.7 0.6 broadcast_in_dim.48.gain_ref
  8.3 6.7 %project.1 = (bf16[512,256]{1,0:T(8,128)(2,1)}, bf16[528,256]{1,0:T(8,128)(2,1)}, bf16[512,256]{1,0:T(8,128)(2,1)}) custom-call(s32[2]{0:T(128)} %pad_add_fusion.base_ref, bf16[512,2048]{1,0:T(8,128)(2,1)} %tok_ref.3, bf16[1,2048]{1,0:T(2,128)(2,1)} %broadcast_in_dim.48.gain_ref, bf16[2048,256]{1,0:T(8,128)(2,1)} %wq_ref.1, bf16[2048,128]{1,0:T(8,128)(2,1)} %wk_ref.1, ...), custom_call_target="tpu_custom_call" | custom-call | tf_op jit(solution)/shard_map/project/pallas_call | solution.py:557
  15.0 0.0 copy-done.3
  15.0 53.6 %gather.1 = (bf16[32,528,256]{2,1,0:T(8,128)(2,1)}, bf16[8,4,64,2048]{3,2,1,0:T(8,128)(2,1)}) custom-call(bf16[528,256]{1,0:T(8,128)(2,1)} %get-tuple-element.11.kv_ref, bf16[4,64,2048]{2,1,0:T(8,128)(2,1)} %bitcast.9), custom_call_target="tpu_custom_call" | custom-call | tf_op jit(solution)/shard_map/gather/pallas_call | solution.py:569
  68.7 1.2 slice_reduce_fusion.1
  69.9 0.1 copy.22
  70.0 0.1 reshape.39
  70.1 0.6 select_reduce_fusion.where_ref
  70.7 0.0 copy-start.6
  70.7 15.0 %attend.1.heads_ref = bf16[512,256]{1,0:T(8,128)(2,1)} custom-call(s32[64]{0:T(128)} %select_reduce_fusion.where_ref, s32[2]{0:T(128)} %pad_add_fusion.base_ref, s32[8]{0:T(128)} %copy-done.3, s32[32]{0:T(128)} %bitcast.14, s32[1]{0:T(128)} %bitcast.3.me_ref, bf16[512,256]{1,0:T(8,128)(2,1)} %get-tuple-element.13.q_ref, ...), custom_call_target="tpu_custom_call" | custom-call | tf_op jit(solution)/shard_map/attend/pallas_call | solution.py:587
  85.8 0.0 copy-done.6
  85.8 0.6 broadcast_in_dim.54.gain_ref
  86.4 0.0 copy-start.4
  86.4 0.0 copy-start.7
  86.4 0.0 copy-start.1
  86.4 65.7 %middle.1.hidden_ref = bf16[512,256]{1,0:T(8,128)(2,1)} custom-call(bf16[512,256]{1,0:T(8,128)(2,1)} %attend.1.heads_ref, bf16[2048,2048]{1,0:T(8,128)(2,1)} %bitcast.8, bf16[512,2048]{1,0:T(8,128)(2,1)} %tok_ref.3, bf16[1,2048]{1,0:T(2,128)(2,1)} %broadcast_in_dim.54.gain_ref, bf16[2048,512]{1,0:T(8,128)(2,1)} %wg_ref.1, bf16[2048,512]{1,0:T(8,128)(2,1)} %wu_ref.1, ...), custom_call_target="tpu_custom_call" | custom-call | tf_op jit(solution)/shard_map/middle/pallas_call | solution.py:605
  152.1 0.0 copy-done.4
  152.1 0.0 copy-start
  152.1 0.1 slice.30
  152.2 0.1 add_add_fusion
  152.2 0.7 compare_convert_fusion.match_ref
  152.9 0.0 copy-done.7
  152.9 0.6 broadcast_in_dim.55.gain_ref
  153.5 49.8 %last.1 = (f32[8,128]{1,0:T(8,128)}, f32[8,128]{1,0:T(8,128)}) custom-call(bf16[8,512]{1,0:T(8,128)(2,1)} %compare_convert_fusion.match_ref, bf16[512,256]{1,0:T(8,128)(2,1)} %middle.1.hidden_ref, bf16[1,2048]{1,0:T(2,128)(2,1)} %broadcast_in_dim.55.gain_ref, bf16[360,2048]{1,0:T(8,128)(2,1)} %head_ref.1), custom_call_target="tpu_custom_call" | custom-call | tf_op jit(solution)/shard_map/last/pallas_call | solution.py:638
  203.4 1.3 slice_reduce_fusion.2
  204.7 1.3 slice_reduce_fusion.3
  206.0 0.0 copy-done.1
  206.0 0.8 reshape.38
  206.7 0.0 copy-done
  206.8 0.7 copy.24
  (3 shorter events, 0.0 us)
Async XLA Ops:
  0.6 4.6 %copy-start.2 = (s32[512]{0:T(512)S(1)}, s32[512]{0:T(512)}, u32[]{:S(2)}) copy-start(s32[512]{0:T(512)} %param.29) | copy-start | bytes 6148
  0.6 7.0 %copy-start.5 = (bf16[2048]{0:T(1024)(128)(2,1)S(1)}, bf16[2048]{0:T(1024)(128)(2,1)}, u32[]{:S(2)}) copy-start(bf16[2048]{0:T(1024)(128)(2,1)} %param.17) | copy-start | bytes 12292
  1.8 13.3 %copy-start.3 = (s32[8]{0:T(128)}, s32[8]{0:T(128)S(1)}, u32[]{:S(2)}) copy-start(s32[8]{0:T(128)S(1)} %convert_reduce_fusion.starts_ref) | copy-start | bytes 100
  70.7 15.0 %copy-start.6 = (bf16[2048]{0:T(1024)(128)(2,1)S(1)}, bf16[2048]{0:T(1024)(128)(2,1)}, u32[]{:S(2)}) copy-start(bf16[2048]{0:T(1024)(128)(2,1)} %param.22) | copy-start | bytes 12292
  86.4 65.7 %copy-start.4 = (s32[8]{0:T(128)S(1)}, s32[8]{0:T(128)}, u32[]{:S(2)}) copy-start(s32[8]{0:T(128)} %copy-done.3) | copy-start | bytes 100
  86.4 66.5 %copy-start.7 = (bf16[2048]{0:T(1024)(128)(2,1)S(1)}, bf16[2048]{0:T(1024)(128)(2,1)}, u32[]{:S(2)}) copy-start(bf16[2048]{0:T(1024)(128)(2,1)} %param.26) | copy-start | bytes 12292
  86.4 119.6 %copy-start.1 = (bf16[512,256]{1,0:T(8,128)(2,1)S(1)}, bf16[512,256]{1,0:T(8,128)(2,1)}, u32[]{:S(2)}) copy-start(bf16[512,256]{1,0:T(8,128)(2,1)} %get-tuple-element.15) | copy-start | bytes 786436
  152.1 54.7 %copy-start = (bf16[512,256]{1,0:T(8,128)(2,1)S(1)}, bf16[512,256]{1,0:T(8,128)(2,1)}, u32[]{:S(2)}) copy-start(bf16[512,256]{1,0:T(8,128)(2,1)} %middle.1.hidden_ref) | copy-start | bytes 786436

commit v2 on v1

v2 whole, which is shorter than its diff:
```python
import functools

import jax
import jax.numpy as jnp
from jax import lax
from jax.experimental import pallas as pl
from jax.experimental.pallas import tpu as pltpu
from jax.sharding import PartitionSpec as P

MESH = pl.DeviceIdType.MESH
HD = 128
REQS = 4
epsilon = 1e-06
rope_base = 1000000.0
neg_fill = -1e30
VM = pl.BlockSpec(memory_space=pltpu.VMEM)
SM = pl.BlockSpec(memory_space=pltpu.SMEM)
HB = pl.BlockSpec(memory_space=pl.ANY)
F32 = jnp.float32
BF16 = jnp.bfloat16
LIMIT = 62 * 1024 * 1024
SCALE = HD ** (-0.5) * 1.4426950408889634


def params(cid=None):
    if cid is None:
        return pltpu.CompilerParams(vmem_limit_bytes=LIMIT)
    return pltpu.CompilerParams(
        collective_id=cid, has_side_effects=True, vmem_limit_bytes=LIMIT
    )


def seq_at(s, dz, dy, dc):
    z, y, c = s // 4, (s // 2) % 2, s % 2
    return ((z + dz + 8) % 8) * 4 + ((y + dy) % 2) * 2 + (c + dc) % 2


def vocab_at(v, dx, dy):
    x, y = v // 2, v % 2
    return ((x + dx + 4) % 4) * 2 + (y + dy) % 2


def greet(peers):
    barrier = pltpu.get_barrier_semaphore()
    for peer in peers:
        pl.semaphore_signal(barrier, inc=1, device_id=peer, device_id_type=MESH)
    pl.semaphore_wait(barrier, len(peers))


def project_kernel(
    base_ref, tok_ref, gain_ref, wq_ref, wk_ref, wv_ref, cos_ref, sin_ref, slot_ref,
    q_ref, kv_ref, cache_ref,
):
    gain = gain_ref[...].astype(F32)

    def rows_step(i, carry):
        rows = pl.ds(pl.multiple_of(i * 128, 128), 128)
        x = tok_ref[rows, :].astype(F32)
        scale = lax.rsqrt(jnp.mean(x * x, axis=-1, keepdims=True) + epsilon)
        normed = (x * scale * gain).astype(BF16)
        cos = cos_ref[rows, :]
        sin = sin_ref[rows, :]

        def turn(u):
            return u * cos + pltpu.roll(u, 64, axis=1) * sin

        q = jnp.dot(normed, wq_ref[...], preferred_element_type=F32)
        q_ref[rows, 0:128] = (turn(q[:, 0:128]) * SCALE).astype(BF16)
        q_ref[rows, 128:256] = (turn(q[:, 128:256]) * SCALE).astype(BF16)
        k = jnp.dot(normed, wk_ref[...], preferred_element_type=F32)
        kv_ref[rows, 0:128] = turn(k).astype(BF16)
        v = jnp.dot(normed, wv_ref[...], preferred_element_type=F32)
        kv_ref[rows, 128:256] = v.astype(BF16)
        return carry

    lax.fori_loop(0, 4, rows_step, 0)
    lane = lax.broadcasted_iota(jnp.int32, (16, 256), 1)
    run = jnp.where(lane < 128, base_ref[0] // 256, base_ref[256] // 256)
    kv_ref[512:528, :] = run.astype(F32).astype(BF16)
    slots = slot_ref[...]

    def cache_step(i, carry):
        row = i * 128 + lax.broadcasted_iota(jnp.int32, (128, 512), 0)
        pick = jnp.where(row == slots, 1.0, 0.0).astype(BF16)
        moved = jnp.dot(pick, kv_ref[0:512, :], preferred_element_type=F32)
        cache_ref[pl.ds(pl.multiple_of(i * 128, 128), 128), :] = moved.astype(BF16)
        return carry

    lax.fori_loop(0, 4, cache_step, 0)


PIECE_ROWS = ((0, 256), (256, 272))


def gather_kernel(kv_ref, w_ref, kv_all, w_all, own_sem, send_sem, kv_sem, w_sem):
    s = lax.axis_index("seq")
    v = lax.axis_index("vocab")
    c = s % 2
    up = (seq_at(s, 1, 0, 0), v)
    down = (seq_at(s, -1, 0, 0), v)
    side = (seq_at(s, 0, 1, 0), v)
    core = (seq_at(s, 0, 0, 1), v)
    right = (s, vocab_at(v, 1, 0))
    left = (s, vocab_at(v, -1, 0))
    near = (s, vocab_at(v, 0, 1))
    greet([up, down, side, core, right, left, near])

    started = []

    def kv_view(block, p):
        low, count = PIECE_ROWS[p]
        return kv_all.at[block, pl.ds(low, count), :]

    def kv_copy(src, block, p, peer):
        return pltpu.make_async_remote_copy(
            src_ref=src, dst_ref=kv_view(block, p), send_sem=send_sem.at[len(started)],
            recv_sem=kv_sem.at[block, p], device_id=peer, device_id_type=MESH,
        )

    def w_copy(src, shard, p, peer):
        return pltpu.make_async_remote_copy(
            src_ref=src, dst_ref=w_all.at[shard, p], send_sem=send_sem.at[len(started)],
            recv_sem=w_sem.at[shard, p], device_id=peer, device_id_type=MESH,
        )

    def go(copy):
        copy.start()
        started.append(copy)

    def kv_take(dz, dy, p, peers):
        block = seq_at(s, dz, dy, 0)
        kv_copy(kv_view(block, p), block, p, core).wait_recv()
        for peer in peers:
            go(kv_copy(kv_view(block, p), block, p, peer))

    def w_take(dx, dy, p, peers):
        shard = vocab_at(v, dx, dy)
        part = 2 * c + p
        w_copy(w_all.at[shard, part], shard, part, core).wait_recv()
        for peer in peers:
            go(w_copy(w_all.at[shard, part], shard, part, peer))

    own = []
    for p in range(2):
        low, count = PIECE_ROWS[p]
        src = kv_ref.at[pl.ds(low, count), :]
        for peer in (up, down, side, core):
            go(kv_copy(src, s, p, peer))
        part = 2 * c + p
        for peer in (right, left, near):
            go(w_copy(w_ref.at[part], v, part, peer))
    own.append(pltpu.make_async_copy(kv_ref, kv_all.at[s], own_sem.at[0]))
    own.append(pltpu.make_async_copy(w_ref, w_all.at[v], own_sem.at[1]))
    for copy in own:
        copy.start()

    for d in (1, 2):
        for p in range(2):
            kv_take(-d, 0, p, (up, core))
            kv_take(d, 0, p, (down, core))
    for p in range(2):
        w_take(-1, 0, p, (right, core) if p == 0 else (core,))
        w_take(1, 0, p, (left, core) if p == 1 else (core,))
    for p in range(2):
        kv_take(0, 1, p, (up, down, core))
    for p in range(2):
        w_take(0, 1, p, (right, left, core))
    for p in range(2):
        kv_take(-3, 0, p, (up, side, core) if p == 0 else (side, core))
        kv_take(3, 0, p, (down, side, core) if p == 1 else (side, core))
    for p in range(2):
        kv_take(-1, 1, p, (up, core))
        kv_take(1, 1, p, (down, core))
    for p in range(2):
        w_take(2, 0, p, (core,))
    for p in range(2):
        kv_take(4, 0, p, (side, core))
    for p in range(2):
        w_take(-1, 1, p, (right, core) if p == 0 else (core,))
        w_take(1, 1, p, (left, core) if p == 1 else (core,))
    for p in range(2):
        kv_take(-2, 1, p, (core,))
        kv_take(2, 1, p, (core,))
    for p in range(2):
        kv_take(-3, 1, p, (core,))
        kv_take(3, 1, p, (core,))
    for p in range(2):
        w_take(2, 1, p, (core,))
    for p in range(2):
        kv_take(4, 1, p, (core,))

    for dz in range(8):
        for dy in range(2):
            for p in range(2):
                block = seq_at(s, dz, dy, 1)
                kv_copy(kv_view(block, p), block, p, core).wait_recv()
    for dx in range(4):
        for dy in range(2):
            if (dx, dy) != (0, 0):
                for p in range(2):
                    shard = vocab_at(v, dx, dy)
                    part = 2 * (1 - c) + p
                    w_copy(w_all.at[shard, part], shard, part, core).wait_recv()
    for copy in own:
        copy.wait()
    for copy in started:
        copy.wait_send()


SLOTS = 8


def attend_kernel(
    where_ref, base_ref, starts_ref, live_ref, me_ref, q_ref, kv_ref, o_ref,
    buf, sem, q_rows, top, total, acc, scores0, scores1, probs0, probs1, keep0, keep1,
):
    me = me_ref[0]
    all_scores, all_probs, all_keep = (scores0, scores1), (probs0, probs1), (keep0, keep1)
    base0, base1 = base_ref[0], base_ref[256]

    def low_of(position):
        low = starts_ref[0]
        for r in range(1, REQS):
            low = jnp.where(starts_ref[r] <= position, starts_ref[r], low)
        return low

    first0, first1 = low_of(base0) // 256, low_of(base1) // 256
    last0, last1 = low_of(base0 + 255), low_of(base1 + 255)
    count0 = base0 // 256 - first0 + 1
    count1 = base1 // 256 - first1 + 1
    n = count0 + count1

    def key_run(i):
        return jnp.where(i < count0, first0 + i, first1 + i - count0)

    def fetch(i):
        entry = where_ref[key_run(i)]
        slot = i % SLOTS
        return pltpu.make_async_copy(
            kv_ref.at[entry // 2, pl.ds((entry % 2) * 256, 256), :], buf.at[slot], sem.at[slot]
        )

    for i in range(SLOTS - 2):

        @pl.when(i < n)
        def _():
            fetch(i).start()

    for r in range(2):
        for h in range(2):
            q_rows[r, pl.ds(h * 256, 256), :] = q_ref[
                pl.ds(r * 256, 256), pl.ds(h * 128, 128)
            ]
    top[...] = jnp.full_like(top, neg_fill)
    total[...] = jnp.zeros_like(total)
    acc[...] = jnp.zeros_like(acc)
    buf[SLOTS - 1] = jnp.zeros((256, 256), BF16)
    probs1[...] = jnp.zeros_like(probs1)
    keep1[...] = jnp.ones_like(keep1)

    def half(i):
        return jnp.where(i < count0, 0, 1)

    def score(i, into):
        into[...] = lax.dot_general(
            buf[i % SLOTS, :, 0:128], q_rows[half(i)],
            (((1,), (1,)), ((), ())), preferred_element_type=F32,
        )

    def collect(i, parity):
        r = half(i)
        added = lax.dot_general(
            buf[(i + SLOTS) % SLOTS, :, 128:256], all_probs[parity][...],
            (((0,), (0,)), ((), ())), preferred_element_type=F32,
        )
        acc[r] = acc[r] * all_keep[parity][...] + added

    def weigh(i, parity, masked, base):
        r = half(i)
        scores = all_scores[parity][...]
        if masked:
            lane = lax.broadcasted_iota(jnp.int32, (1, 512), 1)
            q_pos = base + (lane % 256)
            low = jnp.full((1, 512), starts_ref[0], jnp.int32)
            for req in range(1, REQS):
                low = jnp.where(starts_ref[req] <= q_pos, starts_ref[req], low)
            k_pos = key_run(i) * 256 + lax.broadcasted_iota(jnp.int32, (256, 512), 0)
            allowed = (k_pos <= q_pos) & (k_pos >= low)
            scores = jnp.where(allowed, scores, neg_fill)
        old = top[r]
        new = jnp.maximum(old, jnp.max(scores, axis=0, keepdims=True))
        probs = jnp.exp2(scores - new)
        if masked:
            probs = jnp.where(allowed, probs, 0.0)
        keep = jnp.exp2(old - new)
        top[r] = new
        total[r] = total[r] * keep + jnp.sum(probs, axis=0, keepdims=True)
        all_keep[parity][...] = keep
        all_probs[parity][...] = probs.astype(BF16)

    def stage(i, parity):
        @pl.when(i + SLOTS - 2 < n)
        def _():
            fetch(i + SLOTS - 2).start()

        @pl.when(i + 1 < n)
        def _():
            fetch(i + 1).wait()

        run = key_run(i)
        base = jnp.where(i < count0, base0, base1)
        last_low = jnp.where(i < count0, last0, last1)
        live = live_ref[(me - where_ref[run] // 2 + 32) % 32] > 0
        whole = (run * 256 < base) & (run * 256 >= last_low)

        @pl.when(live & whole)
        def _():
            score(i + 1, all_scores[1 - parity])
            collect(i - 1, 1 - parity)
            weigh(i, parity, False, base)

        @pl.when(live & jnp.logical_not(whole))
        def _():
            score(i + 1, all_scores[1 - parity])
            collect(i - 1, 1 - parity)
            weigh(i, parity, True, base)

        @pl.when(jnp.logical_not(live))
        def _():
            score(i + 1, all_scores[1 - parity])
            collect(i - 1, 1 - parity)
            all_keep[parity][...] = jnp.ones((1, 512), F32)
            all_probs[parity][...] = jnp.zeros((256, 512), BF16)

    def pair(k, carry):
        stage(2 * k, 0)

        @pl.when(2 * k + 1 < n)
        def _():
            stage(2 * k + 1, 1)

        return carry

    fetch(0).wait()
    score(0, scores0)
    lax.fori_loop(0, (n + 1) // 2, pair, 0)

    @pl.when(n % 2 == 1)
    def _():
        collect(n - 1, 0)

    @pl.when(n % 2 == 0)
    def _():
        collect(n - 1, 1)

    for r in range(2):
        done = acc[r] / total[r]
        for h in range(2):
            o_ref[pl.ds(r * 256, 256), pl.ds(h * 128, 128)] = jnp.transpose(
                done[:, h * 256 : (h + 1) * 256]
            ).astype(BF16)


def middle_kernel(
    heads_ref, w_ref, tok_ref, gain_ref, wg_ref, wu_ref, wd_ref, match_ref, final_ref, head_ref,
    out_ref, rms_ref, top_ref,
    heads, w, tok_rows, tok_cols, wg, wu, wd, att, att_send, att_cols, normed, act, part, got,
    head, row_send, seq_got, wide_send, wide_got, last_send, last_got, max_send, seq_max, vocab_max,
    load_sem, send_sem, head_recv, norm_recv, att_recv, part_recv,
    row_recv, wide_recv, last_recv, max_recv, top_recv,
):
    s = lax.axis_index("seq")
    v = lax.axis_index("vocab")
    others = [(v + r) % 8 for r in range(1, 8)]
    seqs = [(s + r) % 32 for r in range(1, 32)]
    cols = pl.ds(pl.multiple_of(v * 256, 256), 256)
    rows = pl.ds(pl.multiple_of(v * 64, 64), 64)
    loads = [
        pltpu.make_async_copy(w_ref, w, load_sem.at[0]),
        pltpu.make_async_copy(tok_ref.at[rows, :], tok_rows, load_sem.at[1]),
        pltpu.make_async_copy(tok_ref.at[:, cols], tok_cols, load_sem.at[2]),
        pltpu.make_async_copy(wg_ref, wg, load_sem.at[3]),
        pltpu.make_async_copy(wu_ref, wu, load_sem.at[4]),
        pltpu.make_async_copy(wd_ref, wd, load_sem.at[5]),
        pltpu.make_async_copy(heads_ref.at[rows, :], heads.at[v], load_sem.at[6]),
        pltpu.make_async_copy(head_ref, head, load_sem.at[8]),
    ]
    for copy in loads:
        copy.start()
    greet([(s, other) for other in others] + [(other, v) for other in seqs])
    sent = []

    def go(src, dst, recv, peer):
        copy = pltpu.make_async_remote_copy(
            src_ref=src, dst_ref=dst, send_sem=send_sem.at[len(sent)], recv_sem=recv,
            device_id=peer, device_id_type=MESH,
        )
        copy.start()
        sent.append(copy)

    def take(dst, recv):
        pltpu.make_async_remote_copy(
            src_ref=dst, dst_ref=dst, send_sem=send_sem.at[0], recv_sem=recv,
            device_id=(s, others[0]), device_id_type=MESH,
        ).wait_recv()

    for other in others:
        src = heads_ref.at[pl.ds(pl.multiple_of(other * 64, 64), 64), :]
        go(src, heads.at[v], head_recv.at[v], (s, other))
    for other in others:
        take(heads.at[other], head_recv.at[other])
    for i in (0, 1, 6):
        loads[i].wait()

    def project(j, square):
        wide = pl.ds(pl.multiple_of(j * 512, 512), 512)
        total = jnp.dot(heads[0], w[0:256, wide], preferred_element_type=F32)
        for k in range(1, 8):
            total += jnp.dot(
                heads[k], w[k * 256 : (k + 1) * 256, wide], preferred_element_type=F32
            )
        att_send[2 * j] = total[:, 0:256].astype(BF16)
        att_send[2 * j + 1] = total[:, 256:512].astype(BF16)
        residual = tok_rows[:, wide].astype(F32) + total
        att[:, wide] = residual
        return square + jnp.sum(residual * residual, axis=-1, keepdims=True)

    square = lax.fori_loop(0, 4, project, jnp.zeros((64, 1), F32))
    gain = gain_ref[...].astype(F32)
    mine = (att[...] * lax.rsqrt(square / 2048 + epsilon) * gain).astype(BF16)
    normed[2 * v] = mine[0:32]
    normed[2 * v + 1] = mine[32:64]

    right, left, near = vocab_at(v, 1, 0), vocab_at(v, -1, 0), vocab_at(v, 0, 1)

    def pass_on(owner, p, other):
        view = normed.at[2 * owner + p]
        go(view, view, norm_recv.at[owner, p], (s, other))

    def arrive(dx, dy, p, peers):
        owner = vocab_at(v, dx, dy)
        take(normed.at[2 * owner + p], norm_recv.at[owner, p])
        for peer in peers:
            pass_on(owner, p, peer)

    for other in others:
        go(att_send.at[other], att_cols.at[v], att_recv.at[v], (s, other))
    for p in range(2):
        for peer in (right, left, near):
            pass_on(v, p, peer)
    own_cols = pltpu.make_async_copy(att_send.at[v], att_cols.at[v], load_sem.at[7])
    own_cols.start()

    loads[2].wait()
    own_cols.wait()
    for other in others:
        take(att_cols.at[other], att_recv.at[other])
    picked = jnp.zeros((8, 256), F32)
    for i in range(8):
        residual = tok_cols[i * 64 : (i + 1) * 64, :].astype(F32) + att_cols[i].astype(F32)
        high = residual.astype(BF16)
        low = (residual - high.astype(F32)).astype(BF16)
        picked += jnp.dot(match_ref[i], high, preferred_element_type=F32)
        picked += jnp.dot(match_ref[i], low, preferred_element_type=F32)
    row_send[...] = picked
    seq_got[s] = picked
    for other in seqs:
        go(row_send, seq_got.at[s], row_recv.at[s], (other, v))

    for p in range(2):
        arrive(-1, 0, p, (right,) if p == 0 else ())
        arrive(1, 0, p, (left,) if p == 1 else ())
        arrive(0, 1, p, (right, left))

    for other in seqs:
        take(seq_got.at[other], row_recv.at[other])
    picked = jnp.sum(seq_got[...], axis=0)
    wide_send[...] = picked
    wide_got[v] = picked
    for other in others:
        go(wide_send, wide_got.at[v], wide_recv.at[v], (s, other))

    for p in range(2):
        arrive(-1, 1, p, (right,) if p == 0 else ())
        arrive(1, 1, p, (left,) if p == 1 else ())
    for p in range(2):
        arrive(2, 0, p, ())
        arrive(2, 1, p, ())

    for other in others:
        take(wide_got.at[other], wide_recv.at[other])
    square = jnp.zeros((8, 1), F32)
    for k in range(8):
        square += jnp.sum(wide_got[k] * wide_got[k], axis=-1, keepdims=True)
    inverse = lax.rsqrt(square / 2048 + epsilon)
    normed[16, 16:32, :] = jnp.zeros((16, 2048), BF16)
    for k in range(8):
        one = wide_got[k] * inverse * gain[:, k * 256 : (k + 1) * 256]
        normed[16, 0:16, k * 256 : (k + 1) * 256] = jnp.concatenate([one, one], axis=0).astype(BF16)
    for i in (3, 4, 5):
        loads[i].wait()

    def feed(x):
        gate = jnp.dot(x, wg[...], preferred_element_type=F32)
        upward = jnp.dot(x, wu[...], preferred_element_type=F32)
        return (gate / (1.0 + jnp.exp(-gate)) * upward).astype(BF16)

    act[384:544, :] = feed(normed[12:17].reshape(160, 2048))

    group = lax.broadcasted_iota(jnp.int32, (16, 512), 0) // 4

    def packed(quarter):
        out = quarter(0)
        for q in range(1, 4):
            out = jnp.where(group == q, quarter(q), out)
        return out

    last = act[512:528, :]
    mine = packed(
        lambda q: jnp.dot(
            last, wd[:, q * 512 : (q + 1) * 512], preferred_element_type=F32
        )
    ).astype(BF16)
    last_send[...] = mine
    last_got[v] = mine
    for other in others:
        go(last_send, last_got.at[v], last_recv.at[v], (s, other))

    def feed_step(i, carry):
        act[pl.ds(pl.multiple_of(i * 128, 128), 128), :] = feed(
            normed[pl.ds(4 * i, 4)].reshape(128, 2048)
        )
        return carry

    lax.fori_loop(0, 3, feed_step, 0)

    def lower(other):
        wide = pl.ds(pl.multiple_of(other * 256, 256), 256)
        return jnp.dot(act[0:512, :], wd[:, wide], preferred_element_type=F32).astype(BF16)

    for i, other in enumerate(others):
        part[i] = lower(other)
        go(part.at[i], got.at[v], part_recv.at[v], (s, other))
    got[v] = lower(v)

    for other in others:
        take(last_got.at[other], last_recv.at[other])

    def quarter_rows(q):
        one = jnp.concatenate([wide_got[2 * q], wide_got[2 * q + 1]], axis=1)
        return jnp.concatenate([one, one], axis=0)

    total = last_got[0].astype(F32)
    for k in range(1, 8):
        total += last_got[k].astype(F32)
    final = (packed(quarter_rows) + total).astype(BF16).astype(F32)
    square = jnp.broadcast_to(jnp.sum(final * final, axis=-1, keepdims=True), (16, 128))
    square = square + pltpu.roll(square, 8, axis=0)
    square = square + pltpu.roll(square, 4, axis=0)
    mean_square = square / 2048 + epsilon
    diagonal = lax.broadcasted_iota(jnp.int32, (16, 128), 0) == lax.broadcasted_iota(
        jnp.int32, (16, 128), 1
    )

    def along_lanes(value):
        return jnp.sum(jnp.where(diagonal, value, 0.0), axis=0, keepdims=True)

    rms_ref[...] = along_lanes(jnp.sqrt(mean_square))[:, :REQS]
    inverse = lax.rsqrt(mean_square)[:, 0:1]
    spread = packed(
        lambda q: jnp.broadcast_to(
            final_ref[:, q * 512 : (q + 1) * 512].astype(F32), (16, 512)
        )
    )
    final = final * inverse * spread
    loads[7].wait()
    logits = jnp.zeros((16, 360), F32)
    for q in range(4):
        turned = final if q == 0 else pltpu.roll(final, 16 - 4 * q, axis=0)
        logits += lax.dot_general(
            turned.astype(BF16), head[:, q * 512 : (q + 1) * 512], (((1,), (1,)), ((), ())),
            preferred_element_type=F32,
        )
    best = along_lanes(jnp.broadcast_to(jnp.max(logits, axis=-1, keepdims=True), (16, 128)))
    best = jnp.broadcast_to(best, (8, 128))
    max_send[0] = best
    seq_max[s] = best
    for other in seqs:
        go(max_send.at[0], seq_max.at[s], max_recv.at[s], (other, v))
    for other in seqs:
        take(seq_max.at[other], max_recv.at[other])
    best = jnp.max(seq_max[...], axis=0)
    max_send[1] = best
    vocab_max[v] = best
    for other in others:
        go(max_send.at[1], vocab_max.at[v], top_recv.at[v], (s, other))

    for other in others:
        take(got.at[other], part_recv.at[other])

    def finish(i, carry):
        chunk = pl.ds(pl.multiple_of(i * 64, 64), 64)
        residual = tok_cols[chunk, :].astype(F32) + att_cols[i].astype(F32)
        total = got[0, chunk, :].astype(F32)
        for k in range(1, 8):
            total += got[k, chunk, :].astype(F32)
        out_ref[chunk, :] = (residual + total).astype(BF16)
        return carry

    lax.fori_loop(0, 8, finish, 0)
    for other in others:
        take(vocab_max.at[other], top_recv.at[other])
    top_ref[...] = jnp.max(vocab_max[...], axis=0)[0:1, :REQS]
    for copy in sent:
        copy.wait_send()


def per_device(
    tokens,
    attention_gain,
    query_weight,
    key_weight,
    value_weight,
    out_weight,
    forward_gain,
    gate_weight,
    up_weight,
    down_weight,
    final_gain,
    head_weight,
    segment_ids,
    token_order,
    live_blocks,
    cache_slots,
):
    shape = jax.ShapeDtypeStruct
    me = lax.axis_index("seq").astype(jnp.int32)
    request = jnp.arange(8, dtype=jnp.int32)
    starts = jnp.sum((segment_ids[None, :] < request[:, None]).astype(jnp.int32), axis=1)
    begins = jnp.where(starts[None, :REQS] <= token_order[:, None], starts[None, :REQS], 0)
    position = token_order - jnp.max(begins, axis=1)
    lane = jnp.arange(128, dtype=jnp.int32)
    inverse = rope_base ** (-(lane % 64).astype(F32) * 2.0 / 128)
    angle = position.astype(F32)[:, None] * inverse[None, :]
    cos = jnp.cos(angle)
    sin = jnp.where(lane < 64, -1.0, 1.0)[None, :] * jnp.sin(angle)

    query, kv, cache = pl.pallas_call(
        project_kernel,
        out_shape=(shape((512, 256), BF16), shape((528, 256), BF16), shape((512, 256), BF16)),
        in_specs=[SM] + [VM] * 8,
        out_specs=(VM, VM, VM),
        compiler_params=params(),
        name="project",
    )(
        token_order, tokens, attention_gain[None], query_weight, key_weight, value_weight, cos, sin,
        cache_slots[None],
    )

    kv_all, w_all = pl.pallas_call(
        gather_kernel,
        out_shape=(shape((32, 528, 256), BF16), shape((8, 4, 64, 2048), BF16)),
        in_specs=[VM, HB],
        out_specs=(HB, HB),
        scratch_shapes=[
            pltpu.SemaphoreType.DMA((2,)),
            pltpu.SemaphoreType.DMA((128,)),
            pltpu.SemaphoreType.DMA((32, 2)),
            pltpu.SemaphoreType.DMA((8, 4)),
        ],
        compiler_params=params(0),
        name="gather",
    )(kv, out_weight.reshape(4, 64, 2048))

    runs = jnp.stack([kv_all[:, 512, 0], kv_all[:, 512, 128]], axis=1).astype(jnp.int32).reshape(64)
    entry = jnp.arange(64, dtype=jnp.int32)
    where = jnp.sum(jnp.where(runs[None, :] == entry[:, None], entry[None, :], 0), axis=1)
    heads = pl.pallas_call(
        attend_kernel,
        out_shape=shape((512, 256), BF16),
        in_specs=[SM, SM, SM, SM, SM, VM, HB],
        out_specs=VM,
        scratch_shapes=[
            pltpu.VMEM((SLOTS, 256, 256), BF16),
            pltpu.SemaphoreType.DMA((SLOTS,)),
            pltpu.VMEM((2, 512, 128), BF16),
            pltpu.VMEM((2, 1, 512), F32),
            pltpu.VMEM((2, 1, 512), F32),
            pltpu.VMEM((2, 128, 512), F32),
            pltpu.VMEM((256, 512), F32),
            pltpu.VMEM((256, 512), F32),
            pltpu.VMEM((256, 512), BF16),
            pltpu.VMEM((256, 512), BF16),
            pltpu.VMEM((1, 512), F32),
            pltpu.VMEM((1, 512), F32),
        ],
        compiler_params=params(),
        name="attend",
    )(where, token_order, starts, live_blocks[0], me[None], query, kv_all)

    ends = jnp.concatenate([starts[1:REQS], jnp.full((1,), segment_ids.shape[0], jnp.int32)])
    last_index = jnp.concatenate([ends - 1, ends - 1])
    match = (token_order.reshape(8, 1, 64) == last_index[None, :, None]).astype(BF16)
    dma = pltpu.SemaphoreType.DMA
    hidden, rms, top = pl.pallas_call(
        middle_kernel,
        out_shape=(shape((512, 256), BF16), shape((1, REQS), F32), shape((1, REQS), F32)),
        in_specs=[VM, HB, HB, VM, HB, HB, HB, VM, VM, HB],
        out_specs=(VM, VM, VM),
        scratch_shapes=[
            pltpu.VMEM((8, 64, 256), BF16),
            pltpu.VMEM((2048, 2048), BF16),
            pltpu.VMEM((64, 2048), BF16),
            pltpu.VMEM((512, 256), BF16),
            pltpu.VMEM((2048, 512), BF16),
            pltpu.VMEM((2048, 512), BF16),
            pltpu.VMEM((512, 2048), BF16),
            pltpu.VMEM((64, 2048), F32),
            pltpu.VMEM((8, 64, 256), BF16),
            pltpu.VMEM((8, 64, 256), BF16),
            pltpu.VMEM((17, 32, 2048), BF16),
            pltpu.VMEM((544, 512), BF16),
            pltpu.VMEM((7, 512, 256), BF16),
            pltpu.VMEM((8, 512, 256), BF16),
            pltpu.VMEM((360, 2048), BF16),
            pltpu.VMEM((8, 256), F32),
            pltpu.VMEM((32, 8, 256), F32),
            pltpu.VMEM((8, 256), F32),
            pltpu.VMEM((8, 8, 256), F32),
            pltpu.VMEM((16, 512), BF16),
            pltpu.VMEM((8, 16, 512), BF16),
            pltpu.VMEM((2, 8, 128), F32),
            pltpu.VMEM((32, 8, 128), F32),
            pltpu.VMEM((8, 8, 128), F32),
            dma((9,)), dma((128,)), dma((8,)), dma((8, 2)), dma((8,)), dma((8,)),
            dma((32,)), dma((8,)), dma((8,)), dma((32,)), dma((8,)),
        ],
        compiler_params=params(1),
        name="middle",
    )(
        heads, w_all.reshape(2048, 2048), tokens, forward_gain[None], gate_weight, up_weight,
        down_weight, match, final_gain[None], head_weight,
    )
    return (hidden, cache.reshape(512, 2, 128), rms.reshape(REQS), top.reshape(REQS))


def solution(mesh):
    return jax.shard_map(
        per_device,
        mesh=mesh,
        in_specs=(
            P("seq", None),
            P(),
            P(None, "vocab"),
            P(None, "vocab"),
            P(None, "vocab"),
            P("vocab", None),
            P(),
            P(None, "vocab"),
            P(None, "vocab"),
            P("vocab", None),
            P(),
            P(("seq", "vocab"), None),
            P(),
            P("seq"),
            P("seq", None),
            P("seq"),
        ),
        out_specs=(P("seq", "vocab"), P("seq", None, "vocab"), P(), P()),
        check_vma=False,
    )
```

time: 208 us -> 176 us (0.85)
  Pallas kernels: 191 us -> 158 us
    pallas_call x2 -> x1, Pallas kernels: 116 us -> 83.4 us  [per_device(): pl.pallas_call(middle_kernel, out_shape=(shape((512, 256), BF16), shape((...]
    unnamed x17 -> x15, local copies, waits for them, and re-layouts: 0.74 us -> 3.93 us
    slice x3 -> x0, local copies, waits for them, and re-layouts: 3.12 us -> none  [the longest x2 2.61 us: per_device(): return (hidden, cache.reshape(512, 2, 128), rms[:REQS, 0], top[:REQS, 0])]
where the time goes in v2:
time: 176 us; the launch traced here: 174 us
  Pallas kernels  158 us (90%)
  local copies, waits for them, and re-layouts  8.73 us (5%)
  other arithmetic  5.86 us (3%)
    pallas_call x1, Pallas kernels, per_device(): pl.pallas_call(middle_kernel, out_shape=(shape((512, 256), BF16), shape((...  83.4 us
    pallas_call x1, Pallas kernels, per_device(): pl.pallas_call(gather_kernel, out_shape=(shape((32, 528, 256), BF16), sha...  53.6 us
    pallas_call x1, Pallas kernels, per_device(): pl.pallas_call(attend_kernel, out_shape=shape((512, 256), BF16), in_specs...  14.6 us
    pallas_call x1, Pallas kernels, per_device(): pl.pallas_call(project_kernel, out_shape=(shape((512, 256), BF16), shape(...  6.75 us
    unnamed x15, local copies, waits for them, and re-layouts  3.93 us

profile of v2, /device:TPU:1, one launch (start us, length us, event | category | flops | bytes accessed | tf_op | source)
XLA Modules:
  0.0 173.6 jit_solution(15288625525157058592)
XLA Ops:
  0.6 1.1 convert_reduce_fusion.starts_ref
  1.7 0.0 copy-start.2
  1.7 0.8 select_reduce_fusion.1
  2.5 0.7 subtract_convert_fusion
  3.2 1.8 %fusion = (f32[512,128]{1,0:T(8,128)}, f32[512,128]{1,0:T(8,128)}) fusion(f32[128]{0:T(128)S(1)} %get-tuple-element.24, f32[128]{0:T(128)S(1)} %get-tuple-element.25, f32[512]{0:T(512)S(1)} %subtract_convert_fusion), kind=kLoop, calls=%fused_computation.4 | loop fusion | flops 131072 | bytes 527360 | tf_op jit(solution)/shard_map/mul | solution.py:646
  5.0 1.3 broadcast_in_dim.56.gain_ref
  6.3 6.7 %project.1 = (bf16[512,256]{1,0:T(8,128)(2,1)}, bf16[528,256]{1,0:T(8,128)(2,1)}, bf16[512,256]{1,0:T(8,128)(2,1)}) custom-call(s32[512]{0:T(512)} %base_ref.3, bf16[512,2048]{1,0:T(8,128)(2,1)} %tok_ref.3, bf16[1,2048]{1,0:T(2,128)(2,1)} %broadcast_in_dim.56.gain_ref, bf16[2048,256]{1,0:T(8,128)(2,1)} %wq_ref.1, bf16[2048,128]{1,0:T(8,128)(2,1)} %wk_ref.1, ...), custom_call_target="tpu_custom_call" | custom-call | tf_op jit(solution)/shard_map/project/pallas_call | solution.py:648
  13.0 0.0 copy-done.2
  13.1 53.6 %gather.1 = (bf16[32,528,256]{2,1,0:T(8,128)(2,1)}, bf16[8,4,64,2048]{3,2,1,0:T(8,128)(2,1)}) custom-call(bf16[528,256]{1,0:T(8,128)(2,1)} %get-tuple-element.12.kv_ref, bf16[4,64,2048]{2,1,0:T(8,128)(2,1)} %bitcast.11), custom_call_target="tpu_custom_call" | custom-call | tf_op jit(solution)/shard_map/gather/pallas_call | solution.py:660
  66.7 1.2 slice_reduce_fusion.1
  67.9 0.1 copy.22
  68.0 0.1 reshape.60
  68.1 0.6 select_reduce_fusion.where_ref
  68.7 0.0 copy-start.3
  68.7 0.0 copy-start.1
  68.7 0.0 copy-start.4
  68.7 0.0 copy-start.5
  68.8 14.6 %attend.1.heads_ref = bf16[512,256]{1,0:T(8,128)(2,1)} custom-call(s32[64]{0:T(128)} %select_reduce_fusion.where_ref, s32[512]{0:T(512)} %base_ref.3, s32[8]{0:T(128)} %copy-done.2, s32[32]{0:T(128)} %bitcast.16, s32[1]{0:T(128)} %bitcast.3.me_ref, bf16[512,256]{1,0:T(8,128)(2,1)} %get-tuple-element.14.q_ref, bf16[32,528,256]{2,1,0:T(8,128)(2,1)} %get-tuple-element.13.kv_ref), custom_call_target="tpu_custom_call" | custom-call | tf_op jit(solution)/shard_map/attend/pallas_call | solution.py:678
  83.3 0.0 copy-done.3
  83.3 0.1 slice.16
  83.4 0.1 add_add_fusion
  83.5 0.1 pad_add_fusion
  83.6 0.0 copy-done.1
  83.6 0.1 eq.33
  83.7 0.7 compare_convert_fusion.match_ref
  84.3 0.0 copy-done.4
  84.3 0.6 broadcast_in_dim.64.gain_ref
  84.9 0.0 copy-done.5
  84.9 0.6 broadcast_in_dim.65.final_ref
  85.5 0.0 copy-start
  85.5 83.4 %middle.1 = (bf16[512,256]{1,0:T(8,128)(2,1)}, f32[1,4]{1,0:T(1,128)}, f32[1,4]{1,0:T(1,128)}) custom-call(bf16[512,256]{1,0:T(8,128)(2,1)} %attend.1.heads_ref, bf16[2048,2048]{1,0:T(8,128)(2,1)} %bitcast.10, bf16[512,2048]{1,0:T(8,128)(2,1)} %tok_ref.3, bf16[1,2048]{1,0:T(2,128)(2,1)} %broadcast_in_dim.64.gain_ref, bf16[2048,512]{1,0:T(8,128)(2,1)} %wg_ref.1, ...), custom_call_target="tpu_custom_call" | custom-call | tf_op jit(solution)/shard_map/middle/pallas_call | solution.py:705
  168.9 0.0 copy-done
  169.0 0.8 reshape.57
  169.7 1.7 copy.26
  171.4 1.1 copy.27
  172.5 1.1 copy.28
  (2 shorter events, 0.0 us)
Async XLA Ops:
  1.7 11.3 %copy-start.2 = (s32[8]{0:T(128)}, s32[8]{0:T(128)S(1)}, u32[]{:S(2)}) copy-start(s32[8]{0:T(128)S(1)} %convert_reduce_fusion.starts_ref) | copy-start | bytes 100
  68.7 14.6 %copy-start.3 = (s32[8]{0:T(128)S(1)}, s32[8]{0:T(128)}, u32[]{:S(2)}) copy-start(s32[8]{0:T(128)} %copy-done.2) | copy-start | bytes 100
  68.7 14.8 %copy-start.1 = (s32[512]{0:T(512)S(1)}, s32[512]{0:T(512)}, u32[]{:S(2)}) copy-start(s32[512]{0:T(512)} %base_ref.3) | copy-start | bytes 6148
  68.7 15.6 %copy-start.4 = (bf16[2048]{0:T(1024)(128)(2,1)S(1)}, bf16[2048]{0:T(1024)(128)(2,1)}, u32[]{:S(2)}) copy-start(bf16[2048]{0:T(1024)(128)(2,1)} %param.22) | copy-start | bytes 12292
  68.7 16.2 %copy-start.5 = (bf16[2048]{0:T(1024)(128)(2,1)S(1)}, bf16[2048]{0:T(1024)(128)(2,1)}, u32[]{:S(2)}) copy-start(bf16[2048]{0:T(1024)(128)(2,1)} %param.26) | copy-start | bytes 12292
  85.5 83.4 %copy-start = (bf16[512,256]{1,0:T(8,128)(2,1)S(1)}, bf16[512,256]{1,0:T(8,128)(2,1)}, u32[]{:S(2)}) copy-start(bf16[512,256]{1,0:T(8,128)(2,1)} %get-tuple-element.17) | copy-start | bytes 786436

commit v3 on v2

--- a/solution.py
+++ b/solution.py
@@ -364,9 +364,9 @@
 def middle_kernel(
     heads_ref, w_ref, tok_ref, gain_ref, wg_ref, wu_ref, wd_ref, match_ref, final_ref, head_ref,
     out_ref, rms_ref, top_ref,
-    heads, w, tok_rows, tok_cols, wg, wu, wd, att, att_send, att_cols, normed, act, part, got,
-    head, row_send, seq_got, wide_send, wide_got, last_send, last_got, max_send, seq_max, vocab_max,
-    load_sem, send_sem, head_recv, norm_recv, att_recv, part_recv,
+    heads, w, tok_rows, tok_cols, wg, wu, wd, att, att_send, att_cols, normed, act, part, fwd_in,
+    x_in, y_in, head, row_send, seq_got, wide_send, wide_got, last_send, last_got, max_send, seq_max, vocab_max,
+    load_sem, send_sem, head_recv, norm_recv, att_recv, fwd_recv, x_recv, y_recv,
     row_recv, wide_recv, last_recv, max_recv, top_recv,
 ):
     s = lax.axis_index("seq")
@@ -472,6 +472,41 @@
         arrive(1, 0, p, (left,) if p == 1 else ())
         arrive(0, 1, p, (right, left))
 
+    for i in (3, 4, 5):
+        loads[i].wait()
+    x = v // 2
+    y = v % 2
+
+    def feed(values):
+        gate = jnp.dot(values, wg[...], preferred_element_type=F32)
+        upward = jnp.dot(values, wu[...], preferred_element_type=F32)
+        return (gate / (1.0 + jnp.exp(-gate)) * upward).astype(BF16)
+
+    def part_of(chunk, dx, dy):
+        return part.at[chunk, vocab_at(v, dx, dy)]
+
+    def at_y(chunk, dx, lane):
+        return part.at[chunk, ((x + dx + 4) % 4) * 2 + lane]
+
+    def rows_of(dx, extra):
+        chunk = (x + dx + 4) % 4
+        values = normed[pl.ds(4 * chunk, 4)].reshape(128, 2048)
+        if extra:
+            values = jnp.concatenate([values, normed[16]], axis=0)
+        active = feed(values)
+        if extra:
+            act[...] = active[128:144]
+            active = active[0:128]
+        for t in range(8):
+            part[chunk, t] = jnp.dot(
+                active, wd[:, t * 256 : (t + 1) * 256], preferred_element_type=F32
+            ).astype(BF16)
+        go(at_y(chunk, 2, 0), fwd_in.at[chunk, 0], fwd_recv.at[chunk, 0], (s, right))
+        go(at_y(chunk, 2, 1), fwd_in.at[chunk, 1], fwd_recv.at[chunk, 1], (s, left))
+        go(at_y(chunk, 1, 1), x_in.at[chunk, 0, 1], x_recv.at[chunk, 0, 1], (s, right))
+        go(at_y(chunk, -1, 0), x_in.at[chunk, 1, 0], x_recv.at[chunk, 1, 0], (s, left))
+
+    rows_of(0, False)
     for other in seqs:
         take(seq_got.at[other], row_recv.at[other])
     picked = jnp.sum(seq_got[...], axis=0)
@@ -483,10 +518,7 @@
     for p in range(2):
         arrive(-1, 1, p, (right,) if p == 0 else ())
         arrive(1, 1, p, (left,) if p == 1 else ())
-    for p in range(2):
-        arrive(2, 0, p, ())
-        arrive(2, 1, p, ())
-
+    rows_of(-1, False)
     for other in others:
         take(wide_got.at[other], wide_recv.at[other])
     square = jnp.zeros((8, 1), F32)
@@ -497,15 +529,7 @@
     for k in range(8):
         one = wide_got[k] * inverse * gain[:, k * 256 : (k + 1) * 256]
         normed[16, 0:16, k * 256 : (k + 1) * 256] = jnp.concatenate([one, one], axis=0).astype(BF16)
-    for i in (3, 4, 5):
-        loads[i].wait()
-
-    def feed(x):
-        gate = jnp.dot(x, wg[...], preferred_element_type=F32)
-        upward = jnp.dot(x, wu[...], preferred_element_type=F32)
-        return (gate / (1.0 + jnp.exp(-gate)) * upward).astype(BF16)
-
-    act[384:544, :] = feed(normed[12:17].reshape(160, 2048))
+    rows_of(1, True)
 
     group = lax.broadcasted_iota(jnp.int32, (16, 512), 0) // 4
 
@@ -515,7 +539,7 @@
             out = jnp.where(group == q, quarter(q), out)
         return out
 
-    last = act[512:528, :]
+    last = act[...]
     mine = packed(
         lambda q: jnp.dot(
             last, wd[:, q * 512 : (q + 1) * 512], preferred_element_type=F32
@@ -525,23 +549,27 @@
     last_got[v] = mine
     for other in others:
         go(last_send, last_got.at[v], last_recv.at[v], (s, other))
-
-    def feed_step(i, carry):
-        act[pl.ds(pl.multiple_of(i * 128, 128), 128), :] = feed(
-            normed[pl.ds(4 * i, 4)].reshape(128, 2048)
-        )
-        return carry
-
-    lax.fori_loop(0, 3, feed_step, 0)
-
-    def lower(other):
-        wide = pl.ds(pl.multiple_of(other * 256, 256), 256)
-        return jnp.dot(act[0:512, :], wd[:, wide], preferred_element_type=F32).astype(BF16)
-
-    for i, other in enumerate(others):
-        part[i] = lower(other)
-        go(part.at[i], got.at[v], part_recv.at[v], (s, other))
-    got[v] = lower(v)
+    for p in range(2):
+        arrive(2, 0, p, ())
+        arrive(2, 1, p, ())
+    rows_of(2, False)
+
+    def add_to(ref, *incoming):
+        value = ref[...].astype(F32)
+        for one in incoming:
+            value += one[...].astype(F32)
+        ref[...] = value.astype(BF16)
+
+    def onward(dx, way):
+        chunk = (x + dx + 4) % 4
+        take(fwd_in.at[chunk, way], fwd_recv.at[chunk, way])
+        ref = at_y(chunk, 1 if way == 0 else -1, way)
+        add_to(ref, fwd_in.at[chunk, way])
+        go(ref, x_in.at[chunk, way, way], x_recv.at[chunk, way, way], (s, right if way == 0 else left))
+
+    for to_right, to_left in ((-1, 1), (2, 0), (0, 2), (1, -1)):
+        onward(to_right, 0)
+        onward(to_left, 1)
 
     for other in others:
         take(last_got.at[other], last_recv.at[other])
@@ -587,6 +615,14 @@
     seq_max[s] = best
     for other in seqs:
         go(max_send.at[0], seq_max.at[s], max_recv.at[s], (other, v))
+    for dx in (0, -1, 1, 2):
+        chunk = (x + dx + 4) % 4
+        for way in range(2):
+            take(x_in.at[chunk, way, 1 - y], x_recv.at[chunk, way, 1 - y])
+        ref = part_of(chunk, 0, 1)
+        add_to(ref, x_in.at[chunk, 0, 1 - y], x_in.at[chunk, 1, 1 - y])
+        go(ref, y_in.at[chunk], y_recv.at[chunk], (s, near))
+
     for other in seqs:
         take(seq_max.at[other], max_recv.at[other])
     best = jnp.max(seq_max[...], axis=0)
@@ -595,19 +631,19 @@
     for other in others:
         go(max_send.at[1], vocab_max.at[v], top_recv.at[v], (s, other))
 
-    for other in others:
-        take(got.at[other], part_recv.at[other])
-
-    def finish(i, carry):
-        chunk = pl.ds(pl.multiple_of(i * 64, 64), 64)
-        residual = tok_cols[chunk, :].astype(F32) + att_cols[i].astype(F32)
-        total = got[0, chunk, :].astype(F32)
-        for k in range(1, 8):
-            total += got[k, chunk, :].astype(F32)
-        out_ref[chunk, :] = (residual + total).astype(BF16)
-        return carry
-
-    lax.fori_loop(0, 8, finish, 0)
+    for dx in (0, -1, 1, 2):
+        chunk = (x + dx + 4) % 4
+        for way in range(2):
+            take(x_in.at[chunk, way, y], x_recv.at[chunk, way, y])
+        take(y_in.at[chunk], y_recv.at[chunk])
+        rows = pl.ds(pl.multiple_of(chunk * 128, 128), 128)
+        total = tok_cols[rows, :].astype(F32)
+        total += att_cols[pl.ds(2 * chunk, 2)].reshape(128, 256).astype(F32)
+        total += part[chunk, v].astype(F32)
+        total += x_in[chunk, 0, y].astype(F32)
+        total += x_in[chunk, 1, y].astype(F32)
+        total += y_in[chunk].astype(F32)
+        out_ref[rows, :] = total.astype(BF16)
     for other in others:
         take(vocab_max.at[other], top_recv.at[other])
     top_ref[...] = jnp.max(vocab_max[...], axis=0)[0:1, :REQS]
@@ -719,9 +755,11 @@
             pltpu.VMEM((8, 64, 256), BF16),
             pltpu.VMEM((8, 64, 256), BF16),
             pltpu.VMEM((17, 32, 2048), BF16),
-            pltpu.VMEM((544, 512), BF16),
-            pltpu.VMEM((7, 512, 256), BF16),
-            pltpu.VMEM((8, 512, 256), BF16),
+            pltpu.VMEM((16, 512), BF16),
+            pltpu.VMEM((4, 8, 128, 256), BF16),
+            pltpu.VMEM((4, 2, 128, 256), BF16),
+            pltpu.VMEM((4, 2, 2, 128, 256), BF16),
+            pltpu.VMEM((4, 128, 256), BF16),
             pltpu.VMEM((360, 2048), BF16),
             pltpu.VMEM((8, 256), F32),
             pltpu.VMEM((32, 8, 256), F32),
@@ -732,7 +770,7 @@
             pltpu.VMEM((2, 8, 128), F32),
             pltpu.VMEM((32, 8, 128), F32),
             pltpu.VMEM((8, 8, 128), F32),
-            dma((9,)), dma((128,)), dma((8,)), dma((8, 2)), dma((8,)), dma((8,)),
+            dma((9,)), dma((176,)), dma((8,)), dma((8, 2)), dma((8,)), dma((4, 2)), dma((4, 2, 2)), dma((4,)),
             dma((32,)), dma((8,)), dma((8,)), dma((32,)), dma((8,)),
         ],
         compiler_params=params(1),

time: 176 us -> 164 us (0.932)
  Pallas kernels: 158 us -> 147 us
    pallas_call x1, Pallas kernels: 14.6 us -> 8.84 us  [per_device(): pl.pallas_call(attend_kernel, out_shape=shape((512, 256), BF16), in_specs...]
    pallas_call x1, Pallas kernels: 83.4 us -> 77.7 us  [per_device(): pl.pallas_call(middle_kernel, out_shape=(shape((512, 256), BF16), shape((...]
where the time goes in v3:
time: 164 us; the launch traced here: 162 us
  Pallas kernels  147 us (90%)
  local copies, waits for them, and re-layouts  8.73 us (5%)
  other arithmetic  5.86 us (4%)
    pallas_call x1, Pallas kernels, per_device(): pl.pallas_call(middle_kernel, out_shape=(shape((512, 256), BF16), shape((...  77.7 us
    pallas_call x1, Pallas kernels, per_device(): pl.pallas_call(gather_kernel, out_shape=(shape((32, 528, 256), BF16), sha...  53.6 us
    pallas_call x1, Pallas kernels, per_device(): pl.pallas_call(attend_kernel, out_shape=shape((512, 256), BF16), in_specs...  8.84 us
    pallas_call x1, Pallas kernels, per_device(): pl.pallas_call(project_kernel, out_shape=(shape((512, 256), BF16), shape(...  6.75 us
    unnamed x15, local copies, waits for them, and re-layouts  3.93 us

profile of v3, /device:TPU:1, one launch (start us, length us, event | category | flops | bytes accessed | tf_op | source)
XLA Modules:
  0.0 162.2 jit_solution(6859574124328301205)
XLA Ops:
  0.6 1.1 convert_reduce_fusion.starts_ref
  1.7 0.0 copy-start.2
  1.7 0.8 select_reduce_fusion.1
  2.5 0.7 subtract_convert_fusion
  3.2 1.8 %fusion = (f32[512,128]{1,0:T(8,128)}, f32[512,128]{1,0:T(8,128)}) fusion(f32[128]{0:T(128)S(1)} %get-tuple-element.24, f32[128]{0:T(128)S(1)} %get-tuple-element.25, f32[512]{0:T(512)S(1)} %subtract_convert_fusion), kind=kLoop, calls=%fused_computation.4 | loop fusion | flops 131072 | bytes 527360 | tf_op jit(solution)/shard_map/mul | solution.py:682
  5.0 1.3 broadcast_in_dim.56.gain_ref
  6.3 6.7 %project.1 = (bf16[512,256]{1,0:T(8,128)(2,1)}, bf16[528,256]{1,0:T(8,128)(2,1)}, bf16[512,256]{1,0:T(8,128)(2,1)}) custom-call(s32[512]{0:T(512)} %base_ref.3, bf16[512,2048]{1,0:T(8,128)(2,1)} %tok_ref.3, bf16[1,2048]{1,0:T(2,128)(2,1)} %broadcast_in_dim.56.gain_ref, bf16[2048,256]{1,0:T(8,128)(2,1)} %wq_ref.1, bf16[2048,128]{1,0:T(8,128)(2,1)} %wk_ref.1, ...), custom_call_target="tpu_custom_call" | custom-call | tf_op jit(solution)/shard_map/project/pallas_call | solution.py:684
  13.0 0.0 copy-done.2
  13.1 53.6 %gather.1 = (bf16[32,528,256]{2,1,0:T(8,128)(2,1)}, bf16[8,4,64,2048]{3,2,1,0:T(8,128)(2,1)}) custom-call(bf16[528,256]{1,0:T(8,128)(2,1)} %get-tuple-element.12.kv_ref, bf16[4,64,2048]{2,1,0:T(8,128)(2,1)} %bitcast.11), custom_call_target="tpu_custom_call" | custom-call | tf_op jit(solution)/shard_map/gather/pallas_call | solution.py:696
  66.7 1.2 slice_reduce_fusion.1
  67.9 0.1 copy.22
  68.0 0.1 reshape.60
  68.1 0.6 select_reduce_fusion.where_ref
  68.7 0.0 copy-start.3
  68.7 0.0 copy-start.1
  68.7 0.0 copy-start.4
  68.7 0.0 copy-start.5
  68.8 8.8 %attend.1.heads_ref = bf16[512,256]{1,0:T(8,128)(2,1)} custom-call(s32[64]{0:T(128)} %select_reduce_fusion.where_ref, s32[512]{0:T(512)} %base_ref.3, s32[8]{0:T(128)} %copy-done.2, s32[32]{0:T(128)} %bitcast.16, s32[1]{0:T(128)} %bitcast.3.me_ref, bf16[512,256]{1,0:T(8,128)(2,1)} %get-tuple-element.14.q_ref, bf16[32,528,256]{2,1,0:T(8,128)(2,1)} %get-tuple-element.13.kv_ref), custom_call_target="tpu_custom_call" | custom-call | tf_op jit(solution)/shard_map/attend/pallas_call | solution.py:714
  77.6 0.0 copy-done.3
  77.6 0.1 slice.16
  77.7 0.1 add_add_fusion
  77.8 0.1 pad_add_fusion
  77.8 0.0 copy-done.1
  77.8 0.1 eq.33
  77.9 0.7 compare_convert_fusion.match_ref
  78.6 0.0 copy-done.4
  78.6 0.6 broadcast_in_dim.64.gain_ref
  79.2 0.0 copy-done.5
  79.2 0.6 broadcast_in_dim.65.final_ref
  79.8 0.0 copy-start
  79.8 77.7 %middle.1 = (bf16[512,256]{1,0:T(8,128)(2,1)}, f32[1,4]{1,0:T(1,128)}, f32[1,4]{1,0:T(1,128)}) custom-call(bf16[512,256]{1,0:T(8,128)(2,1)} %attend.1.heads_ref, bf16[2048,2048]{1,0:T(8,128)(2,1)} %bitcast.10, bf16[512,2048]{1,0:T(8,128)(2,1)} %tok_ref.3, bf16[1,2048]{1,0:T(2,128)(2,1)} %broadcast_in_dim.64.gain_ref, bf16[2048,512]{1,0:T(8,128)(2,1)} %wg_ref.1, ...), custom_call_target="tpu_custom_call" | custom-call | tf_op jit(solution)/shard_map/middle/pallas_call | solution.py:741
  157.5 0.0 copy-done
  157.5 0.8 reshape.57
  158.3 1.7 %copy.26 = bf16[512,256]{1,0:T(8,128)(2,1)} copy(bf16[512,256]{1,0:T(8,128)(2,1)} %get-tuple-element.30) | data formatting | bytes 524288
  159.9 1.1 copy.27
  161.0 1.1 copy.28
  (2 shorter events, 0.0 us)
Async XLA Ops:
  1.7 11.3 %copy-start.2 = (s32[8]{0:T(128)}, s32[8]{0:T(128)S(1)}, u32[]{:S(2)}) copy-start(s32[8]{0:T(128)S(1)} %convert_reduce_fusion.starts_ref) | copy-start | bytes 100
  68.7 8.9 %copy-start.3 = (s32[8]{0:T(128)S(1)}, s32[8]{0:T(128)}, u32[]{:S(2)}) copy-start(s32[8]{0:T(128)} %copy-done.2) | copy-start | bytes 100
  68.7 9.1 %copy-start.1 = (s32[512]{0:T(512)S(1)}, s32[512]{0:T(512)}, u32[]{:S(2)}) copy-start(s32[512]{0:T(512)} %base_ref.3) | copy-start | bytes 6148
  68.7 9.9 %copy-start.4 = (bf16[2048]{0:T(1024)(128)(2,1)S(1)}, bf16[2048]{0:T(1024)(128)(2,1)}, u32[]{:S(2)}) copy-start(bf16[2048]{0:T(1024)(128)(2,1)} %param.22) | copy-start | bytes 12292
  68.7 10.5 %copy-start.5 = (bf16[2048]{0:T(1024)(128)(2,1)S(1)}, bf16[2048]{0:T(1024)(128)(2,1)}, u32[]{:S(2)}) copy-start(bf16[2048]{0:T(1024)(128)(2,1)} %param.26) | copy-start | bytes 12292
  79.8 77.7 %copy-start = (bf16[512,256]{1,0:T(8,128)(2,1)S(1)}, bf16[512,256]{1,0:T(8,128)(2,1)}, u32[]{:S(2)}) copy-start(bf16[512,256]{1,0:T(8,128)(2,1)} %get-tuple-element.17) | copy-start | bytes 786436

commit v4 on v3

--- a/solution.py
+++ b/solution.py
@@ -48,7 +48,7 @@
 
 
 def project_kernel(
-    base_ref, tok_ref, gain_ref, wq_ref, wk_ref, wv_ref, cos_ref, sin_ref, slot_ref,
+    base_ref, tok_ref, gain_ref, wq_ref, wk_ref, wv_ref, cos_ref, sin_ref, slot_ref, live_ref,
     q_ref, kv_ref, cache_ref,
 ):
     gain = gain_ref[...].astype(F32)
@@ -76,7 +76,10 @@
     lax.fori_loop(0, 4, rows_step, 0)
     lane = lax.broadcasted_iota(jnp.int32, (16, 256), 1)
     run = jnp.where(lane < 128, base_ref[0] // 256, base_ref[256] // 256)
-    kv_ref[512:528, :] = run.astype(F32).astype(BF16)
+    run = run.astype(F32)
+    kv_ref[512:528, :] = run.astype(BF16)
+    row = lax.broadcasted_iota(jnp.int32, (16, 256), 0)
+    q_ref[512:528, :] = jnp.where(row == 1, live_ref[...], run).astype(BF16)
     slots = slot_ref[...]
 
     def cache_step(i, carry):
@@ -92,115 +95,91 @@
 PIECE_ROWS = ((0, 256), (256, 272))
 
 
-def gather_kernel(kv_ref, w_ref, kv_all, w_all, own_sem, send_sem, kv_sem, w_sem):
+def gather_kernel(kv_ref, q_ref, w_ref, kv_all, q_all, w_all, own_sem, send_sem, kv_sem, q_sem, w_sem):
     s = lax.axis_index("seq")
     v = lax.axis_index("vocab")
-    c = s % 2
+    z, c, x = s // 4, s % 2, v // 2
     up = (seq_at(s, 1, 0, 0), v)
     down = (seq_at(s, -1, 0, 0), v)
     side = (seq_at(s, 0, 1, 0), v)
     core = (seq_at(s, 0, 0, 1), v)
     right = (s, vocab_at(v, 1, 0))
     left = (s, vocab_at(v, -1, 0))
-    near = (s, vocab_at(v, 0, 1))
-    greet([up, down, side, core, right, left, near])
-
+    greet([up, down, side, core, right, left])
     started = []
+
+    def go(src, dst, recv, peer):
+        copy = pltpu.make_async_remote_copy(
+            src_ref=src, dst_ref=dst, send_sem=send_sem.at[len(started)], recv_sem=recv,
+            device_id=peer, device_id_type=MESH,
+        )
+        copy.start()
+        started.append(copy)
+
+    def take(dst, recv):
+        pltpu.make_async_remote_copy(
+            src_ref=dst, dst_ref=dst, send_sem=send_sem.at[0], recv_sem=recv,
+            device_id=core, device_id_type=MESH,
+        ).wait_recv()
 
     def kv_view(block, p):
         low, count = PIECE_ROWS[p]
         return kv_all.at[block, pl.ds(low, count), :]
 
-    def kv_copy(src, block, p, peer):
-        return pltpu.make_async_remote_copy(
-            src_ref=src, dst_ref=kv_view(block, p), send_sem=send_sem.at[len(started)],
-            recv_sem=kv_sem.at[block, p], device_id=peer, device_id_type=MESH,
-        )
-
-    def w_copy(src, shard, p, peer):
-        return pltpu.make_async_remote_copy(
-            src_ref=src, dst_ref=w_all.at[shard, p], send_sem=send_sem.at[len(started)],
-            recv_sem=w_sem.at[shard, p], device_id=peer, device_id_type=MESH,
-        )
-
-    def go(copy):
-        copy.start()
-        started.append(copy)
-
-    def kv_take(dz, dy, p, peers):
-        block = seq_at(s, dz, dy, 0)
-        kv_copy(kv_view(block, p), block, p, core).wait_recv()
+    def kv_take(dz, p, peers):
+        block = ((z + dz + 8) % 8) * 2 + c
+        take(kv_view(block, p), kv_sem.at[block, p])
         for peer in peers:
-            go(kv_copy(kv_view(block, p), block, p, peer))
-
-    def w_take(dx, dy, p, peers):
-        shard = vocab_at(v, dx, dy)
-        part = 2 * c + p
-        w_copy(w_all.at[shard, part], shard, part, core).wait_recv()
+            go(kv_view(block, p), kv_view(block, p), kv_sem.at[block, p], peer)
+
+    def w_take(dx, p, peers):
+        shard, piece = (x + dx + 4) % 4, 2 * c + p
+        take(w_all.at[shard, piece], w_sem.at[shard, piece])
         for peer in peers:
-            go(w_copy(w_all.at[shard, part], shard, part, peer))
-
-    own = []
+            go(w_all.at[shard, piece], w_all.at[shard, piece], w_sem.at[shard, piece], peer)
+
+    mine = z * 2 + c
     for p in range(2):
         low, count = PIECE_ROWS[p]
-        src = kv_ref.at[pl.ds(low, count), :]
-        for peer in (up, down, side, core):
-            go(kv_copy(src, s, p, peer))
-        part = 2 * c + p
-        for peer in (right, left, near):
-            go(w_copy(w_ref.at[part], v, part, peer))
-    own.append(pltpu.make_async_copy(kv_ref, kv_all.at[s], own_sem.at[0]))
-    own.append(pltpu.make_async_copy(w_ref, w_all.at[v], own_sem.at[1]))
+        for peer in (up, down, core):
+            go(kv_ref.at[pl.ds(low, count), :], kv_view(mine, p), kv_sem.at[mine, p], peer)
+        piece = 2 * c + p
+        for peer in (right, left):
+            go(w_ref.at[piece], w_all.at[x, piece], w_sem.at[x, piece], peer)
+    go(q_ref, q_all, q_sem.at[0], side)
+    own = [
+        pltpu.make_async_copy(kv_ref, kv_all.at[mine], own_sem.at[0]),
+        pltpu.make_async_copy(w_ref, w_all.at[x], own_sem.at[1]),
+    ]
     for copy in own:
         copy.start()
 
     for d in (1, 2):
         for p in range(2):
-            kv_take(-d, 0, p, (up, core))
-            kv_take(d, 0, p, (down, core))
+            kv_take(-d, p, (up, core))
+            kv_take(d, p, (down, core))
+        if d == 1:
+            w_take(-1, 0, (right, core))
+            w_take(1, 0, (core,))
+    w_take(-1, 1, (core,))
+    w_take(1, 1, (left, core))
     for p in range(2):
-        w_take(-1, 0, p, (right, core) if p == 0 else (core,))
-        w_take(1, 0, p, (left, core) if p == 1 else (core,))
+        kv_take(-3, p, (up, core) if p == 0 else (core,))
+        kv_take(3, p, (down, core) if p == 1 else (core,))
     for p in range(2):
-        kv_take(0, 1, p, (up, down, core))
+        w_take(2, p, (core,))
     for p in range(2):
-        w_take(0, 1, p, (right, left, core))
-    for p in range(2):
-        kv_take(-3, 0, p, (up, side, core) if p == 0 else (side, core))
-        kv_take(3, 0, p, (down, side, core) if p == 1 else (side, core))
-    for p in range(2):
-        kv_take(-1, 1, p, (up, core))
-        kv_take(1, 1, p, (down, core))
-    for p in range(2):
-        w_take(2, 0, p, (core,))
-    for p in range(2):
-        kv_take(4, 0, p, (side, core))
-    for p in range(2):
-        w_take(-1, 1, p, (right, core) if p == 0 else (core,))
-        w_take(1, 1, p, (left, core) if p == 1 else (core,))
-    for p in range(2):
-        kv_take(-2, 1, p, (core,))
-        kv_take(2, 1, p, (core,))
-    for p in range(2):
-        kv_take(-3, 1, p, (core,))
-        kv_take(3, 1, p, (core,))
-    for p in range(2):
-        w_take(2, 1, p, (core,))
-    for p in range(2):
-        kv_take(4, 1, p, (core,))
+        kv_take(4, p, (core,))
 
     for dz in range(8):
-        for dy in range(2):
-            for p in range(2):
-                block = seq_at(s, dz, dy, 1)
-                kv_copy(kv_view(block, p), block, p, core).wait_recv()
-    for dx in range(4):
-        for dy in range(2):
-            if (dx, dy) != (0, 0):
-                for p in range(2):
-                    shard = vocab_at(v, dx, dy)
-                    part = 2 * (1 - c) + p
-                    w_copy(w_all.at[shard, part], shard, part, core).wait_recv()
+        for p in range(2):
+            block = ((z + dz) % 8) * 2 + 1 - c
+            take(kv_view(block, p), kv_sem.at[block, p])
+    for dx in range(1, 4):
+        for p in range(2):
+            shard, piece = (x + dx) % 4, 2 * (1 - c) + p
+            take(w_all.at[shard, piece], w_sem.at[shard, piece])
+    take(q_all, q_sem.at[0])
     for copy in own:
         copy.wait()
     for copy in started:
@@ -211,12 +190,38 @@
 
 
 def attend_kernel(
-    where_ref, base_ref, starts_ref, live_ref, me_ref, q_ref, kv_ref, o_ref,
+    runs_ref, tail_ref, base_ref, starts_ref, live_ref, me_ref, q_ref, other_ref, kv_ref, o_ref, st_ref,
     buf, sem, q_rows, top, total, acc, scores0, scores1, probs0, probs1, keep0, keep1,
+    table, sorted_run, sorted_entry, before,
 ):
     me = me_ref[0]
+    my_y = (me // 2) % 2
+    other = me + 2 - 4 * my_y
     all_scores, all_probs, all_keep = (scores0, scores1), (probs0, probs1), (keep0, keep1)
-    base0, base1 = base_ref[0], base_ref[256]
+    q_run = [base_ref[0] // 256, base_ref[256] // 256, tail_ref[0], tail_ref[1]]
+
+    def clear(i, carry):
+        table[i] = -1
+        return carry
+
+    def enter(i, carry):
+        table[runs_ref[i]] = i
+        return carry
+
+    def gather_up(i, count):
+        before[i] = count
+        entry = table[i]
+
+        @pl.when(entry >= 0)
+        def _():
+            sorted_run[count] = i
+            sorted_entry[count] = entry
+
+        return jnp.where(entry >= 0, count + 1, count)
+
+    lax.fori_loop(0, 64, clear, 0)
+    lax.fori_loop(0, 32, enter, 0)
+    before[64] = lax.fori_loop(0, 64, gather_up, 0)
 
     def low_of(position):
         low = starts_ref[0]
@@ -224,17 +229,31 @@
             low = jnp.where(starts_ref[r] <= position, starts_ref[r], low)
         return low
 
-    first0, first1 = low_of(base0) // 256, low_of(base1) // 256
-    last0, last1 = low_of(base0 + 255), low_of(base1 + 255)
-    count0 = base0 // 256 - first0 + 1
-    count1 = base1 // 256 - first1 + 1
-    n = count0 + count1
+    lasts, shifts, offsets = [], [], [0]
+    for r in range(4):
+        first = before[low_of(q_run[r] * 256) // 256]
+        lasts.append(low_of(q_run[r] * 256 + 255))
+        shifts.append(first - offsets[-1])
+        offsets.append(offsets[-1] + before[q_run[r] + 1] - first)
+    n = offsets[4]
+
+    def choose(i, values):
+        out = values[0]
+        for r in range(1, 4):
+            out = jnp.where(i >= offsets[r], values[r], out)
+        return out
+
+    def half(i):
+        return choose(i, [0, 1, 2, 3])
+
+    def place(i):
+        return jnp.clip(i + choose(i, shifts), 0, 31)
 
     def key_run(i):
-        return jnp.where(i < count0, first0 + i, first1 + i - count0)
+        return sorted_run[place(i)]
 
     def fetch(i):
-        entry = where_ref[key_run(i)]
+        entry = sorted_entry[place(i)]
         slot = i % SLOTS
         return pltpu.make_async_copy(
             kv_ref.at[entry // 2, pl.ds((entry % 2) * 256, 256), :], buf.at[slot], sem.at[slot]
@@ -246,10 +265,11 @@
         def _():
             fetch(i).start()
 
-    for r in range(2):
+    for r in range(4):
+        source = q_ref if r < 2 else other_ref
         for h in range(2):
-            q_rows[r, pl.ds(h * 256, 256), :] = q_ref[
-                pl.ds(r * 256, 256), pl.ds(h * 128, 128)
+            q_rows[r, pl.ds(h * 256, 256), :] = source[
+                pl.ds((r % 2) * 256, 256), pl.ds(h * 128, 128)
             ]
     top[...] = jnp.full_like(top, neg_fill)
     total[...] = jnp.zeros_like(total)
@@ -257,9 +277,6 @@
     buf[SLOTS - 1] = jnp.zeros((256, 256), BF16)
     probs1[...] = jnp.zeros_like(probs1)
     keep1[...] = jnp.ones_like(keep1)
-
-    def half(i):
-        return jnp.where(i < count0, 0, 1)
 
     def score(i, into):
         into[...] = lax.dot_general(
@@ -308,9 +325,13 @@
             fetch(i + 1).wait()
 
         run = key_run(i)
-        base = jnp.where(i < count0, base0, base1)
-        last_low = jnp.where(i < count0, last0, last1)
-        live = live_ref[(me - where_ref[run] // 2 + 32) % 32] > 0
+        base = choose(i, q_run) * 256
+        last_low = choose(i, lasts)
+        slot = sorted_entry[place(i)] // 2
+        block = (slot // 2) * 4 + my_y * 2 + slot % 2
+        live = jnp.where(
+            i < offsets[2], live_ref[(me - block + 32) % 32], tail_ref[2 + (other - block + 32) % 32]
+        ) > 0
         whole = (run * 256 < base) & (run * 256 >= last_low)
 
         @pl.when(live & whole)
@@ -353,20 +374,24 @@
     def _():
         collect(n - 1, 1)
 
-    for r in range(2):
-        done = acc[r] / total[r]
-        for h in range(2):
-            o_ref[pl.ds(r * 256, 256), pl.ds(h * 128, 128)] = jnp.transpose(
-                done[:, h * 256 : (h + 1) * 256]
-            ).astype(BF16)
+    for r in range(4):
+        weight = total[r]
+        done = (acc[r] * jnp.where(weight > 0, 1.0 / weight, 0.0)).astype(BF16)
+        for part in range(2):
+            k = 2 * (r % 2) + part
+            for h in range(2):
+                low = h * 256 + part * 128
+                o_ref[r // 2, k, h * 128 : (h + 1) * 128, :] = done[:, low : low + 128]
+                st_ref[r // 2, k, h : h + 1, :] = top[r, :, low : low + 128]
+                st_ref[r // 2, k, 2 + h : 3 + h, :] = weight[:, low : low + 128]
 
 
 def middle_kernel(
-    heads_ref, w_ref, tok_ref, gain_ref, wg_ref, wu_ref, wd_ref, match_ref, final_ref, head_ref,
+    heads_ref, stats_ref, w_ref, tok_ref, gain_ref, wg_ref, wu_ref, wd_ref, match_ref, final_ref, head_ref,
     out_ref, rms_ref, top_ref,
-    heads, w, tok_rows, tok_cols, wg, wu, wd, att, att_send, att_cols, normed, act, part, fwd_in,
+    heads, stats, joined, near_send, near_got, w, tok_rows, tok_cols, wg, wu, wd, att, att_send, att_cols, normed, act, part, fwd_in,
     x_in, y_in, head, row_send, seq_got, wide_send, wide_got, last_send, last_got, max_send, seq_max, vocab_max,
-    load_sem, send_sem, head_recv, norm_recv, att_recv, fwd_recv, x_recv, y_recv,
+    load_sem, send_sem, head_recv, stat_recv, near_recv, norm_recv, att_recv, fwd_recv, x_recv, y_recv,
     row_recv, wide_recv, last_recv, max_recv, top_recv,
 ):
     s = lax.axis_index("seq")
@@ -382,12 +407,21 @@
         pltpu.make_async_copy(wg_ref, wg, load_sem.at[3]),
         pltpu.make_async_copy(wu_ref, wu, load_sem.at[4]),
         pltpu.make_async_copy(wd_ref, wd, load_sem.at[5]),
-        pltpu.make_async_copy(heads_ref.at[rows, :], heads.at[v], load_sem.at[6]),
+        pltpu.make_async_copy(heads_ref.at[0, v // 2], heads.at[v // 2, (s // 2) % 2], load_sem.at[6]),
+        pltpu.make_async_copy(stats_ref.at[0, v // 2], stats.at[v // 2, (s // 2) % 2], load_sem.at[9]),
         pltpu.make_async_copy(head_ref, head, load_sem.at[8]),
     ]
     for copy in loads:
         copy.start()
-    greet([(s, other) for other in others] + [(other, v) for other in seqs])
+    x = v // 2
+    y = v % 2
+    my_y = (s // 2) % 2
+    across = seq_at(s, 0, 1, 0)
+    greet(
+        [(s, other) for other in others]
+        + [(other, v) for other in seqs]
+        + [(across, vocab_at(v, dx, 0)) for dx in range(1, 4)]
+    )
     sent = []
 
     def go(src, dst, recv, peer):
@@ -404,21 +438,51 @@
             device_id=(s, others[0]), device_id_type=MESH,
         ).wait_recv()
 
-    for other in others:
-        src = heads_ref.at[pl.ds(pl.multiple_of(other * 64, 64), 64), :]
-        go(src, heads.at[v], head_recv.at[v], (s, other))
-    for other in others:
-        take(heads.at[other], head_recv.at[other])
-    for i in (0, 1, 6):
+    for dx in (2, 1, 3, 0):
+        target = (x + dx) % 4
+        for which in (1, 0):
+            if (dx, which) != (0, 0):
+                peer = (across if which else s, vocab_at(v, dx, 0))
+                go(heads_ref.at[which, target], heads.at[x, my_y], head_recv.at[x, my_y], peer)
+                go(stats_ref.at[which, target], stats.at[x, my_y], stat_recv.at[x, my_y], peer)
+    for i in (0, 1, 6, 7):
         loads[i].wait()
+    for dx in range(4):
+        source = (x + dx) % 4
+        for which in range(2):
+            if (dx, which) != (0, 0):
+                held = (my_y + which) % 2
+                take(heads.at[source, held], head_recv.at[source, held])
+                take(stats.at[source, held], stat_recv.at[source, held])
+    for k in range(4):
+        for h in range(2):
+            tops = [stats[k, i, h : h + 1, :] for i in range(2)]
+            best = jnp.maximum(tops[0], tops[1])
+            weights = [stats[k, i, 2 + h : 3 + h, :] * jnp.exp2(tops[i] - best) for i in range(2)]
+            scale = 1.0 / (weights[0] + weights[1])
+            span = pl.ds(h * 128, 128)
+            joined[k, span, :] = (
+                heads[k, 0, span, :].astype(F32) * (weights[0] * scale)
+                + heads[k, 1, span, :].astype(F32) * (weights[1] * scale)
+            ).astype(BF16)
+
+    near = vocab_at(v, 0, 1)
+    for j in range(4):
+        total = jnp.zeros((128, 512), F32)
+        for k in range(4):
+            total += lax.dot_general(
+                joined[k], w[k * 256 : (k + 1) * 256, j * 512 : (j + 1) * 512],
+                (((0,), (0,)), ((), ())), preferred_element_type=F32,
+            )
+        att[:, j * 512 : (j + 1) * 512] = jnp.where(y == 0, total[0:64], total[64:128])
+        near_send[j] = jnp.where(y == 0, total[64:128], total[0:64]).astype(BF16)
+        go(near_send.at[j], near_got.at[j], near_recv.at[j], (s, near))
+    for j in range(4):
+        take(near_got.at[j], near_recv.at[j])
 
     def project(j, square):
         wide = pl.ds(pl.multiple_of(j * 512, 512), 512)
-        total = jnp.dot(heads[0], w[0:256, wide], preferred_element_type=F32)
-        for k in range(1, 8):
-            total += jnp.dot(
-                heads[k], w[k * 256 : (k + 1) * 256, wide], preferred_element_type=F32
-            )
+        total = att[:, wide] + near_got[j].astype(F32)
         att_send[2 * j] = total[:, 0:256].astype(BF16)
         att_send[2 * j + 1] = total[:, 256:512].astype(BF16)
         residual = tok_rows[:, wide].astype(F32) + total
@@ -431,7 +495,7 @@
     normed[2 * v] = mine[0:32]
     normed[2 * v + 1] = mine[32:64]
 
-    right, left, near = vocab_at(v, 1, 0), vocab_at(v, -1, 0), vocab_at(v, 0, 1)
+    right, left = vocab_at(v, 1, 0), vocab_at(v, -1, 0)
 
     def pass_on(owner, p, other):
         view = normed.at[2 * owner + p]
@@ -474,9 +538,6 @@
 
     for i in (3, 4, 5):
         loads[i].wait()
-    x = v // 2
-    y = v % 2
-
     def feed(values):
         gate = jnp.dot(values, wg[...], preferred_element_type=F32)
         upward = jnp.dot(values, wu[...], preferred_element_type=F32)
@@ -601,7 +662,7 @@
         )
     )
     final = final * inverse * spread
-    loads[7].wait()
+    loads[8].wait()
     logits = jnp.zeros((16, 360), F32)
     for q in range(4):
         turned = final if q == 0 else pltpu.roll(final, 16 - 4 * q, axis=0)
@@ -683,56 +744,62 @@
 
     query, kv, cache = pl.pallas_call(
         project_kernel,
-        out_shape=(shape((512, 256), BF16), shape((528, 256), BF16), shape((512, 256), BF16)),
-        in_specs=[SM] + [VM] * 8,
+        out_shape=(shape((528, 256), BF16), shape((528, 256), BF16), shape((512, 256), BF16)),
+        in_specs=[SM] + [VM] * 9,
         out_specs=(VM, VM, VM),
         compiler_params=params(),
         name="project",
     )(
         token_order, tokens, attention_gain[None], query_weight, key_weight, value_weight, cos, sin,
-        cache_slots[None],
+        cache_slots[None], jnp.pad(live_blocks.astype(F32), ((0, 0), (0, 224))),
     )
 
-    kv_all, w_all = pl.pallas_call(
+    kv_all, q_other, w_all = pl.pallas_call(
         gather_kernel,
-        out_shape=(shape((32, 528, 256), BF16), shape((8, 4, 64, 2048), BF16)),
-        in_specs=[VM, HB],
-        out_specs=(HB, HB),
+        out_shape=(
+            shape((16, 528, 256), BF16), shape((528, 256), BF16), shape((4, 4, 64, 2048), BF16),
+        ),
+        in_specs=[VM, VM, HB],
+        out_specs=(HB, HB, HB),
         scratch_shapes=[
             pltpu.SemaphoreType.DMA((2,)),
-            pltpu.SemaphoreType.DMA((128,)),
-            pltpu.SemaphoreType.DMA((32, 2)),
-            pltpu.SemaphoreType.DMA((8, 4)),
+            pltpu.SemaphoreType.DMA((96,)),
+            pltpu.SemaphoreType.DMA((16, 2)),
+            pltpu.SemaphoreType.DMA((1,)),
+            pltpu.SemaphoreType.DMA((4, 4)),
         ],
         compiler_params=params(0),
         name="gather",
-    )(kv, out_weight.reshape(4, 64, 2048))
-
-    runs = jnp.stack([kv_all[:, 512, 0], kv_all[:, 512, 128]], axis=1).astype(jnp.int32).reshape(64)
-    entry = jnp.arange(64, dtype=jnp.int32)
-    where = jnp.sum(jnp.where(runs[None, :] == entry[:, None], entry[None, :], 0), axis=1)
-    heads = pl.pallas_call(
+    )(kv, query, out_weight.reshape(4, 64, 2048))
+
+    runs = jnp.stack([kv_all[:, 512, 0], kv_all[:, 512, 128]], axis=1).astype(jnp.int32).reshape(32)
+    tail = jnp.concatenate([q_other[512, 0:256:128], q_other[513, 0:32]]).astype(jnp.int32)
+    heads, stats = pl.pallas_call(
         attend_kernel,
-        out_shape=shape((512, 256), BF16),
-        in_specs=[SM, SM, SM, SM, SM, VM, HB],
-        out_specs=VM,
+        out_shape=(shape((2, 4, 256, 128), BF16), shape((2, 4, 8, 128), F32)),
+        in_specs=[SM] * 6 + [VM, VM, HB],
+        out_specs=(VM, VM),
         scratch_shapes=[
             pltpu.VMEM((SLOTS, 256, 256), BF16),
             pltpu.SemaphoreType.DMA((SLOTS,)),
-            pltpu.VMEM((2, 512, 128), BF16),
-            pltpu.VMEM((2, 1, 512), F32),
-            pltpu.VMEM((2, 1, 512), F32),
-            pltpu.VMEM((2, 128, 512), F32),
+            pltpu.VMEM((4, 512, 128), BF16),
+            pltpu.VMEM((4, 1, 512), F32),
+            pltpu.VMEM((4, 1, 512), F32),
+            pltpu.VMEM((4, 128, 512), F32),
             pltpu.VMEM((256, 512), F32),
             pltpu.VMEM((256, 512), F32),
             pltpu.VMEM((256, 512), BF16),
             pltpu.VMEM((256, 512), BF16),
             pltpu.VMEM((1, 512), F32),
             pltpu.VMEM((1, 512), F32),
+            pltpu.SMEM((64,), jnp.int32),
+            pltpu.SMEM((32,), jnp.int32),
+            pltpu.SMEM((32,), jnp.int32),
+            pltpu.SMEM((65,), jnp.int32),
         ],
         compiler_params=params(),
         name="attend",
-    )(where, token_order, starts, live_blocks[0], me[None], query, kv_all)
+    )(runs, tail, token_order, starts, live_blocks[0], me[None], query, q_other, kv_all)
 
     ends = jnp.concatenate([starts[1:REQS], jnp.full((1,), segment_ids.shape[0], jnp.int32)])
     last_index = jnp.concatenate([ends - 1, ends - 1])
@@ -741,11 +808,15 @@
     hidden, rms, top = pl.pallas_call(
         middle_kernel,
         out_shape=(shape((512, 256), BF16), shape((1, REQS), F32), shape((1, REQS), F32)),
-        in_specs=[VM, HB, HB, VM, HB, HB, HB, VM, VM, HB],
+        in_specs=[VM, VM, HB, HB, VM, HB, HB, HB, VM, VM, HB],
         out_specs=(VM, VM, VM),
         scratch_shapes=[
-            pltpu.VMEM((8, 64, 256), BF16),
-            pltpu.VMEM((2048, 2048), BF16),
+            pltpu.VMEM((4, 2, 256, 128), BF16),
+            pltpu.VMEM((4, 2, 8, 128), F32),
+            pltpu.VMEM((4, 256, 128), BF16),
+            pltpu.VMEM((4, 64, 512), BF16),
+            pltpu.VMEM((4, 64, 512), BF16),
+            pltpu.VMEM((1024, 2048), BF16),
             pltpu.VMEM((64, 2048), BF16),
             pltpu.VMEM((512, 256), BF16),
             pltpu.VMEM((2048, 512), BF16),
@@ -770,13 +841,13 @@
             pltpu.VMEM((2, 8, 128), F32),
             pltpu.VMEM((32, 8, 128), F32),
             pltpu.VMEM((8, 8, 128), F32),
-            dma((9,)), dma((176,)), dma((8,)), dma((8, 2)), dma((8,)), dma((4, 2)), dma((4, 2, 2)), dma((4,)),
+            dma((10,)), dma((192,)), dma((4, 2)), dma((4, 2)), dma((4,)), dma((8, 2)), dma((8,)), dma((4, 2)), dma((4, 2, 2)), dma((4,)),
             dma((32,)), dma((8,)), dma((8,)), dma((32,)), dma((8,)),
         ],
         compiler_params=params(1),
         name="middle",
     )(
-        heads, w_all.reshape(2048, 2048), tokens, forward_gain[None], gate_weight, up_weight,
+        heads, stats, w_all.reshape(1024, 2048), tokens, forward_gain[None], gate_weight, up_weight,
         down_weight, match, final_gain[None], head_weight,
     )
     return (hidden, cache.reshape(512, 2, 128), rms.reshape(REQS), top.reshape(REQS))

time: 164 us -> 168 us (1.024)
  local copies, waits for them, and re-layouts: 8.73 us -> 11.2 us
  Pallas kernels: 147 us -> 149 us
    pallas_call x1, Pallas kernels: 77.7 us -> 88.7 us  [per_device(): pl.pallas_call(middle_kernel, out_shape=(shape((512, 256), BF16), shape((...]
    pallas_call x3, Pallas kernels: 69.2 us -> 60.5 us  [the longest x1 41.7 us: per_device(): pl.pallas_call(gather_kernel, out_shape=(shape((16, 528, 256), BF16), sha...]
where the time goes in v4:
time: 168 us
  Pallas kernels  149 us (89%)
  local copies, waits for them, and re-layouts  11.2 us (7%)
  other arithmetic  6.47 us (4%)
    pallas_call x1, Pallas kernels, per_device(): pl.pallas_call(middle_kernel, out_shape=(shape((512, 256), BF16), shape((...  88.7 us
    pallas_call x1, Pallas kernels, per_device(): pl.pallas_call(gather_kernel, out_shape=(shape((16, 528, 256), BF16), sha...  41.7 us
    pallas_call x1, Pallas kernels, per_device(): pl.pallas_call(attend_kernel, out_shape=(shape((2, 4, 256, 128), BF16), s...  12 us
    pallas_call x1, Pallas kernels, per_device(): pl.pallas_call(project_kernel, out_shape=(shape((528, 256), BF16), shape(...  6.78 us
    unnamed x15, local copies, waits for them, and re-layouts  4.04 us

profile of v4, /device:TPU:1, one launch (start us, length us, event | category | flops | bytes accessed | tf_op | source)
XLA Modules:
  0.0 167.5 jit_solution(10199804252784099380)
XLA Ops:
  0.6 1.1 convert_reduce_fusion.starts_ref
  1.7 0.0 copy-start.2
  1.7 0.8 select_reduce_fusion
  2.5 0.7 subtract_convert_fusion
  3.2 1.8 %fusion = (f32[512,128]{1,0:T(8,128)}, f32[512,128]{1,0:T(8,128)}) fusion(f32[128]{0:T(128)S(1)} %get-tuple-element.30, f32[128]{0:T(128)S(1)} %get-tuple-element.31, f32[512]{0:T(512)S(1)} %subtract_convert_fusion), kind=kLoop, calls=%fused_computation.4 | loop fusion | flops 131072 | bytes 527360 | tf_op jit(solution)/shard_map/mul | solution.py:743
  5.0 1.3 broadcast_in_dim.42.gain_ref
  6.3 0.7 convert_element_type.34
  7.0 0.6 pad.4.live_ref
  7.5 6.8 %project.1 = (bf16[528,256]{1,0:T(8,128)(2,1)}, bf16[528,256]{1,0:T(8,128)(2,1)}, bf16[512,256]{1,0:T(8,128)(2,1)}) custom-call(s32[512]{0:T(512)} %base_ref.3, bf16[512,2048]{1,0:T(8,128)(2,1)} %tok_ref.3, bf16[1,2048]{1,0:T(2,128)(2,1)} %broadcast_in_dim.42.gain_ref, bf16[2048,256]{1,0:T(8,128)(2,1)} %wq_ref.1, bf16[2048,128]{1,0:T(8,128)(2,1)} %wk_ref.1, ...), custom_call_target="tpu_custom_call" | custom-call | tf_op jit(solution)/shard_map/project/pallas_call | solution.py:745
  14.3 0.0 copy-done.2
  14.3 41.7 %gather.1 = (bf16[16,528,256]{2,1,0:T(8,128)(2,1)}, bf16[528,256]{1,0:T(8,128)(2,1)}, bf16[4,4,64,2048]{3,2,1,0:T(8,128)(2,1)}) custom-call(bf16[528,256]{1,0:T(8,128)(2,1)} %get-tuple-element.15.kv_ref, bf16[528,256]{1,0:T(8,128)(2,1)} %get-tuple-element.16.q_ref, bf16[4,64,2048]{2,1,0:T(8,128)(2,1)} %bitcast.14), custom_call_target="tpu_custom_call" | custom-call | tf_op jit(solution)/shard_map/gather/pallas_call | solution.py:757
  56.0 0.8 slice.22
  56.8 0.7 slice_bitcast_fusion
  57.5 0.6 maximum_convert_fusion.1.tail_ref
  58.1 1.0 slice_reduce_fusion.1
  59.1 0.1 copy.22
  59.1 0.6 reshape.57.runs_ref
  59.7 0.0 copy-start.3
  59.8 0.0 copy-start.1
  59.8 0.0 copy-start.4
  59.8 0.0 copy-start.5
  59.8 12.0 %attend.1 = (bf16[2,4,256,128]{3,2,1,0:T(8,128)(2,1)}, f32[2,4,8,128]{3,2,1,0:T(8,128)}) custom-call(s32[32]{0:T(128)} %reshape.57.runs_ref, s32[34]{0:T(128)} %maximum_convert_fusion.1.tail_ref, s32[512]{0:T(512)} %base_ref.3, s32[8]{0:T(128)} %copy-done.2, s32[32]{0:T(128)} %bitcast.19, s32[1]{0:T(128)} %bitcast.5.me_ref, ...), custom_call_target="tpu_custom_call" | custom-call | tf_op jit(solution)/shard_map/attend/pallas_call | solution.py:777
  71.8 0.0 copy-done.3
  71.8 0.1 slice.24
  71.9 0.1 add_add_fusion
  71.9 0.1 pad_add_fusion
  72.0 0.0 copy-done.1
  72.0 0.1 eq.17
  72.1 0.7 compare_convert_fusion.match_ref
  72.8 0.0 copy-done.4
  72.8 0.6 broadcast_in_dim.48.gain_ref
  73.4 0.0 copy-done.5
  73.4 0.6 broadcast_in_dim.49.final_ref
  74.0 0.0 copy-start
  74.0 88.7 %middle.1 = (bf16[512,256]{1,0:T(8,128)(2,1)}, f32[1,4]{1,0:T(1,128)}, f32[1,4]{1,0:T(1,128)}) custom-call(bf16[2,4,256,128]{3,2,1,0:T(8,128)(2,1)} %get-tuple-element.19.heads_ref, f32[2,4,8,128]{3,2,1,0:T(8,128)} %get-tuple-element.20.stats_ref, bf16[1024,2048]{1,0:T(8,128)(2,1)} %bitcast.13, bf16[512,2048]{1,0:T(8,128)(2,1)} %tok_ref.3, ...), custom_call_target="tpu_custom_call" | custom-call | tf_op jit(solution)/shard_map/middle/pallas_call | solution.py:808
  162.7 0.0 copy-done
  162.8 0.8 reshape.54
  163.5 1.7 copy.26
  165.2 1.2 copy.27
  166.4 1.2 copy.28
  (2 shorter events, 0.0 us)
Async XLA Ops:
  1.7 12.6 %copy-start.2 = (s32[8]{0:T(128)}, s32[8]{0:T(128)S(1)}, u32[]{:S(2)}) copy-start(s32[8]{0:T(128)S(1)} %convert_reduce_fusion.starts_ref) | copy-start | bytes 100
  59.7 12.0 %copy-start.3 = (s32[8]{0:T(128)S(1)}, s32[8]{0:T(128)}, u32[]{:S(2)}) copy-start(s32[8]{0:T(128)} %copy-done.2) | copy-start | bytes 100
  59.8 12.3 %copy-start.1 = (s32[512]{0:T(512)S(1)}, s32[512]{0:T(512)}, u32[]{:S(2)}) copy-start(s32[512]{0:T(512)} %base_ref.3) | copy-start | bytes 6148
  59.8 13.0 %copy-start.4 = (bf16[2048]{0:T(1024)(128)(2,1)S(1)}, bf16[2048]{0:T(1024)(128)(2,1)}, u32[]{:S(2)}) copy-start(bf16[2048]{0:T(1024)(128)(2,1)} %param.22) | copy-start | bytes 12292
  59.8 13.6 %copy-start.5 = (bf16[2048]{0:T(1024)(128)(2,1)S(1)}, bf16[2048]{0:T(1024)(128)(2,1)}, u32[]{:S(2)}) copy-start(bf16[2048]{0:T(1024)(128)(2,1)} %param.26) | copy-start | bytes 12292
  74.0 88.8 %copy-start = (bf16[512,256]{1,0:T(8,128)(2,1)S(1)}, bf16[512,256]{1,0:T(8,128)(2,1)}, u32[]{:S(2)}) copy-start(bf16[512,256]{1,0:T(8,128)(2,1)} %get-tuple-element.23) | copy-start | bytes 786436

commit v5 on v4

--- a/solution.py
+++ b/solution.py
@@ -92,10 +92,12 @@
     lax.fori_loop(0, 4, cache_step, 0)
 
 
-PIECE_ROWS = ((0, 256), (256, 272))
-
-
-def gather_kernel(kv_ref, q_ref, w_ref, kv_all, q_all, w_all, own_sem, send_sem, kv_sem, q_sem, w_sem):
+PIECE_ROWS = ((0, 128), (128, 128), (256, 128), (384, 144))
+
+
+def gather_kernel(
+    kv_ref, q_ref, w_ref, kv_all, q_all, w_all, tail_ref, tails, own_sem, send_sem, kv_sem, q_sem, w_sem
+):
     s = lax.axis_index("seq")
     v = lax.axis_index("vocab")
     z, c, x = s // 4, s % 2, v // 2
@@ -139,23 +141,20 @@
             go(w_all.at[shard, piece], w_all.at[shard, piece], w_sem.at[shard, piece], peer)
 
     mine = z * 2 + c
-    for p in range(2):
+    for p in range(4):
         low, count = PIECE_ROWS[p]
         for peer in (up, down, core):
             go(kv_ref.at[pl.ds(low, count), :], kv_view(mine, p), kv_sem.at[mine, p], peer)
+    for p in range(2):
         piece = 2 * c + p
         for peer in (right, left):
             go(w_ref.at[piece], w_all.at[x, piece], w_sem.at[x, piece], peer)
     go(q_ref, q_all, q_sem.at[0], side)
-    own = [
-        pltpu.make_async_copy(kv_ref, kv_all.at[mine], own_sem.at[0]),
-        pltpu.make_async_copy(w_ref, w_all.at[x], own_sem.at[1]),
-    ]
-    for copy in own:
-        copy.start()
+    own = pltpu.make_async_copy(kv_ref, kv_all.at[mine], own_sem.at[0])
+    own.start()
 
     for d in (1, 2):
-        for p in range(2):
+        for p in range(4):
             kv_take(-d, p, (up, core))
             kv_take(d, p, (down, core))
         if d == 1:
@@ -163,25 +162,40 @@
             w_take(1, 0, (core,))
     w_take(-1, 1, (core,))
     w_take(1, 1, (left, core))
-    for p in range(2):
-        kv_take(-3, p, (up, core) if p == 0 else (core,))
-        kv_take(3, p, (down, core) if p == 1 else (core,))
+    for p in range(4):
+        kv_take(-3, p, (up, core) if p < 2 else (core,))
+        kv_take(3, p, (down, core) if p >= 2 else (core,))
     for p in range(2):
         w_take(2, p, (core,))
-    for p in range(2):
+    for p in range(4):
         kv_take(4, p, (core,))
 
     for dz in range(8):
-        for p in range(2):
+        for p in range(4):
             block = ((z + dz) % 8) * 2 + 1 - c
             take(kv_view(block, p), kv_sem.at[block, p])
+    take(q_all, q_sem.at[0])
+    own.wait()
+    ends = [
+        pltpu.make_async_copy(kv_all.at[:, pl.ds(512, 16), :], tails.at[pl.ds(0, 16)], own_sem.at[0]),
+        pltpu.make_async_copy(q_all.at[pl.ds(512, 16), :], tails.at[16], own_sem.at[1]),
+    ]
+    for copy in ends:
+        copy.start()
     for dx in range(1, 4):
         for p in range(2):
             shard, piece = (x + dx) % 4, 2 * (1 - c) + p
             take(w_all.at[shard, piece], w_sem.at[shard, piece])
-    take(q_all, q_sem.at[0])
-    for copy in own:
+    for copy in ends:
         copy.wait()
+    rows = tails[0:16].astype(F32)[:, 0, :].astype(jnp.int32)
+    tail_ref[0:16, :] = rows[:, 0:128]
+    tail_ref[16:32, :] = rows[:, 128:256]
+    rows = tails[16].astype(F32)[0:8, :].astype(jnp.int32)
+    tail_ref[32:33, :] = rows[0:1, 0:128]
+    tail_ref[33:34, :] = rows[0:1, 128:256]
+    tail_ref[34:35, :] = rows[1:2, 0:128]
+    tail_ref[35:40, :] = jnp.zeros((5, 128), jnp.int32)
     for copy in started:
         copy.wait_send()
 
@@ -190,7 +204,7 @@
 
 
 def attend_kernel(
-    runs_ref, tail_ref, base_ref, starts_ref, live_ref, me_ref, q_ref, other_ref, kv_ref, o_ref, st_ref,
+    tail_ref, base_ref, starts_ref, live_ref, me_ref, q_ref, other_ref, kv_ref, o_ref, st_ref,
     buf, sem, q_rows, top, total, acc, scores0, scores1, probs0, probs1, keep0, keep1,
     table, sorted_run, sorted_entry, before,
 ):
@@ -198,14 +212,14 @@
     my_y = (me // 2) % 2
     other = me + 2 - 4 * my_y
     all_scores, all_probs, all_keep = (scores0, scores1), (probs0, probs1), (keep0, keep1)
-    q_run = [base_ref[0] // 256, base_ref[256] // 256, tail_ref[0], tail_ref[1]]
+    q_run = [base_ref[0] // 256, base_ref[256] // 256, tail_ref[32, 0], tail_ref[33, 0]]
 
     def clear(i, carry):
         table[i] = -1
         return carry
 
     def enter(i, carry):
-        table[runs_ref[i]] = i
+        table[tail_ref[i, 0]] = i
         return carry
 
     def gather_up(i, count):
@@ -256,7 +270,7 @@
         entry = sorted_entry[place(i)]
         slot = i % SLOTS
         return pltpu.make_async_copy(
-            kv_ref.at[entry // 2, pl.ds((entry % 2) * 256, 256), :], buf.at[slot], sem.at[slot]
+            kv_ref.at[entry % 16, pl.ds((entry // 16) * 256, 256), :], buf.at[slot], sem.at[slot]
         )
 
     for i in range(SLOTS - 2):
@@ -327,24 +341,24 @@
         run = key_run(i)
         base = choose(i, q_run) * 256
         last_low = choose(i, lasts)
-        slot = sorted_entry[place(i)] // 2
+        slot = sorted_entry[place(i)] % 16
         block = (slot // 2) * 4 + my_y * 2 + slot % 2
         live = jnp.where(
-            i < offsets[2], live_ref[(me - block + 32) % 32], tail_ref[2 + (other - block + 32) % 32]
+            i < offsets[2], live_ref[(me - block + 32) % 32], tail_ref[34, (other - block + 32) % 32]
         ) > 0
         whole = (run * 256 < base) & (run * 256 >= last_low)
 
         @pl.when(live & whole)
         def _():
+            weigh(i, parity, False, base)
             score(i + 1, all_scores[1 - parity])
             collect(i - 1, 1 - parity)
-            weigh(i, parity, False, base)
 
         @pl.when(live & jnp.logical_not(whole))
         def _():
+            weigh(i, parity, True, base)
             score(i + 1, all_scores[1 - parity])
             collect(i - 1, 1 - parity)
-            weigh(i, parity, True, base)
 
         @pl.when(jnp.logical_not(live))
         def _():
@@ -387,7 +401,7 @@
 
 
 def middle_kernel(
-    heads_ref, stats_ref, w_ref, tok_ref, gain_ref, wg_ref, wu_ref, wd_ref, match_ref, final_ref, head_ref,
+    heads_ref, stats_ref, w_ref, w_own, tok_ref, gain_ref, wg_ref, wu_ref, wd_ref, match_ref, final_ref, head_ref,
     out_ref, rms_ref, top_ref,
     heads, stats, joined, near_send, near_got, w, tok_rows, tok_cols, wg, wu, wd, att, att_send, att_cols, normed, act, part, fwd_in,
     x_in, y_in, head, row_send, seq_got, wide_send, wide_got, last_send, last_got, max_send, seq_max, vocab_max,
@@ -401,7 +415,7 @@
     cols = pl.ds(pl.multiple_of(v * 256, 256), 256)
     rows = pl.ds(pl.multiple_of(v * 64, 64), 64)
     loads = [
-        pltpu.make_async_copy(w_ref, w, load_sem.at[0]),
+        pltpu.make_async_copy(w_own, w.at[v // 2], load_sem.at[0]),
         pltpu.make_async_copy(tok_ref.at[rows, :], tok_rows, load_sem.at[1]),
         pltpu.make_async_copy(tok_ref.at[:, cols], tok_cols, load_sem.at[2]),
         pltpu.make_async_copy(wg_ref, wg, load_sem.at[3]),
@@ -410,6 +424,11 @@
         pltpu.make_async_copy(heads_ref.at[0, v // 2], heads.at[v // 2, (s // 2) % 2], load_sem.at[6]),
         pltpu.make_async_copy(stats_ref.at[0, v // 2], stats.at[v // 2, (s // 2) % 2], load_sem.at[9]),
         pltpu.make_async_copy(head_ref, head, load_sem.at[8]),
+    ] + [
+        pltpu.make_async_copy(
+            w_ref.at[(v // 2 + d) % 4], w.at[(v // 2 + d) % 4], load_sem.at[9 + d]
+        )
+        for d in range(1, 4)
     ]
     for copy in loads:
         copy.start()
@@ -445,7 +464,7 @@
                 peer = (across if which else s, vocab_at(v, dx, 0))
                 go(heads_ref.at[which, target], heads.at[x, my_y], head_recv.at[x, my_y], peer)
                 go(stats_ref.at[which, target], stats.at[x, my_y], stat_recv.at[x, my_y], peer)
-    for i in (0, 1, 6, 7):
+    for i in (0, 1, 6, 7, 9, 10, 11):
         loads[i].wait()
     for dx in range(4):
         source = (x + dx) % 4
@@ -471,7 +490,7 @@
         total = jnp.zeros((128, 512), F32)
         for k in range(4):
             total += lax.dot_general(
-                joined[k], w[k * 256 : (k + 1) * 256, j * 512 : (j + 1) * 512],
+                joined[k], w[k, :, j * 512 : (j + 1) * 512],
                 (((0,), (0,)), ((), ())), preferred_element_type=F32,
             )
         att[:, j * 512 : (j + 1) * 512] = jnp.where(y == 0, total[0:64], total[64:128])
@@ -577,8 +596,10 @@
         go(wide_send, wide_got.at[v], wide_recv.at[v], (s, other))
 
     for p in range(2):
-        arrive(-1, 1, p, (right,) if p == 0 else ())
-        arrive(1, 1, p, (left,) if p == 1 else ())
+        arrive(2, 0, p, (near,))
+    for p in range(2):
+        arrive(-1, 1, p, ())
+        arrive(1, 1, p, ())
     rows_of(-1, False)
     for other in others:
         take(wide_got.at[other], wide_recv.at[other])
@@ -611,7 +632,6 @@
     for other in others:
         go(last_send, last_got.at[v], last_recv.at[v], (s, other))
     for p in range(2):
-        arrive(2, 0, p, ())
         arrive(2, 1, p, ())
     rows_of(2, False)
 
@@ -712,6 +732,12 @@
         copy.wait_send()
 
 
+def hand_over_kernel(hidden_ref, rms_ref, top_ref, hidden_out, rms_out, top_out):
+    hidden_out[...] = hidden_ref[...]
+    rms_out[...] = rms_ref[...]
+    top_out[...] = top_ref[...]
+
+
 def per_device(
     tokens,
     attention_gain,
@@ -734,8 +760,9 @@
     me = lax.axis_index("seq").astype(jnp.int32)
     request = jnp.arange(8, dtype=jnp.int32)
     starts = jnp.sum((segment_ids[None, :] < request[:, None]).astype(jnp.int32), axis=1)
-    begins = jnp.where(starts[None, :REQS] <= token_order[:, None], starts[None, :REQS], 0)
-    position = token_order - jnp.max(begins, axis=1)
+    position = token_order - starts[0]
+    for r in range(1, REQS):
+        position = jnp.where(starts[r] <= token_order, token_order - starts[r], position)
     lane = jnp.arange(128, dtype=jnp.int32)
     inverse = rope_base ** (-(lane % 64).astype(F32) * 2.0 / 128)
     angle = position.astype(F32)[:, None] * inverse[None, :]
@@ -754,17 +781,19 @@
         cache_slots[None], jnp.pad(live_blocks.astype(F32), ((0, 0), (0, 224))),
     )
 
-    kv_all, q_other, w_all = pl.pallas_call(
+    kv_all, q_other, w_all, tail = pl.pallas_call(
         gather_kernel,
         out_shape=(
             shape((16, 528, 256), BF16), shape((528, 256), BF16), shape((4, 4, 64, 2048), BF16),
+            shape((40, 128), jnp.int32),
         ),
         in_specs=[VM, VM, HB],
-        out_specs=(HB, HB, HB),
+        out_specs=(HB, HB, HB, VM),
         scratch_shapes=[
+            pltpu.VMEM((17, 16, 256), BF16),
             pltpu.SemaphoreType.DMA((2,)),
-            pltpu.SemaphoreType.DMA((96,)),
-            pltpu.SemaphoreType.DMA((16, 2)),
+            pltpu.SemaphoreType.DMA((128,)),
+            pltpu.SemaphoreType.DMA((16, 4)),
             pltpu.SemaphoreType.DMA((1,)),
             pltpu.SemaphoreType.DMA((4, 4)),
         ],
@@ -772,12 +801,10 @@
         name="gather",
     )(kv, query, out_weight.reshape(4, 64, 2048))
 
-    runs = jnp.stack([kv_all[:, 512, 0], kv_all[:, 512, 128]], axis=1).astype(jnp.int32).reshape(32)
-    tail = jnp.concatenate([q_other[512, 0:256:128], q_other[513, 0:32]]).astype(jnp.int32)
     heads, stats = pl.pallas_call(
         attend_kernel,
         out_shape=(shape((2, 4, 256, 128), BF16), shape((2, 4, 8, 128), F32)),
-        in_specs=[SM] * 6 + [VM, VM, HB],
+        in_specs=[SM] * 5 + [VM, VM, HB],
         out_specs=(VM, VM),
         scratch_shapes=[
             pltpu.VMEM((SLOTS, 256, 256), BF16),
@@ -799,7 +826,7 @@
         ],
         compiler_params=params(),
         name="attend",
-    )(runs, tail, token_order, starts, live_blocks[0], me[None], query, q_other, kv_all)
+    )(tail, token_order, starts, live_blocks[0], me[None], query, q_other, kv_all)
 
     ends = jnp.concatenate([starts[1:REQS], jnp.full((1,), segment_ids.shape[0], jnp.int32)])
     last_index = jnp.concatenate([ends - 1, ends - 1])
@@ -808,7 +835,7 @@
     hidden, rms, top = pl.pallas_call(
         middle_kernel,
         out_shape=(shape((512, 256), BF16), shape((1, REQS), F32), shape((1, REQS), F32)),
-        in_specs=[VM, VM, HB, HB, VM, HB, HB, HB, VM, VM, HB],
+        in_specs=[VM, VM, HB, HB, HB, VM, HB, HB, HB, VM, VM, HB],
         out_specs=(VM, VM, VM),
         scratch_shapes=[
             pltpu.VMEM((4, 2, 256, 128), BF16),
@@ -816,7 +843,7 @@
             pltpu.VMEM((4, 256, 128), BF16),
             pltpu.VMEM((4, 64, 512), BF16),
             pltpu.VMEM((4, 64, 512), BF16),
-            pltpu.VMEM((1024, 2048), BF16),
+            pltpu.VMEM((4, 256, 2048), BF16),
             pltpu.VMEM((64, 2048), BF16),
             pltpu.VMEM((512, 256), BF16),
             pltpu.VMEM((2048, 512), BF16),
@@ -841,15 +868,23 @@
             pltpu.VMEM((2, 8, 128), F32),
             pltpu.VMEM((32, 8, 128), F32),
             pltpu.VMEM((8, 8, 128), F32),
-            dma((10,)), dma((192,)), dma((4, 2)), dma((4, 2)), dma((4,)), dma((8, 2)), dma((8,)), dma((4, 2)), dma((4, 2, 2)), dma((4,)),
+            dma((13,)), dma((192,)), dma((4, 2)), dma((4, 2)), dma((4,)), dma((8, 2)), dma((8,)), dma((4, 2)), dma((4, 2, 2)), dma((4,)),
             dma((32,)), dma((8,)), dma((8,)), dma((32,)), dma((8,)),
         ],
         compiler_params=params(1),
         name="middle",
     )(
-        heads, stats, w_all.reshape(1024, 2048), tokens, forward_gain[None], gate_weight, up_weight,
+        heads, stats, w_all.reshape(4, 256, 2048), out_weight, tokens, forward_gain[None], gate_weight, up_weight,
         down_weight, match, final_gain[None], head_weight,
     )
+    hidden, rms, top = pl.pallas_call(
+        hand_over_kernel,
+        out_shape=(shape((512, 256), BF16), shape((1, REQS), F32), shape((1, REQS), F32)),
+        in_specs=[VM, VM, VM],
+        out_specs=(VM, VM, VM),
+        compiler_params=params(),
+        name="hand_over",
+    )(hidden, rms, top)
     return (hidden, cache.reshape(512, 2, 128), rms.reshape(REQS), top.reshape(REQS))
 
 

time: 168 us -> 150 us (0.89)
  Pallas kernels: 149 us -> 137 us
  local copies, waits for them, and re-layouts: 11.2 us -> 4.56 us
    pallas_call x1, Pallas kernels: 88.7 us -> 73 us  [per_device(): pl.pallas_call(middle_kernel, out_shape=(shape((512, 256), BF16), shape((...]
    pallas_call x1, Pallas kernels: 12 us -> 17.9 us  [per_device(): pl.pallas_call(attend_kernel, out_shape=(shape((2, 4, 256, 128), BF16), s...]
    pallas_call x1, Pallas kernels: 41.7 us -> 37.4 us  [per_device(): pl.pallas_call(gather_kernel, out_shape=(shape((16, 528, 256), BF16), sha...]
    unnamed x15 -> x12, local copies, waits for them, and re-layouts: 4.04 us -> 0.03 us
    convert_element_type x1, other arithmetic: 0.69 us -> 3.27 us  [per_device(): angle = position.astype(F32)[:, None] * inverse[None, :]]
    pallas_call x0 -> x1, Pallas kernels: none -> 1.68 us  [per_device(): pl.pallas_call(hand_over_kernel, out_shape=(shape((512, 256), BF16), shap...]
where the time goes in v5:
time: 150 us
  Pallas kernels  137 us (91%)
  other arithmetic  7.69 us (5%)
  local copies, waits for them, and re-layouts  4.56 us (3%)
    pallas_call x1, Pallas kernels, per_device(): pl.pallas_call(middle_kernel, out_shape=(shape((512, 256), BF16), shape((...  73 us
    pallas_call x1, Pallas kernels, per_device(): pl.pallas_call(gather_kernel, out_shape=(shape((16, 528, 256), BF16), sha...  37.4 us
    pallas_call x1, Pallas kernels, per_device(): pl.pallas_call(attend_kernel, out_shape=(shape((2, 4, 256, 128), BF16), s...  17.9 us
    pallas_call x1, Pallas kernels, per_device(): pl.pallas_call(project_kernel, out_shape=(shape((528, 256), BF16), shape(...  6.78 us
    convert_element_type x1, other arithmetic, per_device(): angle = position.astype(F32)[:, None] * inverse[None, :]  3.27 us

profile of v5, /device:TPU:1, one launch (start us, length us, event | category | flops | bytes accessed | tf_op | source)
XLA Modules:
  0.0 149.8 jit_solution(12308726651118213709)
XLA Ops:
  0.6 1.1 convert_reduce_fusion.starts_ref
  1.7 0.0 copy-start.2
  1.7 0.6 fusion.5
  2.3 3.3 %select_convert_fusion = f32[512]{0:T(512)S(1)} fusion(s32[512]{0:T(512)} %base_ref.3, s32[]{:T(128)} %bitcast.3, s32[]{:T(128)} %bitcast.2, s32[]{:T(128)} %bitcast.1, s32[]{:T(128)} %bitcast), kind=kLoop, calls=%fused_computation.6 | loop fusion | flops 5632 | bytes 4112 | tf_op jit(solution)/shard_map/convert_element_type | solution.py:768
  5.6 1.8 %fusion = (f32[512,128]{1,0:T(8,128)}, f32[512,128]{1,0:T(8,128)}) fusion(f32[128]{0:T(128)S(1)} %get-tuple-element.40, f32[128]{0:T(128)S(1)} %get-tuple-element.41, f32[512]{0:T(512)S(1)} %select_convert_fusion), kind=kLoop, calls=%fused_computation.4 | loop fusion | flops 131072 | bytes 527360 | tf_op jit(solution)/shard_map/mul | solution.py:770
  7.4 1.3 broadcast_in_dim.29.gain_ref
  8.7 0.7 convert_element_type.24
  9.4 0.5 pad.4.live_ref
  9.9 6.8 %project.1 = (bf16[528,256]{1,0:T(8,128)(2,1)}, bf16[528,256]{1,0:T(8,128)(2,1)}, bf16[512,256]{1,0:T(8,128)(2,1)}) custom-call(s32[512]{0:T(512)} %base_ref.3, bf16[512,2048]{1,0:T(8,128)(2,1)} %tok_ref.3, bf16[1,2048]{1,0:T(2,128)(2,1)} %broadcast_in_dim.29.gain_ref, bf16[2048,256]{1,0:T(8,128)(2,1)} %wq_ref.1, bf16[2048,128]{1,0:T(8,128)(2,1)} %wk_ref.1, ...), custom_call_target="tpu_custom_call" | custom-call | tf_op jit(solution)/shard_map/project/pallas_call | solution.py:772
  16.7 0.0 copy-done.2
  16.7 37.4 %gather.1 = (bf16[16,528,256]{2,1,0:T(8,128)(2,1)}, bf16[528,256]{1,0:T(8,128)(2,1)}, bf16[4,4,64,2048]{3,2,1,0:T(8,128)(2,1)}, s32[40,128]{1,0:T(8,128)}) custom-call(bf16[528,256]{1,0:T(8,128)(2,1)} %get-tuple-element.19.kv_ref, bf16[528,256]{1,0:T(8,128)(2,1)} %get-tuple-element.20.q_ref, bf16[4,64,2048]{2,1,0:T(8,128)(2,1)} %bitcast.12), custom_call_target="tpu_custom_call" | custom-call | tf_op jit(solution)/shard_map/gather/pallas_call | solution.py:784
  54.1 0.0 copy-start.3
  54.2 0.0 copy-start.1
  54.2 0.0 copy-start.4
  54.2 0.0 copy-start.5
  54.2 17.9 %attend.1 = (bf16[2,4,256,128]{3,2,1,0:T(8,128)(2,1)}, f32[2,4,8,128]{3,2,1,0:T(8,128)}) custom-call(s32[40,128]{1,0:T(8,128)} %get-tuple-element.21.tail_ref, s32[512]{0:T(512)} %base_ref.3, s32[8]{0:T(128)} %copy-done.2, s32[32]{0:T(128)} %bitcast.14, s32[1]{0:T(128)} %bitcast.7.me_ref, bf16[528,256]{1,0:T(8,128)(2,1)} %get-tuple-element.20.q_ref, ...), custom_call_target="tpu_custom_call" | custom-call | tf_op jit(solution)/shard_map/attend/pallas_call | solution.py:804
  72.1 0.0 copy-done.3
  72.1 0.1 slice.22
  72.2 0.1 add_add_fusion
  72.3 0.1 pad_add_fusion
  72.4 0.0 copy-done.1
  72.4 0.1 eq.17
  72.5 0.7 compare_convert_fusion.match_ref
  73.1 0.0 copy-done.4
  73.1 0.6 broadcast_in_dim.34.gain_ref
  73.7 0.0 copy-done.5
  73.7 0.6 broadcast_in_dim.35.final_ref
  74.3 0.0 copy-start
  74.3 73.0 %middle.1 = (bf16[512,256]{1,0:T(8,128)(2,1)}, f32[1,4]{1,0:T(1,128)}, f32[1,4]{1,0:T(1,128)}) custom-call(bf16[2,4,256,128]{3,2,1,0:T(8,128)(2,1)} %get-tuple-element.24.heads_ref, f32[2,4,8,128]{3,2,1,0:T(8,128)} %get-tuple-element.25.stats_ref, bf16[4,256,2048]{2,1,0:T(8,128)(2,1)} %bitcast.11, bf16[256,2048]{1,0:T(8,128)(2,1)} %w_own.1, ...), custom_call_target="tpu_custom_call" | custom-call | tf_op jit(solution)/shard_map/middle/pallas_call | solution.py:835
  147.3 1.7 %hand_over.1 = (bf16[512,256]{1,0:T(8,128)(2,1)}, f32[1,4]{1,0:T(1,128)}, f32[1,4]{1,0:T(1,128)}) custom-call(bf16[512,256]{1,0:T(8,128)(2,1)} %get-tuple-element.27.hidden_ref, f32[1,4]{1,0:T(1,128)} %get-tuple-element.28.rms_ref, f32[1,4]{1,0:T(1,128)} %get-tuple-element.29.top_ref), custom_call_target="tpu_custom_call" | custom-call | tf_op jit(solution)/shard_map/hand_over/pallas_call | solution.py:880
  149.0 0.0 copy-done
  149.0 0.8 reshape.48
  (1 shorter events, 0.0 us)
Async XLA Ops:
  1.7 15.0 %copy-start.2 = (s32[8]{0:T(128)}, s32[8]{0:T(128)S(1)}, u32[]{:S(2)}) copy-start(s32[8]{0:T(128)S(1)} %convert_reduce_fusion.starts_ref) | copy-start | bytes 100
  54.1 18.0 %copy-start.3 = (s32[8]{0:T(128)S(1)}, s32[8]{0:T(128)}, u32[]{:S(2)}) copy-start(s32[8]{0:T(128)} %copy-done.2) | copy-start | bytes 100
  54.2 18.2 %copy-start.1 = (s32[512]{0:T(512)S(1)}, s32[512]{0:T(512)}, u32[]{:S(2)}) copy-start(s32[512]{0:T(512)} %base_ref.3) | copy-start | bytes 6148
  54.2 19.0 %copy-start.4 = (bf16[2048]{0:T(1024)(128)(2,1)S(1)}, bf16[2048]{0:T(1024)(128)(2,1)}, u32[]{:S(2)}) copy-start(bf16[2048]{0:T(1024)(128)(2,1)} %param.22) | copy-start | bytes 12292
  54.2 19.6 %copy-start.5 = (bf16[2048]{0:T(1024)(128)(2,1)S(1)}, bf16[2048]{0:T(1024)(128)(2,1)}, u32[]{:S(2)}) copy-start(bf16[2048]{0:T(1024)(128)(2,1)} %param.26) | copy-start | bytes 12292
  74.3 74.7 %copy-start = (bf16[512,256]{1,0:T(8,128)(2,1)S(1)}, bf16[512,256]{1,0:T(8,128)(2,1)}, u32[]{:S(2)}) copy-start(bf16[512,256]{1,0:T(8,128)(2,1)} %get-tuple-element.31) | copy-start | bytes 786436

commit v6 on v5

--- a/solution.py
+++ b/solution.py
@@ -2,6 +2,7 @@
 
 import jax
 import jax.numpy as jnp
+import numpy as np
 from jax import lax
 from jax.experimental import pallas as pl
 from jax.experimental.pallas import tpu as pltpu
@@ -40,6 +41,11 @@
     return ((x + dx + 4) % 4) * 2 + (y + dy) % 2
 
 
+def wide_row(ref):
+    rows = ref[...].astype(F32)
+    return jnp.concatenate([rows[i : i + 1] for i in range(16)], axis=1)
+
+
 def greet(peers):
     barrier = pltpu.get_barrier_semaphore()
     for peer in peers:
@@ -47,56 +53,19 @@
     pl.semaphore_wait(barrier, len(peers))
 
 
-def project_kernel(
-    base_ref, tok_ref, gain_ref, wq_ref, wk_ref, wv_ref, cos_ref, sin_ref, slot_ref, live_ref,
-    q_ref, kv_ref, cache_ref,
-):
-    gain = gain_ref[...].astype(F32)
-
-    def rows_step(i, carry):
-        rows = pl.ds(pl.multiple_of(i * 128, 128), 128)
-        x = tok_ref[rows, :].astype(F32)
-        scale = lax.rsqrt(jnp.mean(x * x, axis=-1, keepdims=True) + epsilon)
-        normed = (x * scale * gain).astype(BF16)
-        cos = cos_ref[rows, :]
-        sin = sin_ref[rows, :]
-
-        def turn(u):
-            return u * cos + pltpu.roll(u, 64, axis=1) * sin
-
-        q = jnp.dot(normed, wq_ref[...], preferred_element_type=F32)
-        q_ref[rows, 0:128] = (turn(q[:, 0:128]) * SCALE).astype(BF16)
-        q_ref[rows, 128:256] = (turn(q[:, 128:256]) * SCALE).astype(BF16)
-        k = jnp.dot(normed, wk_ref[...], preferred_element_type=F32)
-        kv_ref[rows, 0:128] = turn(k).astype(BF16)
-        v = jnp.dot(normed, wv_ref[...], preferred_element_type=F32)
-        kv_ref[rows, 128:256] = v.astype(BF16)
-        return carry
-
-    lax.fori_loop(0, 4, rows_step, 0)
-    lane = lax.broadcasted_iota(jnp.int32, (16, 256), 1)
-    run = jnp.where(lane < 128, base_ref[0] // 256, base_ref[256] // 256)
-    run = run.astype(F32)
-    kv_ref[512:528, :] = run.astype(BF16)
-    row = lax.broadcasted_iota(jnp.int32, (16, 256), 0)
-    q_ref[512:528, :] = jnp.where(row == 1, live_ref[...], run).astype(BF16)
-    slots = slot_ref[...]
-
-    def cache_step(i, carry):
-        row = i * 128 + lax.broadcasted_iota(jnp.int32, (128, 512), 0)
-        pick = jnp.where(row == slots, 1.0, 0.0).astype(BF16)
-        moved = jnp.dot(pick, kv_ref[0:512, :], preferred_element_type=F32)
-        cache_ref[pl.ds(pl.multiple_of(i * 128, 128), 128), :] = moved.astype(BF16)
-        return carry
-
-    lax.fori_loop(0, 4, cache_step, 0)
+FREQUENCY = rope_base ** (-(np.arange(128) % 64) * 2.0 / 128)
+STEP_COS = np.cos(np.arange(256)[:, None] * FREQUENCY[None, :]).astype(np.float32)
+STEP_SIN = np.sin(np.arange(256)[:, None] * FREQUENCY[None, :]).astype(np.float32)
 
 
 PIECE_ROWS = ((0, 128), (128, 128), (256, 128), (384, 144))
 
 
 def gather_kernel(
-    kv_ref, q_ref, w_ref, kv_all, q_all, w_all, tail_ref, tails, own_sem, send_sem, kv_sem, q_sem, w_sem
+    base_ref, starts_ref, live_ref, tok_ref, gain_ref, wq_ref, wk_ref, wv_ref,
+    step_cos, step_sin, run_cos, run_sin, slot_ref, w_ref,
+    q_ref, cache_ref, match_ref, kv_all, q_all, w_all, tail_ref,
+    kv_ref, normed, cosines, sines, tails, own_sem, send_sem, kv_sem, q_sem, w_sem,
 ):
     s = lax.axis_index("seq")
     v = lax.axis_index("vocab")
@@ -107,7 +76,44 @@
     core = (seq_at(s, 0, 0, 1), v)
     right = (s, vocab_at(v, 1, 0))
     left = (s, vocab_at(v, -1, 0))
-    greet([up, down, side, core, right, left])
+    barrier = pltpu.get_barrier_semaphore()
+    for peer in (up, down, side, core, right, left):
+        pl.semaphore_signal(barrier, inc=1, device_id=peer, device_id_type=MESH)
+    gain = wide_row(gain_ref)
+    lane = lax.broadcasted_iota(jnp.int32, (128, 128), 1)
+
+    def turn(u, i):
+        rows = pl.ds(i * 128, 128)
+        return u * cosines[rows, :] + pltpu.roll(u, 64, axis=1) * sines[rows, :]
+
+    def keys_values(i):
+        rows = pl.ds(i * 128, 128)
+        values = tok_ref[rows, :].astype(F32)
+        scale = lax.rsqrt(jnp.mean(values * values, axis=-1, keepdims=True) + epsilon)
+        values = (values * scale * gain).astype(BF16)
+        normed[rows, :] = values
+        r = i // 2
+        steps = pl.ds((i % 2) * 128, 128)
+        order = base_ref[r * 256] + (i % 2) * 128 + lax.broadcasted_iota(jnp.int32, (128, 128), 0)
+        near_cos = jnp.broadcast_to(run_cos[4 * r : 4 * r + 1, :], (128, 128))
+        near_sin = jnp.broadcast_to(run_sin[4 * r : 4 * r + 1, :], (128, 128))
+        for req in range(1, REQS):
+            later = order >= starts_ref[req]
+            near_cos = jnp.where(later, run_cos[4 * r + req : 4 * r + req + 1, :], near_cos)
+            near_sin = jnp.where(later, run_sin[4 * r + req : 4 * r + req + 1, :], near_sin)
+        cosines[rows, :] = step_cos[steps, :] * near_cos - step_sin[steps, :] * near_sin
+        sine = step_sin[steps, :] * near_cos + step_cos[steps, :] * near_sin
+        sines[rows, :] = jnp.where(lane < 64, -sine, sine)
+        key = jnp.dot(values, wk_ref[...], preferred_element_type=F32)
+        kv_ref[rows, 0:128] = turn(key, i).astype(BF16)
+        value = jnp.dot(values, wv_ref[...], preferred_element_type=F32)
+        kv_ref[rows, 128:256] = value.astype(BF16)
+
+    half = lax.broadcasted_iota(jnp.int32, (16, 256), 1)
+    run = jnp.where(half < 128, base_ref[0] // 256, base_ref[256] // 256).astype(F32)
+    kv_ref[512:528, :] = run.astype(BF16)
+    keys_values(0)
+    pl.semaphore_wait(barrier, 6)
     started = []
 
     def go(src, dst, recv, peer):
@@ -142,16 +148,27 @@
 
     mine = z * 2 + c
     for p in range(4):
+        if p:
+            keys_values(p)
         low, count = PIECE_ROWS[p]
         for peer in (up, down, core):
             go(kv_ref.at[pl.ds(low, count), :], kv_view(mine, p), kv_sem.at[mine, p], peer)
-    for p in range(2):
-        piece = 2 * c + p
-        for peer in (right, left):
-            go(w_ref.at[piece], w_all.at[x, piece], w_sem.at[x, piece], peer)
-    go(q_ref, q_all, q_sem.at[0], side)
+        if p < 2:
+            piece = 2 * c + p
+            for peer in (right, left):
+                go(w_ref.at[piece], w_all.at[x, piece], w_sem.at[x, piece], peer)
     own = pltpu.make_async_copy(kv_ref, kv_all.at[mine], own_sem.at[0])
     own.start()
+    for p in range(4):
+        rows = pl.ds(p * 128, 128)
+        query = jnp.dot(normed[rows, :], wq_ref[...], preferred_element_type=F32)
+        q_ref[rows, 0:128] = (turn(query[:, 0:128], p) * SCALE).astype(BF16)
+        q_ref[rows, 128:256] = (turn(query[:, 128:256], p) * SCALE).astype(BF16)
+    row = lax.broadcasted_iota(jnp.int32, (16, 256), 0)
+    for i in range(32):
+        run = jnp.where((row == 1) & (half == i), live_ref[i].astype(F32), run)
+    q_ref[512:528, :] = run.astype(BF16)
+    go(q_ref, q_all, q_sem.at[0], side)
 
     for d in (1, 2):
         for p in range(4):
@@ -162,6 +179,19 @@
             w_take(1, 0, (core,))
     w_take(-1, 1, (core,))
     w_take(1, 1, (left, core))
+    slots = slot_ref[...]
+    for i in range(4):
+        row = i * 128 + lax.broadcasted_iota(jnp.int32, (128, 512), 0)
+        pick = jnp.where(row == slots, 1.0, 0.0).astype(BF16)
+        moved = jnp.dot(pick, kv_ref[0:512, :], preferred_element_type=F32)
+        cache_ref[i * 128 : (i + 1) * 128, :] = moved.astype(BF16)
+    request = lax.broadcasted_iota(jnp.int32, (8, 64), 0) % REQS
+    last = jnp.full((8, 64), starts_ref[1] - 1, jnp.int32)
+    for req in range(1, REQS):
+        last = jnp.where(request == req, starts_ref[req + 1] - 1, last)
+    for i in range(8):
+        order = base_ref[256 * (i // 4)] + (i % 4) * 64 + lax.broadcasted_iota(jnp.int32, (8, 64), 1)
+        match_ref[i] = jnp.where(order == last, 1.0, 0.0).astype(BF16)
     for p in range(4):
         kv_take(-3, p, (up, core) if p < 2 else (core,))
         kv_take(3, p, (down, core) if p >= 2 else (core,))
@@ -509,7 +539,7 @@
         return square + jnp.sum(residual * residual, axis=-1, keepdims=True)
 
     square = lax.fori_loop(0, 4, project, jnp.zeros((64, 1), F32))
-    gain = gain_ref[...].astype(F32)
+    gain = wide_row(gain_ref)
     mine = (att[...] * lax.rsqrt(square / 2048 + epsilon) * gain).astype(BF16)
     normed[2 * v] = mine[0:32]
     normed[2 * v + 1] = mine[32:64]
@@ -676,10 +706,9 @@
 
     rms_ref[...] = along_lanes(jnp.sqrt(mean_square))[:, :REQS]
     inverse = lax.rsqrt(mean_square)[:, 0:1]
+    last_gain = wide_row(final_ref)
     spread = packed(
-        lambda q: jnp.broadcast_to(
-            final_ref[:, q * 512 : (q + 1) * 512].astype(F32), (16, 512)
-        )
+        lambda q: jnp.broadcast_to(last_gain[:, q * 512 : (q + 1) * 512], (16, 512))
     )
     final = final * inverse * spread
     loads[8].wait()
@@ -760,36 +789,23 @@
     me = lax.axis_index("seq").astype(jnp.int32)
     request = jnp.arange(8, dtype=jnp.int32)
     starts = jnp.sum((segment_ids[None, :] < request[:, None]).astype(jnp.int32), axis=1)
-    position = token_order - starts[0]
-    for r in range(1, REQS):
-        position = jnp.where(starts[r] <= token_order, token_order - starts[r], position)
-    lane = jnp.arange(128, dtype=jnp.int32)
-    inverse = rope_base ** (-(lane % 64).astype(F32) * 2.0 / 128)
-    angle = position.astype(F32)[:, None] * inverse[None, :]
-    cos = jnp.cos(angle)
-    sin = jnp.where(lane < 64, -1.0, 1.0)[None, :] * jnp.sin(angle)
-
-    query, kv, cache = pl.pallas_call(
-        project_kernel,
-        out_shape=(shape((528, 256), BF16), shape((528, 256), BF16), shape((512, 256), BF16)),
-        in_specs=[SM] + [VM] * 9,
-        out_specs=(VM, VM, VM),
-        compiler_params=params(),
-        name="project",
-    )(
-        token_order, tokens, attention_gain[None], query_weight, key_weight, value_weight, cos, sin,
-        cache_slots[None], jnp.pad(live_blocks.astype(F32), ((0, 0), (0, 224))),
-    )
-
-    kv_all, q_other, w_all, tail = pl.pallas_call(
+    delta = (token_order[::256][:, None] - starts[None, :REQS]).reshape(8, 1).astype(F32)
+    angle = delta * jnp.asarray(FREQUENCY.astype(np.float32))[None, :]
+
+    query, cache, match, kv_all, q_other, w_all, tail = pl.pallas_call(
         gather_kernel,
         out_shape=(
+            shape((528, 256), BF16), shape((512, 256), BF16), shape((8, 8, 64), BF16),
             shape((16, 528, 256), BF16), shape((528, 256), BF16), shape((4, 4, 64, 2048), BF16),
             shape((40, 128), jnp.int32),
         ),
-        in_specs=[VM, VM, HB],
-        out_specs=(HB, HB, HB, VM),
+        in_specs=[SM] * 3 + [VM] * 10 + [HB],
+        out_specs=(VM, VM, VM, HB, HB, HB, VM),
         scratch_shapes=[
+            pltpu.VMEM((528, 256), BF16),
+            pltpu.VMEM((512, 2048), BF16),
+            pltpu.VMEM((512, 128), F32),
+            pltpu.VMEM((512, 128), F32),
             pltpu.VMEM((17, 16, 256), BF16),
             pltpu.SemaphoreType.DMA((2,)),
             pltpu.SemaphoreType.DMA((128,)),
@@ -799,7 +815,11 @@
         ],
         compiler_params=params(0),
         name="gather",
-    )(kv, query, out_weight.reshape(4, 64, 2048))
+    )(
+        token_order, starts, live_blocks[0], tokens, attention_gain.reshape(16, 128), query_weight,
+        key_weight, value_weight, jnp.asarray(STEP_COS), jnp.asarray(STEP_SIN), jnp.cos(angle),
+        jnp.sin(angle), cache_slots[None], out_weight.reshape(4, 64, 2048),
+    )
 
     heads, stats = pl.pallas_call(
         attend_kernel,
@@ -828,9 +848,6 @@
         name="attend",
     )(tail, token_order, starts, live_blocks[0], me[None], query, q_other, kv_all)
 
-    ends = jnp.concatenate([starts[1:REQS], jnp.full((1,), segment_ids.shape[0], jnp.int32)])
-    last_index = jnp.concatenate([ends - 1, ends - 1])
-    match = (token_order.reshape(8, 1, 64) == last_index[None, :, None]).astype(BF16)
     dma = pltpu.SemaphoreType.DMA
     hidden, rms, top = pl.pallas_call(
         middle_kernel,
@@ -874,8 +891,8 @@
         compiler_params=params(1),
         name="middle",
     )(
-        heads, stats, w_all.reshape(4, 256, 2048), out_weight, tokens, forward_gain[None], gate_weight, up_weight,
-        down_weight, match, final_gain[None], head_weight,
+        heads, stats, w_all.reshape(4, 256, 2048), out_weight, tokens, forward_gain.reshape(16, 128), gate_weight, up_weight,
+        down_weight, match, final_gain.reshape(16, 128), head_weight,
     )
     hidden, rms, top = pl.pallas_call(
         hand_over_kernel,

time: 150 us -> 142 us (0.947)
  other arithmetic: 7.69 us -> 2.52 us
  local copies, waits for them, and re-layouts: 4.56 us -> 1.63 us
    pallas_call x1, Pallas kernels: 73 us -> 80.3 us  [per_device(): pl.pallas_call(middle_kernel, out_shape=(shape((512, 256), BF16), shape((...]
    pallas_call x2 -> x1, Pallas kernels: 44.2 us -> 39 us  [per_device(): pl.pallas_call(gather_kernel, out_shape=(shape((528, 256), BF16), shape((...]
    convert_element_type x3 -> x1, other arithmetic: 4.61 us -> 0.07 us  [per_device(): (token_order[::256][:, None] - starts[None, :REQS]).reshape(8, 1)]
    broadcast_in_dim x3 -> x0, local copies, waits for them, and re-layouts: 2.48 us -> none  [the longest x1 1.29 us: per_device(): attention_gain[None]]
    pallas_call x1, Pallas kernels: 17.9 us -> 15.5 us  [per_device(): pl.pallas_call(attend_kernel, out_shape=(shape((2, 4, 256, 128), BF16), s...]
    mul x1 -> x0, other arithmetic: 1.83 us -> none  [per_device(): sin = jnp.where(lane < 64, -1.0, 1.0)[None, :] * jnp.sin(angle)]
where the time goes in v6:
time: 142 us; the launch traced here: 141 us
  Pallas kernels  136 us (96%)
  other arithmetic  2.52 us (2%)
  local copies, waits for them, and re-layouts  1.63 us (1%)
    pallas_call x1, Pallas kernels, per_device(): pl.pallas_call(middle_kernel, out_shape=(shape((512, 256), BF16), shape((...  80.3 us
    pallas_call x1, Pallas kernels, per_device(): pl.pallas_call(gather_kernel, out_shape=(shape((528, 256), BF16), shape((...  39 us
    pallas_call x1, Pallas kernels, per_device(): pl.pallas_call(attend_kernel, out_shape=(shape((2, 4, 256, 128), BF16), s...  15.5 us

profile of v6, /device:TPU:1, one launch (start us, length us, event | category | flops | bytes accessed | tf_op | source)
XLA Modules:
  0.0 141.3 jit_solution(9183972535036794899)
XLA Ops:
  0.6 1.1 convert_reduce_fusion.starts_ref
  1.7 0.0 copy-start.1
  1.7 0.8 slice.6
  2.5 0.1 subtract_convert_fusion
  2.6 0.1 convert_element_type.16
  2.7 1.4 multiply_sine_fusion
  4.0 0.0 copy-done.1
  4.0 39.0 %gather.1 = (bf16[528,256]{1,0:T(8,128)(2,1)}, bf16[512,256]{1,0:T(8,128)(2,1)}, bf16[8,8,64]{2,1,0:T(8,128)(2,1)}, bf16[16,528,256]{2,1,0:T(8,128)(2,1)}, bf16[...) custom-call(s32[512]{0:T(512)} %base_ref.3, s32[8]{0:T(128)} %copy-done.1, s32[32]{0:T(128)} %bitcast.18, ...), custom_call_target="tpu_custom_call" | custom-call | tf_op jit(solution)/shard_map/gather/pallas_call | solution.py:795
  43.0 15.5 %attend.1 = (bf16[2,4,256,128]{3,2,1,0:T(8,128)(2,1)}, f32[2,4,8,128]{3,2,1,0:T(8,128)}) custom-call(s32[40,128]{1,0:T(8,128)} %get-tuple-element.19.tail_ref, s32[512]{0:T(512)} %base_ref.3, s32[8]{0:T(128)} %copy-done.1, s32[32]{0:T(128)} %bitcast.19, s32[1]{0:T(128)} %bitcast.4.me_ref, bf16[528,256]{1,0:T(8,128)(2,1)} %get-tuple-element.20.q_ref, ...), custom_call_target="tpu_custom_call" | custom-call | tf_op jit(solution)/shard_map/attend/pallas_call | solution.py:824
  58.5 0.0 copy-start
  58.6 80.3 %middle.1 = (bf16[512,256]{1,0:T(8,128)(2,1)}, f32[1,4]{1,0:T(1,128)}, f32[1,4]{1,0:T(1,128)}) custom-call(bf16[2,4,256,128]{3,2,1,0:T(8,128)(2,1)} %get-tuple-element.23.heads_ref, f32[2,4,8,128]{3,2,1,0:T(8,128)} %get-tuple-element.24.stats_ref, bf16[4,256,2048]{2,1,0:T(8,128)(2,1)} %bitcast.12, bf16[256,2048]{1,0:T(8,128)(2,1)} %w_own.1, ...), custom_call_target="tpu_custom_call" | custom-call | tf_op jit(solution)/shard_map/middle/pallas_call | solution.py:852
  138.8 1.7 %hand_over.1 = (bf16[512,256]{1,0:T(8,128)(2,1)}, f32[1,4]{1,0:T(1,128)}, f32[1,4]{1,0:T(1,128)}) custom-call(bf16[512,256]{1,0:T(8,128)(2,1)} %get-tuple-element.27.hidden_ref, f32[1,4]{1,0:T(1,128)} %get-tuple-element.28.rms_ref, f32[1,4]{1,0:T(1,128)} %get-tuple-element.29.top_ref), custom_call_target="tpu_custom_call" | custom-call | tf_op jit(solution)/shard_map/hand_over/pallas_call | solution.py:897
  140.5 0.0 copy-done
  140.5 0.8 reshape.58
Async XLA Ops:
  1.7 2.3 %copy-start.1 = (s32[8]{0:T(128)}, s32[8]{0:T(128)S(1)}, u32[]{:S(2)}) copy-start(s32[8]{0:T(128)S(1)} %convert_reduce_fusion.starts_ref) | copy-start | bytes 100
  58.5 82.0 %copy-start = (bf16[512,256]{1,0:T(8,128)(2,1)S(1)}, bf16[512,256]{1,0:T(8,128)(2,1)}, u32[]{:S(2)}) copy-start(bf16[512,256]{1,0:T(8,128)(2,1)} %get-tuple-element.31) | copy-start | bytes 786436

commit v7 on v6

--- a/solution.py
+++ b/solution.py
@@ -56,6 +56,8 @@
 FREQUENCY = rope_base ** (-(np.arange(128) % 64) * 2.0 / 128)
 STEP_COS = np.cos(np.arange(256)[:, None] * FREQUENCY[None, :]).astype(np.float32)
 STEP_SIN = np.sin(np.arange(256)[:, None] * FREQUENCY[None, :]).astype(np.float32)
+FAR_COS = np.cos(256 * np.arange(64)[:, None] * FREQUENCY[None, :]).astype(np.float32)
+FAR_SIN = np.sin(256 * np.arange(64)[:, None] * FREQUENCY[None, :]).astype(np.float32)
 
 
 PIECE_ROWS = ((0, 128), (128, 128), (256, 128), (384, 144))
@@ -63,7 +65,7 @@
 
 def gather_kernel(
     base_ref, starts_ref, live_ref, tok_ref, gain_ref, wq_ref, wk_ref, wv_ref,
-    step_cos, step_sin, run_cos, run_sin, slot_ref, w_ref,
+    step_cos, step_sin, far_cos, far_sin, slot_ref, w_ref,
     q_ref, cache_ref, match_ref, kv_all, q_all, w_all, tail_ref,
     kv_ref, normed, cosines, sines, tails, own_sem, send_sem, kv_sem, q_sem, w_sem,
 ):
@@ -95,12 +97,16 @@
         r = i // 2
         steps = pl.ds((i % 2) * 128, 128)
         order = base_ref[r * 256] + (i % 2) * 128 + lax.broadcasted_iota(jnp.int32, (128, 128), 0)
-        near_cos = jnp.broadcast_to(run_cos[4 * r : 4 * r + 1, :], (128, 128))
-        near_sin = jnp.broadcast_to(run_sin[4 * r : 4 * r + 1, :], (128, 128))
-        for req in range(1, REQS):
-            later = order >= starts_ref[req]
-            near_cos = jnp.where(later, run_cos[4 * r + req : 4 * r + req + 1, :], near_cos)
-            near_sin = jnp.where(later, run_sin[4 * r + req : 4 * r + req + 1, :], near_sin)
+        for req in range(REQS):
+            start = starts_ref[req]
+            runs = jnp.maximum(base_ref[r * 256] // 256 - start // 256, 0)
+            far_c, far_s = far_cos[pl.ds(runs, 1), :], far_sin[pl.ds(runs, 1), :]
+            off_c, off_s = step_cos[pl.ds(start % 256, 1), :], step_sin[pl.ds(start % 256, 1), :]
+            run_c = jnp.broadcast_to(far_c * off_c + far_s * off_s, (128, 128))
+            run_s = jnp.broadcast_to(far_s * off_c - far_c * off_s, (128, 128))
+            later = order >= start
+            near_cos = jnp.where(later, run_c, near_cos) if req else run_c
+            near_sin = jnp.where(later, run_s, near_sin) if req else run_s
         cosines[rows, :] = step_cos[steps, :] * near_cos - step_sin[steps, :] * near_sin
         sine = step_sin[steps, :] * near_cos + step_cos[steps, :] * near_sin
         sines[rows, :] = jnp.where(lane < 64, -sine, sine)
@@ -678,7 +684,7 @@
         add_to(ref, fwd_in.at[chunk, way])
         go(ref, x_in.at[chunk, way, way], x_recv.at[chunk, way, way], (s, right if way == 0 else left))
 
-    for to_right, to_left in ((-1, 1), (2, 0), (0, 2), (1, -1)):
+    for to_right, to_left in ((-1, 1), (2, 0)):
         onward(to_right, 0)
         onward(to_left, 1)
 
@@ -725,6 +731,10 @@
     seq_max[s] = best
     for other in seqs:
         go(max_send.at[0], seq_max.at[s], max_recv.at[s], (other, v))
+    for to_right, to_left in ((0, 2), (1, -1)):
+        onward(to_right, 0)
+        onward(to_left, 1)
+
     for dx in (0, -1, 1, 2):
         chunk = (x + dx + 4) % 4
         for way in range(2):
@@ -789,9 +799,6 @@
     me = lax.axis_index("seq").astype(jnp.int32)
     request = jnp.arange(8, dtype=jnp.int32)
     starts = jnp.sum((segment_ids[None, :] < request[:, None]).astype(jnp.int32), axis=1)
-    delta = (token_order[::256][:, None] - starts[None, :REQS]).reshape(8, 1).astype(F32)
-    angle = delta * jnp.asarray(FREQUENCY.astype(np.float32))[None, :]
-
     query, cache, match, kv_all, q_other, w_all, tail = pl.pallas_call(
         gather_kernel,
         out_shape=(
@@ -817,8 +824,8 @@
         name="gather",
     )(
         token_order, starts, live_blocks[0], tokens, attention_gain.reshape(16, 128), query_weight,
-        key_weight, value_weight, jnp.asarray(STEP_COS), jnp.asarray(STEP_SIN), jnp.cos(angle),
-        jnp.sin(angle), cache_slots[None], out_weight.reshape(4, 64, 2048),
+        key_weight, value_weight, jnp.asarray(STEP_COS), jnp.asarray(STEP_SIN), jnp.asarray(FAR_COS),
+        jnp.asarray(FAR_SIN), cache_slots[None], out_weight.reshape(4, 64, 2048),
     )
 
     heads, stats = pl.pallas_call(

time: 142 us -> 136 us (0.958)
  Pallas kernels: 136 us -> 132 us
    pallas_call x1, Pallas kernels: 80.3 us -> 75 us  [per_device(): pl.pallas_call(middle_kernel, out_shape=(shape((512, 256), BF16), shape((...]
where the time goes in v7:
time: 136 us; the launch traced here: 135 us
  Pallas kernels  132 us (97%)
  other arithmetic  1.6 us (1%)
    pallas_call x1, Pallas kernels, per_device(): pl.pallas_call(middle_kernel, out_shape=(shape((512, 256), BF16), shape((...  75 us
    pallas_call x1, Pallas kernels, per_device(): pl.pallas_call(gather_kernel, out_shape=(shape((528, 256), BF16), shape((...  38.9 us
    pallas_call x1, Pallas kernels, per_device(): pl.pallas_call(attend_kernel, out_shape=(shape((2, 4, 256, 128), BF16), s...  16 us

profile of v7, /device:TPU:1, one launch (start us, length us, event | category | flops | bytes accessed | tf_op | source)
XLA Modules:
  0.0 134.6 jit_solution(6673770406199421630)
XLA Ops:
  0.6 1.6 %convert_reduce_fusion.starts_ref = s32[8]{0:T(128)} fusion(s32[16384]{0:T(1024)} %param.32), kind=kLoop, calls=%fused_computation | loop fusion | flops 393208 | bytes 65568 | tf_op jit(solution)/shard_map/reduce_sum | solution.py:801
  2.2 38.9 %gather.1 = (bf16[528,256]{1,0:T(8,128)(2,1)}, bf16[512,256]{1,0:T(8,128)(2,1)}, bf16[8,8,64]{2,1,0:T(8,128)(2,1)}, bf16[16,528,256]{2,1,0:T(8,128)(2,1)}, bf16[...) custom-call(s32[512]{0:T(512)} %base_ref.3, s32[8]{0:T(128)} %convert_reduce_fusion.starts_ref, ...), custom_call_target="tpu_custom_call" | custom-call | tf_op jit(solution)/shard_map/gather/pallas_call | solution.py:802
  41.2 16.0 %attend.1 = (bf16[2,4,256,128]{3,2,1,0:T(8,128)(2,1)}, f32[2,4,8,128]{3,2,1,0:T(8,128)}) custom-call(s32[40,128]{1,0:T(8,128)} %get-tuple-element.19.tail_ref, s32[512]{0:T(512)} %base_ref.3, s32[8]{0:T(128)} %convert_reduce_fusion.starts_ref, s32[32]{0:T(128)} %bitcast.17, s32[1]{0:T(128)} %bitcast.4.me_ref, bf16[528,256]{1,0:T(8,128)(2,1)} %get-tuple-element.20.q_ref, ...), custom_call_target="tpu_custom_call" | custom-call | tf_op jit(solution)/shard_map/attend/pallas_call | solution.py:831
  57.2 0.0 copy-start
  57.2 75.0 %middle.1 = (bf16[512,256]{1,0:T(8,128)(2,1)}, f32[1,4]{1,0:T(1,128)}, f32[1,4]{1,0:T(1,128)}) custom-call(bf16[2,4,256,128]{3,2,1,0:T(8,128)(2,1)} %get-tuple-element.23.heads_ref, f32[2,4,8,128]{3,2,1,0:T(8,128)} %get-tuple-element.24.stats_ref, bf16[4,256,2048]{2,1,0:T(8,128)(2,1)} %bitcast.11, bf16[256,2048]{1,0:T(8,128)(2,1)} %w_own.1, ...), custom_call_target="tpu_custom_call" | custom-call | tf_op jit(solution)/shard_map/middle/pallas_call | solution.py:859
  132.2 1.7 %hand_over.1 = (bf16[512,256]{1,0:T(8,128)(2,1)}, f32[1,4]{1,0:T(1,128)}, f32[1,4]{1,0:T(1,128)}) custom-call(bf16[512,256]{1,0:T(8,128)(2,1)} %get-tuple-element.27.hidden_ref, f32[1,4]{1,0:T(1,128)} %get-tuple-element.28.rms_ref, f32[1,4]{1,0:T(1,128)} %get-tuple-element.29.top_ref), custom_call_target="tpu_custom_call" | custom-call | tf_op jit(solution)/shard_map/hand_over/pallas_call | solution.py:904
  133.9 0.0 copy-done
  133.9 0.8 reshape.38
Async XLA Ops:
  57.2 76.7 %copy-start = (bf16[512,256]{1,0:T(8,128)(2,1)S(1)}, bf16[512,256]{1,0:T(8,128)(2,1)}, u32[]{:S(2)}) copy-start(bf16[512,256]{1,0:T(8,128)(2,1)} %get-tuple-element.31) | copy-start | bytes 786436

commit v8 on v7

--- a/solution.py
+++ b/solution.py
@@ -297,16 +297,16 @@
         return choose(i, [0, 1, 2, 3])
 
     def place(i):
-        return jnp.clip(i + choose(i, shifts), 0, 31)
+        return (i + choose(i, shifts)) & 31
 
     def key_run(i):
         return sorted_run[place(i)]
 
     def fetch(i):
         entry = sorted_entry[place(i)]
-        slot = i % SLOTS
+        slot = i & (SLOTS - 1)
         return pltpu.make_async_copy(
-            kv_ref.at[entry % 16, pl.ds((entry // 16) * 256, 256), :], buf.at[slot], sem.at[slot]
+            kv_ref.at[entry & 15, pl.ds(pl.multiple_of((entry >> 4) * 256, 256), 256), :], buf.at[slot], sem.at[slot]
         )
 
     for i in range(SLOTS - 2):
@@ -330,14 +330,14 @@
 
     def score(i, into):
         into[...] = lax.dot_general(
-            buf[i % SLOTS, :, 0:128], q_rows[half(i)],
+            buf[i & (SLOTS - 1), :, 0:128], q_rows[half(i)],
             (((1,), (1,)), ((), ())), preferred_element_type=F32,
         )
 
     def collect(i, parity):
         r = half(i)
         added = lax.dot_general(
-            buf[(i + SLOTS) % SLOTS, :, 128:256], all_probs[parity][...],
+            buf[(i + SLOTS) & (SLOTS - 1), :, 128:256], all_probs[parity][...],
             (((0,), (0,)), ((), ())), preferred_element_type=F32,
         )
         acc[r] = acc[r] * all_keep[parity][...] + added
@@ -347,7 +347,7 @@
         scores = all_scores[parity][...]
         if masked:
             lane = lax.broadcasted_iota(jnp.int32, (1, 512), 1)
-            q_pos = base + (lane % 256)
+            q_pos = base + (lane & 255)
             low = jnp.full((1, 512), starts_ref[0], jnp.int32)
             for req in range(1, REQS):
                 low = jnp.where(starts_ref[req] <= q_pos, starts_ref[req], low)
@@ -377,10 +377,10 @@
         run = key_run(i)
         base = choose(i, q_run) * 256
         last_low = choose(i, lasts)
-        slot = sorted_entry[place(i)] % 16
-        block = (slot // 2) * 4 + my_y * 2 + slot % 2
+        slot = sorted_entry[place(i)] & 15
+        block = (slot >> 1) * 4 + my_y * 2 + (slot & 1)
         live = jnp.where(
-            i < offsets[2], live_ref[(me - block + 32) % 32], tail_ref[34, (other - block + 32) % 32]
+            i < offsets[2], live_ref[(me - block) & 31], tail_ref[34, (other - block) & 31]
         ) > 0
         whole = (run * 256 < base) & (run * 256 >= last_low)
 

time: 136 us -> 137 us (level)
  Pallas kernels: 132 us -> 134 us
    pallas_call x1, Pallas kernels: 75 us -> 79.9 us  [per_device(): pl.pallas_call(middle_kernel, out_shape=(shape((512, 256), BF16), shape((...]
    pallas_call x1, Pallas kernels: 16 us -> 13.2 us  [per_device(): pl.pallas_call(attend_kernel, out_shape=(shape((2, 4, 256, 128), BF16), s...]
where the time goes in v8:
time: 137 us
  Pallas kernels  134 us (98%)
  other arithmetic  1.6 us (1%)
    pallas_call x1, Pallas kernels, per_device(): pl.pallas_call(middle_kernel, out_shape=(shape((512, 256), BF16), shape((...  79.9 us
    pallas_call x1, Pallas kernels, per_device(): pl.pallas_call(gather_kernel, out_shape=(shape((528, 256), BF16), shape((...  38.9 us
    pallas_call x1, Pallas kernels, per_device(): pl.pallas_call(attend_kernel, out_shape=(shape((2, 4, 256, 128), BF16), s...  13.2 us

profile of v8, /device:TPU:1, one launch (start us, length us, event | category | flops | bytes accessed | tf_op | source)
XLA Modules:
  0.0 136.8 jit_solution(3011997601237752474)
XLA Ops:
  0.6 1.6 %convert_reduce_fusion.starts_ref = s32[8]{0:T(128)} fusion(s32[16384]{0:T(1024)} %param.32), kind=kLoop, calls=%fused_computation | loop fusion | flops 393208 | bytes 65568 | tf_op jit(solution)/shard_map/reduce_sum | solution.py:801
  2.2 38.9 %gather.1 = (bf16[528,256]{1,0:T(8,128)(2,1)}, bf16[512,256]{1,0:T(8,128)(2,1)}, bf16[8,8,64]{2,1,0:T(8,128)(2,1)}, bf16[16,528,256]{2,1,0:T(8,128)(2,1)}, bf16[...) custom-call(s32[512]{0:T(512)} %base_ref.3, s32[8]{0:T(128)} %convert_reduce_fusion.starts_ref, ...), custom_call_target="tpu_custom_call" | custom-call | tf_op jit(solution)/shard_map/gather/pallas_call | solution.py:802
  41.2 13.2 %attend.1 = (bf16[2,4,256,128]{3,2,1,0:T(8,128)(2,1)}, f32[2,4,8,128]{3,2,1,0:T(8,128)}) custom-call(s32[40,128]{1,0:T(8,128)} %get-tuple-element.19.tail_ref, s32[512]{0:T(512)} %base_ref.3, s32[8]{0:T(128)} %convert_reduce_fusion.starts_ref, s32[32]{0:T(128)} %bitcast.17, s32[1]{0:T(128)} %bitcast.4.me_ref, bf16[528,256]{1,0:T(8,128)(2,1)} %get-tuple-element.20.q_ref, ...), custom_call_target="tpu_custom_call" | custom-call | tf_op jit(solution)/shard_map/attend/pallas_call | solution.py:831
  54.4 0.0 copy-start
  54.4 79.9 %middle.1 = (bf16[512,256]{1,0:T(8,128)(2,1)}, f32[1,4]{1,0:T(1,128)}, f32[1,4]{1,0:T(1,128)}) custom-call(bf16[2,4,256,128]{3,2,1,0:T(8,128)(2,1)} %get-tuple-element.23.heads_ref, f32[2,4,8,128]{3,2,1,0:T(8,128)} %get-tuple-element.24.stats_ref, bf16[4,256,2048]{2,1,0:T(8,128)(2,1)} %bitcast.11, bf16[256,2048]{1,0:T(8,128)(2,1)} %w_own.1, ...), custom_call_target="tpu_custom_call" | custom-call | tf_op jit(solution)/shard_map/middle/pallas_call | solution.py:859
  134.3 1.7 %hand_over.1 = (bf16[512,256]{1,0:T(8,128)(2,1)}, f32[1,4]{1,0:T(1,128)}, f32[1,4]{1,0:T(1,128)}) custom-call(bf16[512,256]{1,0:T(8,128)(2,1)} %get-tuple-element.27.hidden_ref, f32[1,4]{1,0:T(1,128)} %get-tuple-element.28.rms_ref, f32[1,4]{1,0:T(1,128)} %get-tuple-element.29.top_ref), custom_call_target="tpu_custom_call" | custom-call | tf_op jit(solution)/shard_map/hand_over/pallas_call | solution.py:904
  136.0 0.0 copy-done
  136.0 0.8 reshape.38
Async XLA Ops:
  54.4 81.6 %copy-start = (bf16[512,256]{1,0:T(8,128)(2,1)S(1)}, bf16[512,256]{1,0:T(8,128)(2,1)}, u32[]{:S(2)}) copy-start(bf16[512,256]{1,0:T(8,128)(2,1)} %get-tuple-element.31) | copy-start | bytes 786436

commit v9 on v8

--- a/solution.py
+++ b/solution.py
@@ -64,10 +64,10 @@
 
 
 def gather_kernel(
-    base_ref, starts_ref, live_ref, tok_ref, gain_ref, wq_ref, wk_ref, wv_ref,
+    base_ref, starts_ref, live_ref, tok_in, gain_ref, wq_in, wk_ref, wv_ref,
     step_cos, step_sin, far_cos, far_sin, slot_ref, w_ref,
     q_ref, cache_ref, match_ref, kv_all, q_all, w_all, tail_ref,
-    kv_ref, normed, cosines, sines, tails, own_sem, send_sem, kv_sem, q_sem, w_sem,
+    tok_ref, wq_ref, load_sem, kv_ref, normed, cosines, sines, tails, own_sem, send_sem, kv_sem, q_sem, w_sem,
 ):
     s = lax.axis_index("seq")
     v = lax.axis_index("vocab")
@@ -78,6 +78,15 @@
     core = (seq_at(s, 0, 0, 1), v)
     right = (s, vocab_at(v, 1, 0))
     left = (s, vocab_at(v, -1, 0))
+    loads = [
+        pltpu.make_async_copy(
+            tok_in.at[pl.ds(i * 128, 128), :], tok_ref.at[pl.ds(i * 128, 128), :], load_sem.at[i]
+        )
+        for i in range(4)
+    ]
+    loads.append(pltpu.make_async_copy(wq_in, wq_ref, load_sem.at[4]))
+    for copy in loads:
+        copy.start()
     barrier = pltpu.get_barrier_semaphore()
     for peer in (up, down, side, core, right, left):
         pl.semaphore_signal(barrier, inc=1, device_id=peer, device_id_type=MESH)
@@ -90,6 +99,7 @@
 
     def keys_values(i):
         rows = pl.ds(i * 128, 128)
+        loads[i].wait()
         values = tok_ref[rows, :].astype(F32)
         scale = lax.rsqrt(jnp.mean(values * values, axis=-1, keepdims=True) + epsilon)
         values = (values * scale * gain).astype(BF16)
@@ -165,6 +175,7 @@
                 go(w_ref.at[piece], w_all.at[x, piece], w_sem.at[x, piece], peer)
     own = pltpu.make_async_copy(kv_ref, kv_all.at[mine], own_sem.at[0])
     own.start()
+    loads[4].wait()
     for p in range(4):
         rows = pl.ds(p * 128, 128)
         query = jnp.dot(normed[rows, :], wq_ref[...], preferred_element_type=F32)
@@ -261,17 +272,13 @@
     def gather_up(i, count):
         before[i] = count
         entry = table[i]
-
-        @pl.when(entry >= 0)
-        def _():
-            sorted_run[count] = i
-            sorted_entry[count] = entry
-
+        sorted_run[count] = i
+        sorted_entry[count] = entry
         return jnp.where(entry >= 0, count + 1, count)
 
-    lax.fori_loop(0, 64, clear, 0)
-    lax.fori_loop(0, 32, enter, 0)
-    before[64] = lax.fori_loop(0, 64, gather_up, 0)
+    lax.fori_loop(0, 64, clear, 0, unroll=8)
+    lax.fori_loop(0, 32, enter, 0, unroll=8)
+    before[64] = lax.fori_loop(0, 64, gather_up, 0, unroll=8)
 
     def low_of(position):
         low = starts_ref[0]
@@ -806,9 +813,12 @@
             shape((16, 528, 256), BF16), shape((528, 256), BF16), shape((4, 4, 64, 2048), BF16),
             shape((40, 128), jnp.int32),
         ),
-        in_specs=[SM] * 3 + [VM] * 10 + [HB],
+        in_specs=[SM] * 3 + [HB, VM, HB] + [VM] * 7 + [HB],
         out_specs=(VM, VM, VM, HB, HB, HB, VM),
         scratch_shapes=[
+            pltpu.VMEM((512, 2048), BF16),
+            pltpu.VMEM((2048, 256), BF16),
+            pltpu.SemaphoreType.DMA((5,)),
             pltpu.VMEM((528, 256), BF16),
             pltpu.VMEM((512, 2048), BF16),
             pltpu.VMEM((512, 128), F32),
@@ -847,8 +857,8 @@
             pltpu.VMEM((1, 512), F32),
             pltpu.VMEM((1, 512), F32),
             pltpu.SMEM((64,), jnp.int32),
-            pltpu.SMEM((32,), jnp.int32),
-            pltpu.SMEM((32,), jnp.int32),
+            pltpu.SMEM((33,), jnp.int32),
+            pltpu.SMEM((33,), jnp.int32),
             pltpu.SMEM((65,), jnp.int32),
         ],
         compiler_params=params(),

time: 137 us -> 132 us (0.964)
  Pallas kernels: 134 us -> 130 us
    pallas_call x1, Pallas kernels: 79.9 us -> 75.8 us  [per_device(): pl.pallas_call(middle_kernel, out_shape=(shape((512, 256), BF16), shape((...]
where the time goes in v9:
time: 132 us; the launch traced here: 133 us
  Pallas kernels  130 us (98%)
  other arithmetic  1.6 us (1%)
    pallas_call x1, Pallas kernels, per_device(): pl.pallas_call(middle_kernel, out_shape=(shape((512, 256), BF16), shape((...  75.8 us
    pallas_call x1, Pallas kernels, per_device(): pl.pallas_call(gather_kernel, out_shape=(shape((528, 256), BF16), shape((...  38 us
    pallas_call x1, Pallas kernels, per_device(): pl.pallas_call(attend_kernel, out_shape=(shape((2, 4, 256, 128), BF16), s...  14.1 us

profile of v9, /device:TPU:1, one launch (start us, length us, event | category | flops | bytes accessed | tf_op | source)
XLA Modules:
  0.0 132.7 jit_solution(1746422348610163757)
XLA Ops:
  0.6 1.6 %convert_reduce_fusion.starts_ref = s32[8]{0:T(128)} fusion(s32[16384]{0:T(1024)} %param.32), kind=kLoop, calls=%fused_computation | loop fusion | flops 393208 | bytes 65568 | tf_op jit(solution)/shard_map/reduce_sum | solution.py:808
  2.2 38.0 %gather.1 = (bf16[528,256]{1,0:T(8,128)(2,1)}, bf16[512,256]{1,0:T(8,128)(2,1)}, bf16[8,8,64]{2,1,0:T(8,128)(2,1)}, bf16[16,528,256]{2,1,0:T(8,128)(2,1)}, bf16[...) custom-call(s32[512]{0:T(512)} %base_ref.3, s32[8]{0:T(128)} %convert_reduce_fusion.starts_ref, ...), custom_call_target="tpu_custom_call" | custom-call | tf_op jit(solution)/shard_map/gather/pallas_call | solution.py:809
  40.3 14.1 %attend.1 = (bf16[2,4,256,128]{3,2,1,0:T(8,128)(2,1)}, f32[2,4,8,128]{3,2,1,0:T(8,128)}) custom-call(s32[40,128]{1,0:T(8,128)} %get-tuple-element.19.tail_ref, s32[512]{0:T(512)} %base_ref.3, s32[8]{0:T(128)} %convert_reduce_fusion.starts_ref, s32[32]{0:T(128)} %bitcast.17, s32[1]{0:T(128)} %bitcast.4.me_ref, bf16[528,256]{1,0:T(8,128)(2,1)} %get-tuple-element.20.q_ref, ...), custom_call_target="tpu_custom_call" | custom-call | tf_op jit(solution)/shard_map/attend/pallas_call | solution.py:841
  54.4 0.0 copy-start
  54.4 75.8 %middle.1 = (bf16[512,256]{1,0:T(8,128)(2,1)}, f32[1,4]{1,0:T(1,128)}, f32[1,4]{1,0:T(1,128)}) custom-call(bf16[2,4,256,128]{3,2,1,0:T(8,128)(2,1)} %get-tuple-element.23.heads_ref, f32[2,4,8,128]{3,2,1,0:T(8,128)} %get-tuple-element.24.stats_ref, bf16[4,256,2048]{2,1,0:T(8,128)(2,1)} %bitcast.11, bf16[256,2048]{1,0:T(8,128)(2,1)} %w_own.1, ...), custom_call_target="tpu_custom_call" | custom-call | tf_op jit(solution)/shard_map/middle/pallas_call | solution.py:869
  130.2 1.7 %hand_over.1 = (bf16[512,256]{1,0:T(8,128)(2,1)}, f32[1,4]{1,0:T(1,128)}, f32[1,4]{1,0:T(1,128)}) custom-call(bf16[512,256]{1,0:T(8,128)(2,1)} %get-tuple-element.27.hidden_ref, f32[1,4]{1,0:T(1,128)} %get-tuple-element.28.rms_ref, f32[1,4]{1,0:T(1,128)} %get-tuple-element.29.top_ref), custom_call_target="tpu_custom_call" | custom-call | tf_op jit(solution)/shard_map/hand_over/pallas_call | solution.py:914
  131.9 0.0 copy-done
  131.9 0.8 reshape.38
Async XLA Ops:
  54.4 77.5 %copy-start = (bf16[512,256]{1,0:T(8,128)(2,1)S(1)}, bf16[512,256]{1,0:T(8,128)(2,1)}, u32[]{:S(2)}) copy-start(bf16[512,256]{1,0:T(8,128)(2,1)} %get-tuple-element.31) | copy-start | bytes 786436
